TPU v7x, 32 devices: a whole 2x2x4 slice. The times are simulated.
32 devices in a mesh: mode: 4 (over y, x), tm: 8 (over z, core).
Axes of the slice: x: 2, y: 2, z: 4, core: 2. Of those that a mesh axis runs over, the one named last changes fastest.
Arguments:
- field: float32 [96, 2, 4096], P('mode', None, 'tm'), may hold values from -6 to 6
- modes: float32 [96, 1024], P(None, 'mode'), may hold values from -0.1875 to 0.1875
- betas: float32 [96, 4], P('mode'), may hold values from -4 to 4
Outputs:
- field_out: float32 [96, 2, 4096], P('mode', None, 'tm')
All inputs are finite; a program needn't handle non-finite values.
Results may differ from a plain program's by a relative error of at most 0.0003.
Values sent between devices are 32-bit elements; how exact they have to be, the bound alone decides.
No kernel may reach another device: no remote copies, remote signals or barrier semaphores. Data moves between devices by JAX's collectives and lax.ppermute only.
A program may use at most 64 MiB of HBM per device.

v0:
```python
import math

import jax
import jax.numpy as jnp
from jax import lax
from jax.sharding import PartitionSpec as P

RAMAN_TAPS = 256
ITERS = 2


RAMAN_SHARE = 0.18
KERR_GAIN = 6.0
TWO_PI = 2.0 * math.pi
PRECISE = lax.Precision.HIGHEST


def kernel_raw(positions):
    spacing = 256.0 / RAMAN_TAPS
    return jnp.exp(-positions * spacing / 32.0) * jnp.sin(positions * spacing / 12.2)


def contract(pattern, operand, matrix):
    return jnp.einsum(pattern, operand, matrix, precision=PRECISE)


def angle_set(product, length, orient):
    angle_val = (product % length).astype(jnp.float32) * (orient * TWO_PI / length)
    return (jnp.cos(angle_val), jnp.sin(angle_val))


def split_length(length):
    leading = math.isqrt(length)
    while length % leading:
        leading = leading - 1
    return (leading, length // leading)


def make_tables(orient, n_tm, t_index, samples):
    all_samples = samples * n_tm
    piece_len = samples // n_tm
    leading, trailing = split_length(samples)
    device_ids = jnp.arange(n_tm, dtype=jnp.int32)
    dev_table = angle_set(device_ids[:, None] * device_ids[None, :], n_tm, orient)
    time_ids = t_index * piece_len + jnp.arange(piece_len, dtype=jnp.int32)
    twiddle = angle_set(device_ids[:, None] * time_ids[None, :], all_samples, orient)
    first_ids = jnp.arange(leading, dtype=jnp.int32)
    second_ids = jnp.arange(trailing, dtype=jnp.int32)
    lead_table = angle_set(first_ids[:, None] * first_ids[None, :], leading, orient)
    middle = angle_set(first_ids[:, None] * second_ids[None, :], samples, orient)
    trail_table = angle_set(second_ids[:, None] * second_ids[None, :], trailing, orient)
    return (dev_table, twiddle, lead_table, middle, trail_table)


def cdot(couple, tables, pattern):
    cosine, sine_part = tables
    out_real = contract(pattern, couple[0], cosine) - contract(pattern, couple[1], sine_part)
    out_imag = contract(pattern, couple[0], sine_part) + contract(pattern, couple[1], cosine)
    return (out_real, out_imag)


def rotate(couple, tables):
    cosine, sine_part = tables
    return (couple[0] * cosine - couple[1] * sine_part, couple[0] * sine_part + couple[1] * cosine)


def local_dft(couple, tables):
    row_count, samples = couple[0].shape
    leading, trailing = split_length(samples)
    shaped = tuple((values.reshape(row_count, leading, trailing) for values in couple))
    shaped = cdot(shaped, tables[2], "rnm,nk->rkm")
    shaped = rotate(shaped, tables[3])
    shaped = cdot(shaped, tables[4], "rkm,mq->rqk")
    return tuple((values.reshape(row_count, samples) for values in shaped))


def forward(couple, mover, tables, n_tm):
    row_count, samples = couple[0].shape
    piece_len = samples // n_tm
    blocks = tuple((values.reshape(row_count, n_tm, piece_len) for values in couple))
    arrived = mover(blocks)
    arrived = tuple((values.reshape(row_count, n_tm, piece_len) for values in arrived))
    mixed = rotate(cdot(arrived, tables[0], "rdm,dk->rkm"), tables[1])
    arrived = mover(mixed)
    arrived = tuple((values.reshape(row_count, samples) for values in arrived))
    return local_dft(arrived, tables)


def inverse(couple, mover, tables, n_tm):
    row_count, samples = couple[0].shape
    piece_len = samples // n_tm
    spread = local_dft(couple, tables)
    blocks = tuple((values.reshape(row_count, n_tm, piece_len) for values in spread))
    arrived = mover(blocks)
    arrived = tuple((values.reshape(row_count, n_tm, piece_len) for values in arrived))
    mixed = cdot(rotate(arrived, tables[1]), tables[0], "rkm,kd->rdm")
    arrived = mover(mixed)
    scale = 1.0 / (samples * n_tm)
    return tuple((values.reshape(row_count, samples) * scale for values in arrived))


def shuffle_field(couple):
    return (
        lax.all_to_all(couple[0], "tm", split_axis=1, concat_axis=2, tiled=True),
        lax.all_to_all(couple[1], "tm", split_axis=1, concat_axis=2, tiled=True),
    )


def shards(field, modes, betas):
    n_tm = lax.axis_size("tm")
    t_index = lax.axis_index("tm")
    samples = field.shape[2]
    all_samples = samples * n_tm
    grid_local = modes.shape[1]
    forward_set = make_tables(-1.0, n_tm, t_index, samples)
    inverse_set = make_tables(1.0, n_tm, t_index, samples)
    frequency = t_index + n_tm * jnp.arange(samples, dtype=jnp.int32)
    norm_freq = jnp.where(frequency < all_samples // 2, frequency, frequency - all_samples).astype(
        jnp.float32
    ) * (2.0 / all_samples)
    phase = (
        betas[:, 0:1]
        + betas[:, 1:2] * norm_freq
        + betas[:, 2:3] * (norm_freq * norm_freq) / 2.0
        + betas[:, 3:4] * (norm_freq * norm_freq * norm_freq) / 6.0
    )
    half_phase = phase * 0.5
    half_turn = (jnp.cos(half_phase), jnp.sin(half_phase))
    positions = jnp.arange(1, RAMAN_TAPS + 1).astype(jnp.float32)
    raw_total = jnp.sum(kernel_raw(positions))
    kernel = kernel_raw(positions) / raw_total
    tap_ids = jnp.arange(1, RAMAN_TAPS + 1, dtype=jnp.int32)
    tap_angles = angle_set(tap_ids[:, None] * frequency[None, :], all_samples, -1.0)
    spectrum = (
        contract("s,sk->k", kernel, tap_angles[0]),
        contract("s,sk->k", kernel, tap_angles[1]),
    )

    def shuffle_power(couple):
        return (
            lax.all_to_all(couple[0], "tm", split_axis=1, concat_axis=2, tiled=True),
            lax.all_to_all(couple[1], "tm", split_axis=1, concat_axis=2, tiled=True),
        )

    def disperse(couple, turn):
        spectral = rotate(forward(couple, shuffle_field, forward_set, n_tm), turn)
        return inverse(spectral, shuffle_field, inverse_set, n_tm)

    couple = (field[:, 0, :], field[:, 1, :])
    for number in range(ITERS):
        couple = disperse(couple, half_turn)
        grid_real = contract(
            "pg,pt->gt", modes, lax.all_gather(couple[0], "mode", axis=0, tiled=True)
        )
        grid_imag = contract(
            "pg,pt->gt", modes, lax.all_gather(couple[1], "mode", axis=0, tiled=True)
        )
        nonlinear_intensity = grid_real * grid_real + grid_imag * grid_imag
        packed = nonlinear_intensity.reshape(grid_local // 2, 2, samples)
        delayed_couple = (packed[:, 0], packed[:, 1])
        delayed_spectral = rotate(
            forward(delayed_couple, shuffle_power, forward_set, n_tm), spectrum
        )
        back = inverse(delayed_spectral, shuffle_power, inverse_set, n_tm)
        delayed = jnp.stack(back, 1).reshape(grid_local, samples)
        weight = (1.0 - RAMAN_SHARE) * nonlinear_intensity + RAMAN_SHARE * delayed
        drive_real = grid_real * weight
        drive_imag = grid_imag * weight
        response = lax.psum_scatter(
            jnp.stack(
                [
                    jnp.dot(modes, drive_real, precision=PRECISE),
                    jnp.dot(modes, drive_imag, precision=PRECISE),
                ],
                1,
            ),
            "mode",
            scatter_dimension=0,
            tiled=True,
        )
        couple = (couple[0] - KERR_GAIN * response[:, 1], couple[1] + KERR_GAIN * response[:, 0])
        couple = disperse(couple, half_turn)
    return jnp.stack([couple[0], couple[1]], 1)


def solution(mesh):
    return jax.shard_map(
        shards,
        mesh=mesh,
        in_specs=(P("mode", None, "tm"), P(None, "mode"), P("mode", None)),
        out_specs=P("mode", None, "tm"),
        check_vma=False,
    )
```

profile of v0, /device:TPU:0, one launch (start us, length us, event | category | flops | bytes accessed | tf_op | source)
XLA Modules:
  0.0 707.4 jit_solution(16335441743079139447)
XLA Ops:
  8.6 6.4 all-to-all-start
  36.3 5.0 all-to-all-done.2
  74.9 4.9 all-to-all-done.4
  101.7 8.7 %all_gather.13 = f32[96,512]{1,0:T(8,128)S(1)} all-gather(f32[24,512]{1,0:T(8,128)S(1)} %mul.3036), channel_id=1, replica_groups=mesh['mode'=4,'tm'=8] {'mode'}, dimensions={0}, use_global_device_ids=true | all-gather | bytes 245760 | tf_op jit(solution)/shard_map/all_gather | solution.py:156
  110.4 8.8 %all_gather.12 = f32[96,512]{1,0:T(8,128)S(1)} all-gather(f32[24,512]{1,0:T(8,128)S(1)} %mul.3033), channel_id=1, replica_groups=mesh['mode'=4,'tm'=8] {'mode'}, dimensions={0}, use_global_device_ids=true | all-gather | bytes 245760 | tf_op jit(solution)/shard_map/all_gather | solution.py:153
  127.2 8.0 %all-to-all-done.8 = f32[128,8,64]{0,2,1:T(8,128)S(1)} async-done(((f32[128,8,64]{0,2,1:T(8,128)}), f32[128,8,64]{0,2,1:T(8,128)S(1)}, u32[]{:S(2)}, u32[]{:S(2)}) %all-to-all-start.8) | async-done | bytes 262176 | tf_op jit(solution)/shard_map/all_to_all | solution.py:141
  139.5 8.6 %all-to-all-done.9 = f32[128,8,64]{0,2,1:T(8,128)S(1)} async-done(((f32[128,8,64]{0,2,1:T(8,128)}), f32[128,8,64]{0,2,1:T(8,128)S(1)}, u32[]{:S(2)}, u32[]{:S(2)}) %all-to-all-start.9) | async-done | bytes 262176 | tf_op jit(solution)/shard_map/all_to_all | solution.py:142
  167.9 8.6 %all-to-all-done.11 = f32[128,8,64]{0,2,1:T(8,128)S(1)} async-done(((f32[128,8,64]{0,2,1:T(8,128)}), f32[128,8,64]{0,2,1:T(8,128)S(1)}, u32[]{:S(2)}, u32[]{:S(2)}) %all-to-all-start.11) | async-done | bytes 262176 | tf_op jit(solution)/shard_map/all_to_all | solution.py:142
  188.9 8.5 %all-to-all-done.12 = f32[128,8,64]{0,2,1:T(8,128)S(1)} async-done(((f32[128,8,64]{0,2,1:T(8,128)}), f32[128,8,64]{0,2,1:T(8,128)S(1)}, u32[]{:S(2)}, u32[]{:S(2)}) %all-to-all-start.12) | async-done | bytes 262176 | tf_op jit(solution)/shard_map/all_to_all | solution.py:141
  197.4 12.1 %all_to_all.192 = f32[128,8,64]{0,2,1:T(8,128)S(1)} all-to-all(f32[128,8,64]{0,2,1:T(8,128)S(1)} %bitcast.796), channel_id=1, replica_groups=mesh['mode'=4,'tm'=8] {'tm'}, dimensions={1} | all-to-all | bytes 524288 | tf_op jit(solution)/shard_map/all_to_all | solution.py:142
  216.6 7.9 %all-to-all-done.14 = f32[128,8,64]{0,2,1:T(8,128)S(1)} async-done(((f32[128,8,64]{0,2,1:T(8,128)}), f32[128,8,64]{0,2,1:T(8,128)S(1)}, u32[]{:S(2)}, u32[]{:S(2)}) %all-to-all-start.14) | async-done | bytes 262176 | tf_op jit(solution)/shard_map/all_to_all | solution.py:141
  228.0 9.6 %all-to-all-done.15 = f32[128,8,64]{0,2,1:T(8,128)S(1)} async-done(((f32[128,8,64]{0,2,1:T(8,128)}), f32[128,8,64]{0,2,1:T(8,128)S(1)}, u32[]{:S(2)}, u32[]{:S(2)}) %all-to-all-start.15) | async-done | bytes 262176 | tf_op jit(solution)/shard_map/all_to_all | solution.py:142
  240.2 22.8 %reduce-scatter.3.cloned.1.call-done = f32[24,2,512]{2,0,1:T(8,128)} async-done(((f32[96,2,512]{2,0,1:T(8,128)}), f32[24,2,512]{2,0,1:T(8,128)}) %reduce-scatter.3.cloned.1.call-update) | async-done | bytes 98320 | tf_op jit(solution)/shard_map/reduce_scatter | solution.py:169
  270.1 5.1 all-to-all-done.16
  290.6 5.0 all-to-all-done.18
  350.0 4.9 all-to-all-done.22
  361.1 5.0 all-to-all-done.23
  381.5 5.0 all-to-all-done.26
  446.9 8.7 %all_gather.15 = f32[96,512]{1,0:T(8,128)S(1)} all-gather(f32[24,512]{1,0:T(8,128)S(1)} %mul.3137), channel_id=1, replica_groups=mesh['mode'=4,'tm'=8] {'mode'}, dimensions={0}, use_global_device_ids=true | all-gather | bytes 245760 | tf_op jit(solution)/shard_map/all_gather | solution.py:156
  455.6 7.7 %all_gather.14 = f32[96,512]{1,0:T(8,128)S(1)} all-gather(f32[24,512]{1,0:T(8,128)S(1)} %mul.3134), channel_id=1, replica_groups=mesh['mode'=4,'tm'=8] {'mode'}, dimensions={0}, use_global_device_ids=true | all-gather | bytes 245760 | tf_op jit(solution)/shard_map/all_gather | solution.py:153
  470.5 8.8 %all-to-all-done.32 = f32[128,8,64]{0,2,1:T(8,128)S(1)} async-done(((f32[128,8,64]{0,2,1:T(8,128)}), f32[128,8,64]{0,2,1:T(8,128)S(1)}, u32[]{:S(2)}, u32[]{:S(2)}) %all-to-all-start.32) | async-done | bytes 262176 | tf_op jit(solution)/shard_map/all_to_all | solution.py:141
  483.7 8.6 %all-to-all-done.33 = f32[128,8,64]{0,2,1:T(8,128)S(1)} async-done(((f32[128,8,64]{0,2,1:T(8,128)}), f32[128,8,64]{0,2,1:T(8,128)S(1)}, u32[]{:S(2)}, u32[]{:S(2)}) %all-to-all-start.33) | async-done | bytes 262176 | tf_op jit(solution)/shard_map/all_to_all | solution.py:142
  498.3 8.9 %all-to-all-done.34 = f32[128,8,64]{0,2,1:T(8,128)S(1)} async-done(((f32[128,8,64]{0,2,1:T(8,128)}), f32[128,8,64]{0,2,1:T(8,128)S(1)}, u32[]{:S(2)}, u32[]{:S(2)}) %all-to-all-start.34) | async-done | bytes 262176 | tf_op jit(solution)/shard_map/all_to_all | solution.py:141
  511.7 8.6 %all-to-all-done.35 = f32[128,8,64]{0,2,1:T(8,128)S(1)} async-done(((f32[128,8,64]{0,2,1:T(8,128)}), f32[128,8,64]{0,2,1:T(8,128)S(1)}, u32[]{:S(2)}, u32[]{:S(2)}) %all-to-all-start.35) | async-done | bytes 262176 | tf_op jit(solution)/shard_map/all_to_all | solution.py:142
  532.5 8.5 %all-to-all-done.36 = f32[128,8,64]{0,2,1:T(8,128)S(1)} async-done(((f32[128,8,64]{0,2,1:T(8,128)}), f32[128,8,64]{0,2,1:T(8,128)S(1)}, u32[]{:S(2)}, u32[]{:S(2)}) %all-to-all-start.36) | async-done | bytes 262176 | tf_op jit(solution)/shard_map/all_to_all | solution.py:141
  540.9 12.1 %all_to_all.193 = f32[128,8,64]{0,2,1:T(8,128)S(1)} all-to-all(f32[128,8,64]{0,2,1:T(8,128)S(1)} %bitcast.797), channel_id=1, replica_groups=mesh['mode'=4,'tm'=8] {'tm'}, dimensions={1} | all-to-all | bytes 524288 | tf_op jit(solution)/shard_map/all_to_all | solution.py:142
  560.2 7.9 %all-to-all-done.38 = f32[128,8,64]{0,2,1:T(8,128)S(1)} async-done(((f32[128,8,64]{0,2,1:T(8,128)}), f32[128,8,64]{0,2,1:T(8,128)S(1)}, u32[]{:S(2)}, u32[]{:S(2)}) %all-to-all-start.38) | async-done | bytes 262176 | tf_op jit(solution)/shard_map/all_to_all | solution.py:141
  571.6 9.6 %all-to-all-done.39 = f32[128,8,64]{0,2,1:T(8,128)S(1)} async-done(((f32[128,8,64]{0,2,1:T(8,128)}), f32[128,8,64]{0,2,1:T(8,128)S(1)}, u32[]{:S(2)}, u32[]{:S(2)}) %all-to-all-start.39) | async-done | bytes 262176 | tf_op jit(solution)/shard_map/all_to_all | solution.py:142
  583.7 22.9 %reduce-scatter.5.cloned.1.call-done = f32[24,2,512]{2,0,1:T(8,128)} async-done(((f32[96,2,512]{2,0,1:T(8,128)}), f32[24,2,512]{2,0,1:T(8,128)}) %reduce-scatter.5.cloned.1.call-update) | async-done | bytes 98320 | tf_op jit(solution)/shard_map/reduce_scatter | solution.py:169
  613.7 5.1 all-to-all-done.40
  634.2 5.0 all-to-all-done.42
  672.9 4.9 all-to-all-done.44
  (499 shorter events, 419.1 us)
Async XLA Ops:
  8.6 12.2 %all-to-all-start = ((f32[8,1,1536]{2,1,0:T(1,128)}), f32[8,1,1536]{2,1,0:T(1,128)S(1)}, u32[]{:S(2)}, u32[]{:S(2)}) async-start(f32[8,1,1536]{2,1,0:T(1,128)} %reshape.959), calls=%async_computation | async-start | bytes 98304 | tf_op jit(solution)/shard_map/all_to_all | solution.py:104
  32.1 9.1 %all-to-all-start.2 = ((f32[8,1,1536]{2,1,0:T(1,128)}), f32[8,1,1536]{2,1,0:T(1,128)S(1)}, u32[]{:S(2)}, u32[]{:S(2)}) async-start(f32[8,1,1536]{2,1,0:T(1,128)} %reshape.963), calls=%async_computation.2 | async-start | bytes 98304 | tf_op jit(solution)/shard_map/all_to_all | solution.py:104
  61.4 9.3 %all-to-all-start.5 = ((f32[8,1,1536]{2,1,0:T(1,128)}), f32[8,1,1536]{2,1,0:T(1,128)S(1)}, u32[]{:S(2)}, u32[]{:S(2)}) async-start(f32[8,1,1536]{2,1,0:T(1,128)} %reshape.967), calls=%async_computation.5 | async-start | bytes 98304 | tf_op jit(solution)/shard_map/all_to_all | solution.py:105
  70.7 9.1 %all-to-all-start.4 = ((f32[8,1,1536]{2,1,0:T(1,128)}), f32[8,1,1536]{2,1,0:T(1,128)S(1)}, u32[]{:S(2)}, u32[]{:S(2)}) async-start(f32[8,1,1536]{2,1,0:T(1,128)} %reshape.969), calls=%async_computation.4 | async-start | bytes 98304 | tf_op jit(solution)/shard_map/all_to_all | solution.py:104
  91.4 9.1 %all-to-all-start.6 = ((f32[8,1,1536]{2,1,0:T(1,128)}), f32[8,1,1536]{2,1,0:T(1,128)S(1)}, u32[]{:S(2)}, u32[]{:S(2)}) async-start(f32[8,1,1536]{2,1,0:T(1,128)} %reshape.973), calls=%async_computation.6 | async-start | bytes 98304 | tf_op jit(solution)/shard_map/all_to_all | solution.py:104
  122.1 13.1 %all-to-all-start.8 = ((f32[128,8,64]{0,2,1:T(8,128)}), f32[128,8,64]{0,2,1:T(8,128)S(1)}, u32[]{:S(2)}, u32[]{:S(2)}) async-start(f32[128,8,64]{0,2,1:T(8,128)} %bitcast.34), calls=%async_computation.8 | async-start | bytes 524288 | tf_op jit(solution)/shard_map/all_to_all | solution.py:141
  135.1 13.1 %all-to-all-start.9 = ((f32[128,8,64]{0,2,1:T(8,128)}), f32[128,8,64]{0,2,1:T(8,128)S(1)}, u32[]{:S(2)}, u32[]{:S(2)}) async-start(f32[128,8,64]{0,2,1:T(8,128)} %bitcast.35), calls=%async_computation.9 | async-start | bytes 524288 | tf_op jit(solution)/shard_map/all_to_all | solution.py:142
  150.0 13.4 %all-to-all-start.10 = ((f32[128,8,64]{0,2,1:T(8,128)}), f32[128,8,64]{0,2,1:T(8,128)S(1)}, u32[]{:S(2)}, u32[]{:S(2)}) async-start(f32[128,8,64]{0,2,1:T(8,128)} %copy.735), calls=%async_computation.10 | async-start | bytes 524288 | tf_op jit(solution)/shard_map/all_to_all | solution.py:141
  163.5 13.1 %all-to-all-start.11 = ((f32[128,8,64]{0,2,1:T(8,128)}), f32[128,8,64]{0,2,1:T(8,128)S(1)}, u32[]{:S(2)}, u32[]{:S(2)}) async-start(f32[128,8,64]{0,2,1:T(8,128)} %copy.737), calls=%async_computation.11 | async-start | bytes 524288 | tf_op jit(solution)/shard_map/all_to_all | solution.py:142
  184.2 13.2 %all-to-all-start.12 = ((f32[128,8,64]{0,2,1:T(8,128)}), f32[128,8,64]{0,2,1:T(8,128)S(1)}, u32[]{:S(2)}, u32[]{:S(2)}) async-start(f32[128,8,64]{0,2,1:T(8,128)} %bitcast.57), calls=%async_computation.12 | async-start | bytes 524288 | tf_op jit(solution)/shard_map/all_to_all | solution.py:141
  211.4 13.1 %all-to-all-start.14 = ((f32[128,8,64]{0,2,1:T(8,128)}), f32[128,8,64]{0,2,1:T(8,128)S(1)}, u32[]{:S(2)}, u32[]{:S(2)}) async-start(f32[128,8,64]{0,2,1:T(8,128)} %copy.771), calls=%async_computation.14 | async-start | bytes 524288 | tf_op jit(solution)/shard_map/all_to_all | solution.py:141
  224.5 13.1 %all-to-all-start.15 = ((f32[128,8,64]{0,2,1:T(8,128)}), f32[128,8,64]{0,2,1:T(8,128)S(1)}, u32[]{:S(2)}, u32[]{:S(2)}) async-start(f32[128,8,64]{0,2,1:T(8,128)} %copy.774), calls=%async_computation.15 | async-start | bytes 524288 | tf_op jit(solution)/shard_map/all_to_all | solution.py:142
  227.9 35.0 %reduce-scatter.3.cloned.1.call-start = ((), (), s32[]{:S(2)}) async-start(), calls=%async_computation.50 | async-start | bytes 491520 | tf_op jit(solution)/shard_map/reduce_scatter | solution.py:169
  264.7 10.4 %all-to-all-start.16 = ((f32[8,1,1536]{2,1,0:T(1,128)}), f32[8,1,1536]{2,1,0:T(1,128)S(1)}, u32[]{:S(2)}, u32[]{:S(2)}) async-start(f32[8,1,1536]{2,1,0:T(1,128)} %reshape.975), calls=%async_computation.17 | async-start | bytes 98304 | tf_op jit(solution)/shard_map/all_to_all | solution.py:104
  286.5 9.1 %all-to-all-start.18 = ((f32[8,1,1536]{2,1,0:T(1,128)}), f32[8,1,1536]{2,1,0:T(1,128)S(1)}, u32[]{:S(2)}, u32[]{:S(2)}) async-start(f32[8,1,1536]{2,1,0:T(1,128)} %reshape.979), calls=%async_computation.19 | async-start | bytes 98304 | tf_op jit(solution)/shard_map/all_to_all | solution.py:104
  295.6 9.3 %all-to-all-start.19 = ((f32[8,1,1536]{2,1,0:T(1,128)}), f32[8,1,1536]{2,1,0:T(1,128)S(1)}, u32[]{:S(2)}, u32[]{:S(2)}) async-start(f32[8,1,1536]{2,1,0:T(1,128)} %reshape.981), calls=%async_computation.20 | async-start | bytes 98304 | tf_op jit(solution)/shard_map/all_to_all | solution.py:105
  325.0 9.1 %all-to-all-start.20 = ((f32[8,1,1536]{2,1,0:T(1,128)}), f32[8,1,1536]{2,1,0:T(1,128)S(1)}, u32[]{:S(2)}, u32[]{:S(2)}) async-start(f32[8,1,1536]{2,1,0:T(1,128)} %reshape.985), calls=%async_computation.21 | async-start | bytes 98304 | tf_op jit(solution)/shard_map/all_to_all | solution.py:104
  345.8 9.1 %all-to-all-start.22 = ((f32[8,1,1536]{2,1,0:T(1,128)}), f32[8,1,1536]{2,1,0:T(1,128)S(1)}, u32[]{:S(2)}, u32[]{:S(2)}) async-start(f32[8,1,1536]{2,1,0:T(1,128)} %reshape.987), calls=%async_computation.23 | async-start | bytes 98304 | tf_op jit(solution)/shard_map/all_to_all | solution.py:104
  356.5 9.6 %all-to-all-start.23 = ((f32[8,1,1536]{2,1,0:T(1,128)}), f32[8,1,1536]{2,1,0:T(1,128)S(1)}, u32[]{:S(2)}, u32[]{:S(2)}) async-start(f32[8,1,1536]{2,1,0:T(1,128)} %reshape.989), calls=%async_computation.24 | async-start | bytes 98304 | tf_op jit(solution)/shard_map/all_to_all | solution.py:104
  415.8 9.3 %all-to-all-start.28 = ((f32[8,1,1536]{2,1,0:T(1,128)}), f32[8,1,1536]{2,1,0:T(1,128)S(1)}, u32[]{:S(2)}, u32[]{:S(2)}) async-start(f32[8,1,1536]{2,1,0:T(1,128)} %reshape.1001), calls=%async_computation.29 | async-start | bytes 98304 | tf_op jit(solution)/shard_map/all_to_all | solution.py:104
  436.7 9.1 %all-to-all-start.30 = ((f32[8,1,1536]{2,1,0:T(1,128)}), f32[8,1,1536]{2,1,0:T(1,128)S(1)}, u32[]{:S(2)}, u32[]{:S(2)}) async-start(f32[8,1,1536]{2,1,0:T(1,128)} %reshape.1005), calls=%async_computation.31 | async-start | bytes 98304 | tf_op jit(solution)/shard_map/all_to_all | solution.py:104
  466.2 13.1 %all-to-all-start.32 = ((f32[128,8,64]{0,2,1:T(8,128)}), f32[128,8,64]{0,2,1:T(8,128)S(1)}, u32[]{:S(2)}, u32[]{:S(2)}) async-start(f32[128,8,64]{0,2,1:T(8,128)} %bitcast.102), calls=%async_computation.33 | async-start | bytes 524288 | tf_op jit(solution)/shard_map/all_to_all | solution.py:141
  479.3 13.1 %all-to-all-start.33 = ((f32[128,8,64]{0,2,1:T(8,128)}), f32[128,8,64]{0,2,1:T(8,128)S(1)}, u32[]{:S(2)}, u32[]{:S(2)}) async-start(f32[128,8,64]{0,2,1:T(8,128)} %bitcast.103), calls=%async_computation.34 | async-start | bytes 524288 | tf_op jit(solution)/shard_map/all_to_all | solution.py:142
  494.2 13.1 %all-to-all-start.34 = ((f32[128,8,64]{0,2,1:T(8,128)}), f32[128,8,64]{0,2,1:T(8,128)S(1)}, u32[]{:S(2)}, u32[]{:S(2)}) async-start(f32[128,8,64]{0,2,1:T(8,128)} %copy.850), calls=%async_computation.35 | async-start | bytes 524288 | tf_op jit(solution)/shard_map/all_to_all | solution.py:141
  507.2 13.1 %all-to-all-start.35 = ((f32[128,8,64]{0,2,1:T(8,128)}), f32[128,8,64]{0,2,1:T(8,128)S(1)}, u32[]{:S(2)}, u32[]{:S(2)}) async-start(f32[128,8,64]{0,2,1:T(8,128)} %copy.852), calls=%async_computation.36 | async-start | bytes 524288 | tf_op jit(solution)/shard_map/all_to_all | solution.py:142
  527.9 13.1 %all-to-all-start.36 = ((f32[128,8,64]{0,2,1:T(8,128)}), f32[128,8,64]{0,2,1:T(8,128)S(1)}, u32[]{:S(2)}, u32[]{:S(2)}) async-start(f32[128,8,64]{0,2,1:T(8,128)} %bitcast.121), calls=%async_computation.37 | async-start | bytes 524288 | tf_op jit(solution)/shard_map/all_to_all | solution.py:141
  555.0 13.1 %all-to-all-start.38 = ((f32[128,8,64]{0,2,1:T(8,128)}), f32[128,8,64]{0,2,1:T(8,128)S(1)}, u32[]{:S(2)}, u32[]{:S(2)}) async-start(f32[128,8,64]{0,2,1:T(8,128)} %copy.882), calls=%async_computation.39 | async-start | bytes 524288 | tf_op jit(solution)/shard_map/all_to_all | solution.py:141
  568.1 13.1 %all-to-all-start.39 = ((f32[128,8,64]{0,2,1:T(8,128)}), f32[128,8,64]{0,2,1:T(8,128)S(1)}, u32[]{:S(2)}, u32[]{:S(2)}) async-start(f32[128,8,64]{0,2,1:T(8,128)} %copy.885), calls=%async_computation.40 | async-start | bytes 524288 | tf_op jit(solution)/shard_map/all_to_all | solution.py:142
  571.5 35.1 %reduce-scatter.5.cloned.1.call-start = ((), (), s32[]{:S(2)}) async-start(), calls=%async_computation.51 | async-start | bytes 491520 | tf_op jit(solution)/shard_map/reduce_scatter | solution.py:169
  608.3 10.4 %all-to-all-start.40 = ((f32[8,1,1536]{2,1,0:T(1,128)}), f32[8,1,1536]{2,1,0:T(1,128)S(1)}, u32[]{:S(2)}, u32[]{:S(2)}) async-start(f32[8,1,1536]{2,1,0:T(1,128)} %reshape.1007), calls=%async_computation.42 | async-start | bytes 98304 | tf_op jit(solution)/shard_map/all_to_all | solution.py:104
  639.2 9.3 %all-to-all-start.43 = ((f32[8,1,1536]{2,1,0:T(1,128)}), f32[8,1,1536]{2,1,0:T(1,128)S(1)}, u32[]{:S(2)}, u32[]{:S(2)}) async-start(f32[8,1,1536]{2,1,0:T(1,128)} %reshape.1013), calls=%async_computation.45 | async-start | bytes 98304 | tf_op jit(solution)/shard_map/all_to_all | solution.py:105
  668.6 9.1 %all-to-all-start.44 = ((f32[8,1,1536]{2,1,0:T(1,128)}), f32[8,1,1536]{2,1,0:T(1,128)S(1)}, u32[]{:S(2)}, u32[]{:S(2)}) async-start(f32[8,1,1536]{2,1,0:T(1,128)} %reshape.1017), calls=%async_computation.46 | async-start | bytes 98304 | tf_op jit(solution)/shard_map/all_to_all | solution.py:104
  (18 other events, 259.2 us)
Sparse Core Ops, SparseCore 0:
  240.3 22.6 reduce-scatter.2
  583.8 22.6 reduce-scatter.4
where the time goes:
time: 720 us; the launch traced here: 707 us
  waiting for transfers between devices  308 us (43%)
  starting transfers between devices  162 us (22%)
  matrix products  79.7 us (11%)
  blocking collectives  58.2 us (8%)
  local copies, waits for them, and re-layouts  51.9 us (7%)
  other arithmetic  31.4 us (4%)
  between operations  16.4 us (2%)
    all_to_all x16, waiting for transfers between devices, shuffle_field(): lax.all_to_all(couple[0], 'tm', split_axis=1, concat_axis=2, tiled=True)  78.2 us
    dot_general x150, matrix products, contract(): return jnp.einsum(pattern, operand, matrix, precision=PRECISE)  77.5 us
    all_to_all x16, waiting for transfers between devices, shuffle_field(): lax.all_to_all(couple[1], 'tm', split_axis=1, concat_axis=2, tiled=True)  68.7 us
    all_to_all x8, waiting for transfers between devices, shuffle_power(): lax.all_to_all(couple[0], 'tm', split_axis=1, concat_axis=2, tiled=True)  61.4 us
    all_to_all x16, starting transfers between devices, shuffle_field(): lax.all_to_all(couple[0], 'tm', split_axis=1, concat_axis=2, tiled=True)  59.7 us
    all_to_all x16, starting transfers between devices, shuffle_field(): lax.all_to_all(couple[1], 'tm', split_axis=1, concat_axis=2, tiled=True)  54.2 us
    all_to_all x6, waiting for transfers between devices, shuffle_power(): lax.all_to_all(couple[1], 'tm', split_axis=1, concat_axis=2, tiled=True)  53.6 us
    reduce_scatter x2, waiting for transfers between devices, shards(): lax.psum_scatter(jnp.stack([jnp.dot(modes, drive_real, precision=PRECISE)...  45.6 us
  transfers between devices with their start and end apart: 48, of which 48 were waited for; matrix products, arithmetic and copies ran while one was open for 8% of the time, Pallas kernels for 0%

commit v1 on v0

v1 whole, which is shorter than its diff:
```python
import math

import jax
import jax.numpy as jnp
import numpy as np
from jax import lax
from jax.sharding import PartitionSpec as P

RAMAN_TAPS = 256
ITERS = 2
RAMAN_SHARE = 0.18
KERR_GAIN = 6.0
PRECISE = lax.Precision.HIGHEST
BOTH = ("mode", "tm")


def exp_table(product, length):
    angle = (product % length) * (2.0 * math.pi / length)
    return np.cos(angle), np.sin(angle)


def block_matrix(cosine, sine):
    return np.stack([np.stack([cosine, -sine], 1), np.stack([sine, cosine], 1)], 0)


def raman_matrix(block, halo):
    positions = np.arange(1, RAMAN_TAPS + 1)
    spacing = 256.0 / RAMAN_TAPS
    raw = np.exp(-positions * spacing / 32.0) * np.sin(positions * spacing / 12.2)
    taps = raw / raw.sum()
    lag = np.arange(block)[None, :] + halo * block - np.arange((halo + 1) * block)[:, None]
    return np.where((lag >= 1) & (lag <= RAMAN_TAPS), taps[np.clip(lag, 1, RAMAN_TAPS) - 1], 0.0)


def general(field, modes, betas):
    n_mode, n_tm = lax.axis_size("mode"), lax.axis_size("tm")
    t_index = lax.axis_index("tm")
    own_modes, _, samples = field.shape
    n_dev = n_mode * n_tm
    total = samples * n_tm
    block = total // n_dev
    halo = -(-RAMAN_TAPS // block)
    rows = -(-own_modes // n_tm)
    spare = n_tm * rows - own_modes
    f32 = jnp.float32

    dev, pos = np.arange(n_dev), np.arange(block)
    cos_a, sin_a = exp_table(dev[:, None] * dev[None, :], n_dev)
    cos_t, sin_t = exp_table(dev[:, None] * pos[None, :], total)
    cos_b, sin_b = exp_table(pos[:, None] * pos[None, :], block)
    first = jnp.asarray(block_matrix(cos_a, sin_a), f32)
    first_back = jnp.asarray(block_matrix(cos_a, -sin_a) / total, f32)
    last = jnp.asarray(block_matrix(cos_b, sin_b), f32)
    last_back = jnp.asarray(block_matrix(cos_b, -sin_b), f32)
    twist = (jnp.asarray(cos_t, f32), jnp.asarray(sin_t, f32))

    frequency = dev[:, None] + n_dev * pos[None, :]
    norm_freq = jnp.asarray(np.where(frequency < total // 2, frequency, frequency - total) * (2.0 / total), f32)
    rates = lax.dynamic_slice_in_dim(jnp.pad(betas, ((0, spare), (0, 0))), t_index * rows, rows, 0)
    rates = rates[:, :, None, None]
    phase = (
        rates[:, 0]
        + rates[:, 1] * norm_freq
        + rates[:, 2] * (norm_freq * norm_freq) / 2.0
        + rates[:, 3] * (norm_freq * norm_freq * norm_freq) / 6.0
    )
    half_turn = (jnp.cos(phase * 0.5), jnp.sin(phase * 0.5))
    full_turn = (jnp.cos(phase), jnp.sin(phase))

    def disperse(blocks, turn):
        x = jnp.einsum("arcb,cadk->drkb", blocks, first, precision=PRECISE)
        x = jnp.stack([x[0] * twist[0] + x[1] * twist[1], x[1] * twist[0] - x[0] * twist[1]], 0)
        x = jnp.einsum("crkb,cbdq->drkq", x, last, precision=PRECISE)
        x = jnp.stack([x[0] * turn[0] - x[1] * turn[1], x[0] * turn[1] + x[1] * turn[0]], 0)
        x = jnp.einsum("crkq,cqdb->drkb", x, last_back, precision=PRECISE)
        x = jnp.stack([x[0] * twist[0] - x[1] * twist[1], x[1] * twist[0] + x[0] * twist[1]], 0)
        return jnp.einsum("crkb,ckda->ardb", x, first_back, precision=PRECISE)

    raman = jnp.asarray(raman_matrix(block, halo), f32)
    all_profiles = lax.all_gather(modes, "mode", axis=1, tiled=True)
    all_modes = n_mode * own_modes

    def nonlinear(blocks):
        windows = jnp.stack([jnp.roll(blocks, halo - h, axis=0) for h in range(halo + 1)], 3)
        windows = lax.all_to_all(windows, BOTH, 0, 0, tiled=True)
        windows = windows.reshape(n_mode, n_tm * rows, 2, (halo + 1) * block)[:, :own_modes]
        windows = windows.reshape(all_modes, 2, (halo + 1) * block)
        grid = jnp.einsum("pg,pct->cgt", all_profiles, windows, precision=PRECISE)
        intensity = grid[0] * grid[0] + grid[1] * grid[1]
        delayed = jnp.dot(intensity, raman, precision=PRECISE)
        own = slice(halo * block, None)
        weight = (1.0 - RAMAN_SHARE) * intensity[:, own] + RAMAN_SHARE * delayed
        response = jnp.einsum("pg,cgt->pct", all_profiles, grid[:, :, own] * weight, precision=PRECISE)
        values = jnp.stack(
            [
                windows[:, 0, own] - KERR_GAIN * response[:, 1],
                windows[:, 1, own] + KERR_GAIN * response[:, 0],
            ],
            1,
        )
        values = jnp.pad(values.reshape(n_mode, own_modes, 2, block), ((0, 0), (0, spare), (0, 0), (0, 0)))
        return lax.all_to_all(values.reshape(n_dev, rows, 2, block), BOTH, 0, 0, tiled=True)

    entry = jnp.pad(field, ((0, spare), (0, 0), (0, 0))).reshape(n_tm, rows, 2, samples)
    entry = lax.all_to_all(entry, "tm", 0, 0, tiled=True)
    per_tm = samples // block
    blocks = entry.reshape(n_tm, rows, 2, per_tm, block).transpose(0, 3, 1, 2, 4).reshape(n_dev, rows, 2, block)
    blocks = disperse(blocks, half_turn)
    for number in range(ITERS):
        blocks = nonlinear(blocks)
        blocks = disperse(blocks, full_turn if number < ITERS - 1 else half_turn)
    leave = blocks.reshape(n_tm, per_tm, rows, 2, block).transpose(0, 2, 3, 1, 4).reshape(n_tm, rows, 2, samples)
    leave = lax.all_to_all(leave, "tm", 0, 0, tiled=True)
    return leave.reshape(n_tm * rows, 2, samples)[:own_modes]


def solution(mesh):
    return jax.shard_map(
        general,
        mesh=mesh,
        in_specs=(P("mode", None, "tm"), P(None, "mode"), P("mode", None)),
        out_specs=P("mode", None, "tm"),
        check_vma=False,
    )
```

time: 720 us -> 92.8 us (0.13); the launches traced: 707 us -> 92.2 us
  waiting for transfers between devices: 308 us -> 6 us
  starting transfers between devices: 162 us -> 9.94 us
  matrix products: 79.7 us -> 15.1 us
  local copies, waits for them, and re-layouts: 51.9 us -> 3.45 us
  other arithmetic: 31.4 us -> 2.89 us
  between operations: 16.4 us -> 0.49 us
    all_to_all x46 -> x2, waiting for transfers between devices: 262 us -> 6 us  [the longest x1 5.92 us: general(): entry = lax.all_to_all(entry, 'tm', 0, 0, tiled=True)]
    all_to_all x46 -> x2, starting transfers between devices: 162 us -> 9.94 us  [the longest x1 6.51 us: general(): entry = lax.all_to_all(entry, 'tm', 0, 0, tiled=True)]
    dot_general x154 -> x18, matrix products: 79.7 us -> 15.1 us  [the longest x2 5.32 us: nonlinear(): grid = jnp.einsum('pg,pct->cgt', all_profiles, windows, precision=PRECISE)]
    reduce_scatter x2 -> x0, waiting for transfers between devices: 45.6 us -> none  [shards(): lax.psum_scatter(jnp.stack([jnp.dot(modes, drive_real, precision=PRECISE)...]
    unnamed x72 -> x25, local copies, waits for them, and re-layouts: 29.9 us -> 1.19 us
    all_to_all x32 -> x0, other arithmetic: 25.3 us -> none  [the longest x16 12.7 us: shuffle_field(): lax.all_to_all(couple[1], 'tm', split_axis=1, concat_axis=2, tiled=True)]
    all_gather x4 -> x1, blocking collectives: 34 us -> 11.2 us  [general(): all_profiles = lax.all_gather(modes, 'mode', axis=1, tiled=True)]
    all_to_all x2 -> x4, blocking collectives: 24.2 us -> 43.1 us  [the longest x2 21.4 us: nonlinear(): lax.all_to_all(values.reshape(n_dev, rows, 2, block), BOTH, 0, 0, tiled=T...]
  transfers between devices with their start and end apart: 48 -> 2, of which waited for: 48 -> 2; matrix products, arithmetic and copies ran while one was open for 8% -> 0% of each run, Pallas kernels for 0% -> 0%
where the time goes in v1:
time: 92.8 us; the launch traced here: 92.2 us
  blocking collectives  54.4 us (59%)
  matrix products  15.1 us (16%)
  starting transfers between devices  9.94 us (11%)
  waiting for transfers between devices  6 us (6%)
  local copies, waits for them, and re-layouts  3.45 us (4%)
  other arithmetic  2.89 us (3%)
    all_to_all x2, blocking collectives, nonlinear(): lax.all_to_all(values.reshape(n_dev, rows, 2, block), BOTH, 0, 0, tiled=T...  21.4 us
    all_to_all x1, blocking collectives, nonlinear(): windows = lax.all_to_all(windows, BOTH, 0, 0, tiled=True)  13 us
    all_gather x1, blocking collectives, general(): all_profiles = lax.all_gather(modes, 'mode', axis=1, tiled=True)  11.2 us
    all_to_all x1, blocking collectives, general(): leave = lax.all_to_all(leave, 'tm', 0, 0, tiled=True)  8.7 us
    all_to_all x1, starting transfers between devices, general(): entry = lax.all_to_all(entry, 'tm', 0, 0, tiled=True)  6.51 us
    all_to_all x1, waiting for transfers between devices, general(): entry = lax.all_to_all(entry, 'tm', 0, 0, tiled=True)  5.92 us
    dot_general x2, matrix products, nonlinear(): grid = jnp.einsum('pg,pct->cgt', all_profiles, windows, precision=PRECISE)  5.32 us
    all_to_all x1, starting transfers between devices, nonlinear(): windows = lax.all_to_all(windows, BOTH, 0, 0, tiled=True)  3.43 us
  transfers between devices with their start and end apart: 2, of which 2 were waited for; matrix products, arithmetic and copies ran while one was open for 0% of the time, Pallas kernels for 0%

profile of v1, /device:TPU:0, one launch (start us, length us, event | category | flops | bytes accessed | tf_op | source)
XLA Modules:
  0.0 92.2 jit_solution(7750674868088641409)
XLA Ops:
  0.1 6.5 %all-to-all-start = ((f32[8,3,2,512]{3,2,1,0:T(2,128)}), f32[8,3,2,512]{3,2,1,0:T(2,128)S(1)}, u32[]{:S(2)}, u32[]{:S(2)}) async-start(f32[8,3,2,512]{3,2,1,0:T(2,128)} %bitcast.202), calls=%async_computation | async-start | bytes 196608 | tf_op jit(solution)/shard_map/all_to_all | solution.py:105
  7.0 5.9 %all-to-all-done = f32[8,3,2,512]{3,2,1,0:T(2,128)S(1)} async-done(((f32[8,3,2,512]{3,2,1,0:T(2,128)}), f32[8,3,2,512]{3,2,1,0:T(2,128)S(1)}, u32[]{:S(2)}, u32[]{:S(2)}) %all-to-all-start) | async-done | bytes 98336 | tf_op jit(solution)/shard_map/all_to_all | solution.py:105
  13.0 1.1 %convolution_bitcast_fusion.12 = f32[2,3,32,128]{3,2,0,1:T(8,128)S(1)} fusion(f32[2,32,2,32,1]{1,3,0,2,4:T(8,128)} %constant.49, f32[32,3,2,128,1]{3,2,1,0,4:T(2,128)S(1)} %bitcast.194), kind=kOutput, calls=%fused_computation.24 | convolution fusion | flops 18874368 | bytes 212992 | tf_op jit(solution)/shard_map/arcb,cadk->drkb/dot_general | solution.py:71
  14.1 0.8 multiply_add_fusion.9
  14.9 1.2 %convolution_bitcast_fusion.11 = f32[2,3,32,128]{3,2,0,1:T(8,128)S(1)} fusion(f32[2,128,2,128,1]{3,1,0,2,4:T(8,128)} %constant.50, f32[1,3,32,128]{3,2,0,1:T(8,128)S(1)} %get-tuple-element.30, f32[1,3,32,128]{3,2,0,1:T(8,128)S(1)} %get-tuple-element.29), kind=kOutput, calls=%fused_computation.23 | convolution fusion | flops 75522048 | bytes 458752 | tf_op jit(solution)/shard_map/crkb,cbdq->drkq/dot_general | solution.py:73
  16.1 0.3 multiply_subtract_fusion.7
  16.7 0.3 fusion.16
  17.1 0.9 %copy.34 = f32[32,3,2,3,128]{4,2,1,3,0:T(2,128)} copy(f32[32,3,2,3,128]{4,0,2,1,3:T(8,128)S(1)} %pad_maximum_fusion) | data formatting | bytes 589824 | tf_op jit(solution)/shard_map/stack | solution.py:84
  18.1 3.4 %all-to-all-start.1 = ((f32[32,3,2,3,128]{4,2,1,3,0:T(2,128)}), f32[32,3,2,3,128]{4,2,1,3,0:T(2,128)S(1)}, u32[]{:S(2)}, u32[]{:S(2)}) async-start(f32[32,3,2,3,128]{4,2,1,3,0:T(2,128)} %copy.34), calls=%async_computation.1 | async-start | bytes 589824 | tf_op jit(solution)/shard_map/all_to_all | solution.py:85
  21.5 11.2 %all_gather.3 = f32[96,1024]{1,0:T(8,128)S(1)} all-gather(f32[96,256]{1,0:T(8,128)S(1)} %copy-done.11), channel_id=1, replica_groups=mesh['mode'=4,'tm'=8] {'mode'}, dimensions={1}, use_global_device_ids=true | all-gather | bytes 491520 | tf_op jit(solution)/shard_map/all_gather | solution.py:80
  33.1 2.7 %convolution_bitcast_fusion.1 = f32[2,1024,384]{1,2,0:T(8,128)S(1)} fusion(f32[96,2,384]{2,0,1:T(8,128)S(1)} %reshape_reshape.6, f32[96,1024]{1,0:T(8,128)S(1)} %all_gather.3), kind=kOutput, calls=%fused_computation.1 | convolution fusion | flops 905969664 | bytes 3833856 | tf_op jit(solution)/shard_map/pg,pct->cgt/dot_general | solution.py:88
  35.8 0.4 fusion.3
  36.2 0.5 copy-done.3
  36.7 1.2 %fusion.5 = f32[1024,128]{0,1:T(8,128)S(1)} fusion(f32[1024,384]{0,1:T(8,128)S(1)} %fusion.3, f32[384,128]{1,0:T(8,128)S(1)} %copy-done.3), kind=kOutput, calls=%fused_computation.13 | convolution fusion | flops 604372992 | bytes 2818048 | tf_op jit(solution)/shard_map/dot_general | solution.py:90
  38.0 1.1 %convolution_bitcast_fusion.3 = f32[96,2,128]{2,0,1:T(8,128)S(1)} fusion(f32[2,1024,384]{1,2,0:T(8,128)S(1)} %convolution_bitcast_fusion.1, f32[1024,128]{0,1:T(8,128)S(1)} %fusion.5, f32[96,1024]{1,0:T(8,128)S(1)} %all_gather.3), kind=kOutput, calls=%fused_computation.15 | convolution fusion | flops 302252032 | bytes 2064384 | tf_op jit(solution)/shard_map/pg,cgt->pct/dot_general | solution.py:93
  39.2 11.7 %all_to_all.30 = f32[32,3,2,128]{3,2,1,0:T(2,128)S(1)} all-to-all(f32[32,3,2,128]{3,2,1,0:T(2,128)S(1)} %pad_maximum_fusion.3), channel_id=1, replica_groups=mesh['mode'=4,'tm'=8] {'mode','tm'}, dimensions={0} | all-to-all | bytes 196608 | tf_op jit(solution)/shard_map/all_to_all | solution.py:102
  50.9 0.3 convolution_bitcast_fusion.9
  51.2 0.3 convolution_bitcast_fusion.8
  51.5 0.3 multiply_subtract_fusion.4
  52.0 0.3 fusion.23
  52.7 13.0 %all_to_all.31 = f32[32,3,2,3,128]{4,2,1,3,0:T(2,128)S(1)} all-to-all(f32[32,3,2,3,128]{4,2,1,3,0:T(2,128)S(1)} %copy.39), channel_id=1, replica_groups=mesh['mode'=4,'tm'=8] {'mode','tm'}, dimensions={0} | all-to-all | bytes 589824 | tf_op jit(solution)/shard_map/all_to_all | solution.py:85
  66.0 2.7 %convolution_bitcast_fusion = f32[2,1024,384]{1,2,0:T(8,128)S(1)} fusion(f32[96,2,384]{2,0,1:T(8,128)S(1)} %reshape_reshape.7, f32[96,1024]{1,0:T(8,128)S(1)} %all_gather.3), kind=kOutput, calls=%fused_computation | convolution fusion | flops 905969664 | bytes 3833856 | tf_op jit(solution)/shard_map/pg,pct->cgt/dot_general | solution.py:88
  68.6 0.4 fusion.1
  69.1 1.2 %fusion.4 = f32[1024,128]{0,1:T(8,128)S(1)} fusion(f32[1024,384]{0,1:T(8,128)S(1)} %fusion.1, f32[384,128]{1,0:T(8,128)S(1)} %copy-done.3), kind=kOutput, calls=%fused_computation.11 | convolution fusion | flops 604372992 | bytes 2818048 | tf_op jit(solution)/shard_map/dot_general | solution.py:90
  70.3 1.1 %convolution_bitcast_fusion.2 = f32[96,2,128]{2,0,1:T(8,128)S(1)} fusion(f32[2,1024,384]{1,2,0:T(8,128)S(1)} %convolution_bitcast_fusion, f32[1024,128]{0,1:T(8,128)S(1)} %fusion.4, f32[96,1024]{1,0:T(8,128)S(1)} %all_gather.3), kind=kOutput, calls=%fused_computation.14 | convolution fusion | flops 302252032 | bytes 2064384 | tf_op jit(solution)/shard_map/pg,cgt->pct/dot_general | solution.py:93
  71.5 9.7 %all_to_all.32 = f32[32,3,2,128]{3,2,1,0:T(2,128)S(1)} all-to-all(f32[32,3,2,128]{3,2,1,0:T(2,128)S(1)} %pad_maximum_fusion.4), channel_id=1, replica_groups=mesh['mode'=4,'tm'=8] {'mode','tm'}, dimensions={0} | all-to-all | bytes 196608 | tf_op jit(solution)/shard_map/all_to_all | solution.py:102
  81.3 0.3 convolution_bitcast_fusion.6
  81.9 0.3 multiply_subtract_fusion.1
  82.1 0.3 convolution_bitcast_fusion.4
  82.4 0.3 fusion.30
  82.9 8.7 %all_to_all.33 = f32[8,3,2,512]{3,2,1,0:T(2,128)S(1)} all-to-all(f32[8,3,2,512]{3,2,1,0:T(2,128)S(1)} %copy.44), channel_id=1, replica_groups=mesh['mode'=4,'tm'=8] {'tm'}, dimensions={0} | all-to-all | bytes 196608 | tf_op jit(solution)/shard_map/all_to_all | solution.py:113
  91.6 0.6 copy.86
  (57 shorter events, 2.7 us)
Async XLA Ops:
  0.0 6.6 %copy-start = (f32[24,4]{0,1:T(4,128)S(1)}, f32[24,4]{0,1:T(4,128)}, u32[]{:S(2)}) copy-start(f32[24,4]{0,1:T(4,128)} %param.13) | copy-start | bytes 1156
  0.0 16.7 %copy-start.4 = (f32[32,128]{1,0:T(8,128)S(1)}, f32[32,128]{1,0:T(8,128)}, u32[]{:S(2)}) copy-start(f32[32,128]{1,0:T(8,128)} %constant.44.clone) | copy-start | bytes 49156
  0.0 16.7 %copy-start.5 = (f32[32,128]{1,0:T(8,128)S(1)}, f32[32,128]{1,0:T(8,128)}, u32[]{:S(2)}) copy-start(f32[32,128]{1,0:T(8,128)} %constant.43.clone) | copy-start | bytes 49156
  0.0 16.1 %copy-start.8 = (f32[32,128]{1,0:T(8,128)S(1)}, f32[32,128]{1,0:T(8,128)}, u32[]{:S(2)}) copy-start(f32[32,128]{1,0:T(8,128)} %constant.48) | copy-start | bytes 49156
  0.0 16.1 %copy-start.9 = (f32[32,128]{1,0:T(8,128)S(1)}, f32[32,128]{1,0:T(8,128)}, u32[]{:S(2)}) copy-start(f32[32,128]{1,0:T(8,128)} %constant.47) | copy-start | bytes 49156
  0.0 16.1 %copy-start.10 = (f32[32,128]{1,0:T(8,128)S(1)}, f32[32,128]{1,0:T(8,128)}, u32[]{:S(2)}) copy-start(f32[32,128]{1,0:T(8,128)} %constant.45.clone) | copy-start | bytes 49156
  0.0 16.4 %copy-start.1 = (f32[2,128,2,128,1]{3,1,0,2,4:T(8,128)S(1)}, f32[2,128,2,128,1]{3,1,0,2,4:T(8,128)}, u32[]{:S(2)}) copy-start(f32[2,128,2,128,1]{3,1,0,2,4:T(8,128)} %constant.51) | copy-start | bytes 786436
  0.1 16.7 %copy-start.6 = (f32[2,32,2,32,1]{1,3,0,2,4:T(8,128)S(1)}, f32[2,32,2,32,1]{1,3,0,2,4:T(8,128)}, u32[]{:S(2)}) copy-start(f32[2,32,2,32,1]{1,3,0,2,4:T(8,128)} %constant.52) | copy-start | bytes 49156
  0.1 12.8 %all-to-all-start = ((f32[8,3,2,512]{3,2,1,0:T(2,128)}), f32[8,3,2,512]{3,2,1,0:T(2,128)S(1)}, u32[]{:S(2)}, u32[]{:S(2)}) async-start(f32[8,3,2,512]{3,2,1,0:T(2,128)} %bitcast.202), calls=%async_computation | async-start | bytes 196608 | tf_op jit(solution)/shard_map/all_to_all | solution.py:105
  16.4 5.1 %copy-start.11 = (f32[96,256]{1,0:T(8,128)S(1)}, f32[96,256]{1,0:T(8,128)}, u32[]{:S(2)}) copy-start(f32[96,256]{1,0:T(8,128)} %param.12) | copy-start | bytes 294916
  18.1 14.8 %all-to-all-start.1 = ((f32[32,3,2,3,128]{4,2,1,3,0:T(2,128)}), f32[32,3,2,3,128]{4,2,1,3,0:T(2,128)S(1)}, u32[]{:S(2)}, u32[]{:S(2)}) async-start(f32[32,3,2,3,128]{4,2,1,3,0:T(2,128)} %copy.34), calls=%async_computation.1 | async-start | bytes 589824 | tf_op jit(solution)/shard_map/all_to_all | solution.py:85
  35.8 0.9 %copy-start.3 = (f32[384,128]{1,0:T(8,128)S(1)}, f32[384,128]{1,0:T(8,128)}, u32[]{:S(2)}) copy-start(f32[384,128]{1,0:T(8,128)} %constant.46.clone) | copy-start | bytes 589828
  37.9 12.9 %copy-start.7 = (f32[2,32,2,32,1]{1,3,0,2,4:T(8,128)S(1)}, f32[2,32,2,32,1]{1,3,0,2,4:T(8,128)}, u32[]{:S(2)}) copy-start(f32[2,32,2,32,1]{1,3,0,2,4:T(8,128)} %constant.49) | copy-start | bytes 49156
  37.9 13.2 %copy-start.2 = (f32[2,128,2,128,1]{3,1,0,2,4:T(8,128)S(1)}, f32[2,128,2,128,1]{3,1,0,2,4:T(8,128)}, u32[]{:S(2)}) copy-start(f32[2,128,2,128,1]{3,1,0,2,4:T(8,128)} %constant.50) | copy-start | bytes 786436

commit v2 on v1

--- a/solution.py
+++ b/solution.py
@@ -1,10 +1,14 @@
+import functools
 import math
 
 import jax
 import jax.numpy as jnp
 import numpy as np
 from jax import lax
+from jax.experimental import pallas as pl
+from jax.experimental.pallas import tpu as pltpu
 from jax.sharding import PartitionSpec as P
+
 
 RAMAN_TAPS = 256
 ITERS = 2
@@ -12,6 +16,7 @@
 KERR_GAIN = 6.0
 PRECISE = lax.Precision.HIGHEST
 BOTH = ("mode", "tm")
+PARAMS = pltpu.CompilerParams(vmem_limit_bytes=16 * 1024 * 1024)
 
 
 def exp_table(product, length):
@@ -114,9 +119,253 @@
     return leave.reshape(n_tm * rows, 2, samples)[:own_modes]
 
 
+def split_two(values):
+    high = values.astype(jnp.bfloat16)
+    return high, (values - high.astype(jnp.float32)).astype(jnp.bfloat16)
+
+
+def np_split(values):
+    high = values.astype(jnp.bfloat16)
+    return high, (values - high.astype(np.float64)).astype(jnp.bfloat16)
+
+
+def product(left, right):
+    return jnp.dot(left, right, preferred_element_type=jnp.float32)
+
+
+def turn_kernel(scale, rates_ref, freq_ref, half_ref, full_ref):
+    freq = freq_ref[...]
+    square = freq * freq
+    size = freq.shape[0]
+    for r in range(rates_ref.shape[0]):
+        phase = (
+            rates_ref[r, 0]
+            + rates_ref[r, 1] * freq
+            + rates_ref[r, 2] * square / 2.0
+            + rates_ref[r, 3] * (square * freq) / 6.0
+        )
+        cosine, sine = jnp.cos(phase * 0.5), jnp.sin(phase * 0.5)
+        part = pl.ds(r * size, size)
+        half_ref[0, part] = cosine * scale
+        half_ref[1, part] = sine * scale
+        full_ref[0, part] = (cosine * cosine - sine * sine) * scale
+        full_ref[1, part] = (2.0 * scale) * cosine * sine
+
+
+def disperse_kernel(rows, load, store, x_ref, first_ref, last_ref, twist_ref, turn_ref, final_ref, o_ref):
+    n_dev, block = twist_ref.shape[1:]
+    width = 2 * block
+    twist = [jnp.concatenate([twist_ref[c]] * rows, axis=1) for c in range(2)]
+
+    def across(matrix_ref, values):
+        high, low = split_two(values)
+        return product(matrix_ref[...], jnp.concatenate([high, high, low, low], axis=0))
+
+    def twisted(values):
+        re, im = values[:n_dev], values[n_dev:]
+        return re * twist[0] + im * twist[1], im * twist[0] - re * twist[1]
+
+    def along(re, im):
+        high, low = split_two(jnp.concatenate([re, im], axis=1))
+        both = product(jnp.concatenate([high, low], axis=0), last_ref[:, :width])
+        size = high.shape[0]
+        return both[:size] + both[size:] + product(high, last_ref[:, width:])
+
+    def row_of(values):
+        return jnp.concatenate([values[:, r * block : (r + 1) * block] for r in range(rows)], axis=0)
+
+    def lane_of(values):
+        return jnp.concatenate([values[r * n_dev : (r + 1) * n_dev] for r in range(rows)], axis=1)
+
+    x = jnp.concatenate(
+        [jnp.concatenate([load(x_ref, r, c) for r in range(rows)], axis=1) for c in range(2)], axis=0
+    )
+    re, im = twisted(across(first_ref, x))
+    z = along(row_of(re), row_of(im))
+    z_re, z_im = z[:, :block], z[:, block:]
+    turn_re, turn_im = turn_ref[0], turn_ref[1]
+    z = along(z_re * turn_re - z_im * turn_im, -(z_re * turn_im + z_im * turn_re))
+    re, im = twisted(jnp.concatenate([lane_of(z[:, :block]), lane_of(z[:, block:])], axis=0))
+    x = across(final_ref, jnp.concatenate([re, im], axis=0))
+    for r in range(rows):
+        lanes = slice(r * block, (r + 1) * block)
+        store(o_ref, r, 0, x[:n_dev, lanes])
+        store(o_ref, r, 1, -x[n_dev:, lanes])
+
+
+def nonlinear_kernel(rows, halo, step, w_ref, up_ref, down_ref, raman_ref, o_ref):
+    block = w_ref.shape[1]
+    span = (halo + 1) * block
+    n_dev = w_ref.shape[0] // ((halo + 1) * rows * 2)
+    n_modes = n_dev * rows
+    n_grid = up_ref.shape[0]
+    chunk = (halo + 1) * rows * 2
+
+    def window(c):
+        return jnp.concatenate(
+            [
+                jnp.concatenate(
+                    [w_ref[pl.ds(h * 2 * rows + 2 * r + c, n_dev, stride=chunk), :] for r in range(rows)], axis=0
+                )
+                for h in range(halo + 1)
+            ],
+            axis=1,
+        )
+
+    values = [window(0), window(1)]
+    high, low = split_two(jnp.concatenate(values, axis=1))
+    high = jnp.concatenate([high, high], axis=0)
+    low = jnp.concatenate([low, low], axis=0)
+    response = None
+    for start in range(0, n_grid, step):
+        up = up_ref[start : start + step, :]
+        grid = product(up, low) + product(up, high)
+        g_re, g_im = grid[:, :span], grid[:, span:]
+        intensity = g_re * g_re + g_im * g_im
+        i_high, i_low = split_two(intensity)
+        both = product(i_high, raman_ref[...])
+        delayed = both[:, :block] + both[:, block:] + product(i_low, raman_ref[:, :block])
+        weight = (1.0 - RAMAN_SHARE) * intensity[:, halo * block :] + delayed
+        drive = jnp.concatenate([g_re[:, halo * block :] * weight, g_im[:, halo * block :] * weight], axis=1)
+        d_high, d_low = split_two(drive)
+        both = product(down_ref[:, start : start + step], d_high)
+        part = both[:n_modes] + both[n_modes:] + product(down_ref[:n_modes, start : start + step], d_low)
+        response = part if response is None else response + part
+    out = [
+        values[0][:, halo * block :] - KERR_GAIN * response[:, block:],
+        values[1][:, halo * block :] + KERR_GAIN * response[:, :block],
+    ]
+    for c in range(2):
+        for r in range(rows):
+            o_ref[pl.ds(2 * r + c, n_dev, stride=2 * rows), :] = out[c][r * n_dev : (r + 1) * n_dev]
+
+
+def tiled(field, modes, betas):
+    n_mode, n_tm = lax.axis_size("mode"), lax.axis_size("tm")
+    t_index = lax.axis_index("tm")
+    own_modes, _, samples = field.shape
+    n_dev = n_mode * n_tm
+    total = samples * n_tm
+    block = total // n_dev
+    halo = -(-RAMAN_TAPS // block)
+    rows = own_modes // n_tm
+    per_tm = samples // block
+    f32 = jnp.float32
+
+    pieces = [modes]
+    for shift in range(1, n_mode):
+        pieces.append(lax.ppermute(modes, "mode", [(i, (i + shift) % n_mode) for i in range(n_mode)]))
+    profiles = jnp.concatenate(pieces, axis=1)
+    profiles = profiles.reshape(n_dev, rows, -1).transpose(1, 0, 2).reshape(n_dev * rows, -1)
+    high = lax.reduce_precision(profiles, 8, 7)
+    low = profiles - high
+    down = jnp.concatenate([high, low], axis=0).astype(jnp.bfloat16)
+    up = down.T
+
+    dev, pos = np.arange(n_dev), np.arange(block)
+    cos_a, sin_a = exp_table(dev[:, None] * dev[None, :], n_dev)
+    cos_t, sin_t = exp_table(dev[:, None] * pos[None, :], total)
+    cos_b, sin_b = exp_table(pos[:, None] * pos[None, :], block)
+    first = block_matrix(cos_a, sin_a).transpose(2, 3, 0, 1)
+    last = block_matrix(cos_b, sin_b).reshape(2 * block, 2 * block)
+    last = jnp.asarray(np.concatenate(np_split(last), axis=1))
+    twist = jnp.asarray(np.stack([cos_t, sin_t]), f32)
+    edge = np.arange(n_dev).reshape(n_tm, per_tm).T.reshape(-1)
+
+    def flat(matrix):
+        high, low = np_split(matrix.reshape(2 * n_dev, 2 * n_dev))
+        return jnp.asarray(np.concatenate([high, low, high, low], axis=1))
+
+    frequency = dev[:, None] + n_dev * pos[None, :]
+    norm_freq = jnp.asarray(np.where(frequency < total // 2, frequency, frequency - total) * (2.0 / total), f32)
+    rates = lax.dynamic_slice_in_dim(betas, t_index * rows, rows, 0)
+    table = jax.ShapeDtypeStruct((2, rows * n_dev, block), f32)
+    half_turn, full_turn = pl.pallas_call(
+        functools.partial(turn_kernel, 1.0 / total),
+        out_shape=(table, table),
+        in_specs=[pl.BlockSpec(memory_space=pltpu.SMEM), pl.BlockSpec(memory_space=pltpu.VMEM)],
+        name="turns",
+        compiler_params=PARAMS,
+    )(rates, norm_freq)
+
+    def load_edge(ref, r, c):
+        return jnp.concatenate([ref[:, r, c, q * block : (q + 1) * block] for q in range(per_tm)], axis=0)
+
+    def load_inner(ref, r, c):
+        return ref[pl.ds(2 * r + c, n_dev, stride=2 * rows), :]
+
+    def store_edge(ref, r, c, values):
+        for q in range(per_tm):
+            ref[:, r, c, q * block : (q + 1) * block] = values[q * n_tm : (q + 1) * n_tm]
+
+    def store_inner(ref, r, c, values):
+        for h in range(halo + 1):
+            moved = pltpu.roll(values, halo - h, axis=0) if h < halo else values
+            ref[pl.ds(2 * (h * rows + r) + c, n_dev, stride=2 * (halo + 1) * rows), :] = moved
+
+    def disperse(values, turn, entering, leaving):
+        shape = (n_tm, rows, 2, samples) if leaving else (n_dev * (halo + 1) * rows * 2, block)
+        return pl.pallas_call(
+            functools.partial(
+                disperse_kernel,
+                rows,
+                load_edge if entering else load_inner,
+                store_edge if leaving else store_inner,
+            ),
+            out_shape=jax.ShapeDtypeStruct(shape, f32),
+            name="disperse",
+            compiler_params=PARAMS,
+        )(
+            values,
+            flat(first[..., edge] if entering else first),
+            last,
+            twist,
+            turn,
+            flat(first[:, edge] if leaving else first),
+        )
+
+    taps = RAMAN_SHARE * raman_matrix(block, halo)
+    raman = jnp.asarray(np.concatenate(np_split(taps), axis=1))
+    step = math.gcd(up.shape[0], 256)
+
+    def nonlinear(windows):
+        return pl.pallas_call(
+            functools.partial(nonlinear_kernel, rows, halo, step),
+            out_shape=jax.ShapeDtypeStruct((n_dev * rows * 2, block), f32),
+            name="nonlinear",
+            compiler_params=PARAMS,
+        )(windows, up, down, raman)
+
+    def exchange(values):
+        shaped = values.reshape(n_dev, -1, 2, block)
+        return lax.all_to_all(shaped, BOTH, 0, 0, tiled=True).reshape(-1, block)
+
+    values = lax.all_to_all(field.reshape(n_tm, rows, 2, samples), "tm", 0, 0, tiled=True)
+    values = disperse(values, half_turn, True, False)
+    for number in range(ITERS):
+        values = exchange(values)
+        values = nonlinear(values)
+        leaving = number == ITERS - 1
+        values = disperse(exchange(values), half_turn if leaving else full_turn, False, leaving)
+    return lax.all_to_all(values, "tm", 0, 0, tiled=True).reshape(field.shape)
+
+
+def shards(field, modes, betas):
+    n_mode, n_tm = lax.axis_size("mode"), lax.axis_size("tm")
+    fits = (
+        field.shape[2] % (128 * n_mode) == 0
+        and field.shape[0] % n_tm == 0
+        and n_tm % 8 == 0
+        and modes.shape[1] % 128 == 0
+    )
+    if not fits:
+        return general(field, modes, betas)
+    return tiled(field, modes, betas)
+
+
 def solution(mesh):
     return jax.shard_map(
-        general,
+        shards,
         mesh=mesh,
         in_specs=(P("mode", None, "tm"), P(None, "mode"), P("mode", None)),
         out_specs=P("mode", None, "tm"),

time: 92.8 us -> 79.1 us (0.85)
  matrix products: 15.1 us -> 0 us
  blocking collectives: 54.4 us -> 41.3 us
  Pallas kernels: 0 us -> 8.93 us
  waiting for transfers between devices: 6 us -> 11.3 us
  starting transfers between devices: 9.94 us -> 14.4 us
  other arithmetic: 2.89 us -> 0.16 us
  local copies, waits for them, and re-layouts: 3.45 us -> 2.4 us
    dot_general x18 -> x0, matrix products: 15.1 us -> none  [the longest x2 5.32 us: nonlinear(): grid = jnp.einsum('pg,pct->cgt', all_profiles, windows, precision=PRECISE)]
    all_gather x1 -> x0, blocking collectives: 11.2 us -> none  [general(): all_profiles = lax.all_gather(modes, 'mode', axis=1, tiled=True)]
    pallas_call x0 -> x6, Pallas kernels: none -> 8.93 us  [the longest x2 5.25 us: nonlinear(): pl.pallas_call(functools.partial(nonlinear_kernel, rows, halo, step), out...]
    all_to_all x2, waiting for transfers between devices: 6 us -> 11.3 us  [the longest x1 10.5 us: exchange(): return lax.all_to_all(shaped, BOTH, 0, 0, tiled=True).reshape(-1, block)]
    ppermute x0 -> x3, starting transfers between devices: none -> 4.51 us  [tiled(): lax.ppermute(modes, 'mode', [(i, (i + shift) % n_mode) for i in range(n_m...]
    all_to_all x4, blocking collectives: 43.1 us -> 41.3 us  [the longest x3 32.6 us: exchange(): return lax.all_to_all(shaped, BOTH, 0, 0, tiled=True).reshape(-1, block)]
    add x5 -> x0, other arithmetic: 1.65 us -> none  [the longest x2 0.86 us: nonlinear(): intensity = grid[0] * grid[0] + grid[1] * grid[1]]
    another operation x5 -> x0, local copies, waits for them, and re-layouts: 1.52 us -> none  [the longest x2 1.17 us: nonlinear(): jnp.stack([jnp.roll(blocks, halo - h, axis=0) for h in range(halo + 1)], 3)]
  transfers between devices with their start and end apart: 2 -> 5, of which waited for: 2 -> 2; matrix products, arithmetic and copies ran while one was open for 0% -> 1% of each run, Pallas kernels for 0% -> 3%
where the time goes in v2:
time: 79.1 us; the launch traced here: 78.7 us
  blocking collectives  41.3 us (52%)
  starting transfers between devices  14.4 us (18%)
  waiting for transfers between devices  11.3 us (14%)
  Pallas kernels  8.93 us (11%)
  local copies, waits for them, and re-layouts  2.4 us (3%)
    all_to_all x3, blocking collectives, exchange(): return lax.all_to_all(shaped, BOTH, 0, 0, tiled=True).reshape(-1, block)  32.6 us
    all_to_all x1, waiting for transfers between devices, exchange(): return lax.all_to_all(shaped, BOTH, 0, 0, tiled=True).reshape(-1, block)  10.5 us
    all_to_all x1, blocking collectives, tiled(): return lax.all_to_all(values, 'tm', 0, 0, tiled=True).reshape(field.shape)  8.7 us
    all_to_all x1, starting transfers between devices, tiled(): lax.all_to_all(field.reshape(n_tm, rows, 2, samples), 'tm', 0, 0, tiled=T...  6.51 us
    pallas_call x2, Pallas kernels, nonlinear(): pl.pallas_call(functools.partial(nonlinear_kernel, rows, halo, step), out...  5.25 us
    ppermute x3, starting transfers between devices, tiled(): lax.ppermute(modes, 'mode', [(i, (i + shift) % n_mode) for i in range(n_m...  4.51 us
    all_to_all x1, starting transfers between devices, exchange(): return lax.all_to_all(shaped, BOTH, 0, 0, tiled=True).reshape(-1, block)  3.43 us
    pallas_call x3, Pallas kernels, disperse(): pl.pallas_call(functools.partial(disperse_kernel, rows, load_edge if ente...  2.9 us
  transfers between devices with their start and end apart: 5, of which 2 were waited for; matrix products, arithmetic and copies ran while one was open for 1% of the time, Pallas kernels for 3%

profile of v2, /device:TPU:0, one launch (start us, length us, event | category | flops | bytes accessed | tf_op | source)
XLA Modules:
  0.0 78.7 jit_solution(10226099646296823521)
XLA Ops:
  0.0 0.0 copy-start.7
  0.0 6.5 %all-to-all-start = ((f32[8,3,2,512]{3,2,1,0:T(2,128)}), f32[8,3,2,512]{3,2,1,0:T(2,128)S(1)}, u32[]{:S(2)}, u32[]{:S(2)}) async-start(f32[8,3,2,512]{3,2,1,0:T(2,128)} %bitcast.25), calls=%async_computation | async-start | bytes 196608 | tf_op jit(solution)/shard_map/all_to_all | solution.py:343
  6.5 0.0 copy-start.4
  6.6 1.6 %collective-permute-start.1 = (f32[96,256]{1,0:T(8,128)S(1)}, f32[96,256]{1,0:T(8,128)S(1)}, u32[]{:S(2)}, u32[]{:S(2)}) collective-permute-start(f32[96,256]{1,0:T(8,128)S(1)} %copy-done.9), channel_id=1, source_target_pairs={{0,16},{8,24},{16,0},{24,8},{1,17},{9,25},{17,1},{25,9},{2,18},{10... | collective-permute-start | bytes 294920 | tf_op jit(solution)/shard_map/ppermute | solution.py:257
  8.1 1.5 %collective-permute-start = (f32[96,256]{1,0:T(8,128)S(1)}, f32[96,256]{1,0:T(8,128)S(1)}, u32[]{:S(2)}, u32[]{:S(2)}) collective-permute-start(f32[96,256]{1,0:T(8,128)S(1)} %copy-done.9), channel_id=1, source_target_pairs={{0,8},{8,16},{16,24},{24,0},{1,9},{9,17},{17,25},{25,1},{2,10},{10... | collective-permute-start | bytes 294920 | tf_op jit(solution)/shard_map/ppermute | solution.py:257
  9.6 1.4 %collective-permute-start.2 = (f32[96,256]{1,0:T(8,128)S(1)}, f32[96,256]{1,0:T(8,128)S(1)}, u32[]{:S(2)}, u32[]{:S(2)}) collective-permute-start(f32[96,256]{1,0:T(8,128)S(1)} %copy-done.9), channel_id=1, source_target_pairs={{0,24},{8,0},{16,8},{24,16},{1,25},{9,1},{17,9},{25,17},{2,26},{10... | collective-permute-start | bytes 294920 | tf_op jit(solution)/shard_map/ppermute | solution.py:257
  11.1 0.1 constant_dynamic-slice_fusion
  11.1 0.1 copy.22.rates_ref
  11.2 0.8 turns.1
  12.0 0.8 %all-to-all-done.x_ref = f32[8,3,2,512]{3,2,1,0:T(2,128)S(1)} async-done(((f32[8,3,2,512]{3,2,1,0:T(2,128)}), f32[8,3,2,512]{3,2,1,0:T(2,128)S(1)}, u32[]{:S(2)}, u32[]{:S(2)}) %all-to-all-start) | async-done | bytes 98336 | tf_op jit(solution)/shard_map/all_to_all | solution.py:343
  12.9 0.0 copy-start.1
  12.9 0.9 %copy-done.1 = bf16[256,512]{1,0:T(8,128)(2,1)S(1)} copy-done((bf16[256,512]{1,0:T(8,128)(2,1)S(1)}, bf16[256,512]{1,0:T(8,128)(2,1)}, u32[]{:S(2)}) %copy-start.1) | copy-done | bytes 262168
  13.8 1.5 %disperse.3 = f32[576,128]{1,0:T(8,128)} custom-call(f32[8,3,2,512]{3,2,1,0:T(2,128)S(1)} %all-to-all-done.x_ref, bf16[64,256]{1,0:T(8,128)(2,1)S(1)} %copy-done.7, bf16[256,512]{1,0:T(8,128)(2,1)S(1)} %copy-done.1, f32[2,32,128]{2,1,0:T(8,128)S(1)} %copy-done.5, f32[2,96,128]{2,1,0:T(8,128)S(1)} %get-tuple-element.7.turn_ref, bf16[64,256]{1,0:T(8,128)(2,1)S(1)} %copy-done.4), custom_call_target="tpu_custom_call" | custom-call | tf_op jit(solution)/shard_map/disperse/pallas_call | solution.py:308
  15.3 3.4 %all-to-all-start.1 = ((f32[32,9,2,128]{3,2,1,0:T(2,128)}), f32[32,9,2,128]{3,2,1,0:T(2,128)S(1)}, u32[]{:S(2)}, u32[]{:S(2)}) async-start(f32[32,9,2,128]{3,2,1,0:T(2,128)} %bitcast.1), calls=%async_computation.1 | async-start | bytes 589824 | tf_op jit(solution)/shard_map/all_to_all | solution.py:341
  18.7 0.0 collective-permute-done
  18.7 0.0 collective-permute-done.2
  18.8 0.2 reshape.39
  19.0 0.2 copy.19
  19.3 0.1 pad_maximum_fusion.1
  19.3 0.0 copy-start.3
  19.4 0.2 copy.20.up_ref
  19.6 10.5 %all-to-all-done.1 = f32[32,9,2,128]{3,2,1,0:T(2,128)S(1)} async-done(((f32[32,9,2,128]{3,2,1,0:T(2,128)}), f32[32,9,2,128]{3,2,1,0:T(2,128)S(1)}, u32[]{:S(2)}, u32[]{:S(2)}) %all-to-all-start.1) | async-done | bytes 294944 | tf_op jit(solution)/shard_map/all_to_all | solution.py:341
  30.0 2.6 %nonlinear.2 = f32[192,128]{1,0:T(8,128)S(1)} custom-call(f32[576,128]{1,0:T(8,128)S(1)} %bitcast.17, bf16[1024,192]{1,0:T(8,128)(2,1)S(1)} %copy.20.up_ref, bf16[192,1024]{1,0:T(8,128)(2,1)S(1)} %get-tuple-element.9.down_ref, bf16[384,256]{1,0:T(8,128)(2,1)S(1)} %copy-done.3), custom_call_target="tpu_custom_call" | custom-call | tf_op jit(solution)/shard_map/nonlinear/pallas_call | solution.py:332
  32.7 9.8 %all_to_all.30 = f32[32,3,2,128]{3,2,1,0:T(2,128)S(1)} all-to-all(f32[32,3,2,128]{3,2,1,0:T(2,128)S(1)} %bitcast.21), channel_id=1, replica_groups=mesh['mode'=4,'tm'=8] {'mode','tm'}, dimensions={0} | all-to-all | bytes 196608 | tf_op jit(solution)/shard_map/all_to_all | solution.py:341
  42.5 0.7 disperse.4
  43.2 13.0 %all_to_all.31 = f32[32,9,2,128]{3,2,1,0:T(2,128)S(1)} all-to-all(f32[32,9,2,128]{3,2,1,0:T(2,128)S(1)} %bitcast.16), channel_id=1, replica_groups=mesh['mode'=4,'tm'=8] {'mode','tm'}, dimensions={0} | all-to-all | bytes 589824 | tf_op jit(solution)/shard_map/all_to_all | solution.py:341
  56.2 2.6 %nonlinear.3 = f32[192,128]{1,0:T(8,128)S(1)} custom-call(f32[576,128]{1,0:T(8,128)S(1)} %bitcast.18, bf16[1024,192]{1,0:T(8,128)(2,1)S(1)} %copy.20.up_ref, bf16[192,1024]{1,0:T(8,128)(2,1)S(1)} %get-tuple-element.9.down_ref, bf16[384,256]{1,0:T(8,128)(2,1)S(1)} %copy-done.3), custom_call_target="tpu_custom_call" | custom-call | tf_op jit(solution)/shard_map/nonlinear/pallas_call | solution.py:332
  58.9 0.0 copy-start.6
  58.9 9.7 %all_to_all.32 = f32[32,3,2,128]{3,2,1,0:T(2,128)S(1)} all-to-all(f32[32,3,2,128]{3,2,1,0:T(2,128)S(1)} %bitcast.20), channel_id=1, replica_groups=mesh['mode'=4,'tm'=8] {'mode','tm'}, dimensions={0} | all-to-all | bytes 196608 | tf_op jit(solution)/shard_map/all_to_all | solution.py:341
  68.6 0.7 disperse.5
  69.3 8.7 %all_to_all.33 = f32[8,3,2,512]{3,2,1,0:T(2,128)S(1)} all-to-all(f32[8,3,2,512]{3,2,1,0:T(2,128)S(1)} %disperse.5), channel_id=1, replica_groups=mesh['mode'=4,'tm'=8] {'tm'}, dimensions={0} | all-to-all | bytes 196608 | tf_op jit(solution)/shard_map/all_to_all | solution.py:350
  78.0 0.6 copy.24
  (17 shorter events, 0.1 us)
Async XLA Ops:
  0.0 11.1 %copy-start = (f32[24,4]{0,1:T(4,128)S(1)}, f32[24,4]{0,1:T(4,128)}, u32[]{:S(2)}) copy-start(f32[24,4]{0,1:T(4,128)} %param.15) | copy-start | bytes 1156
  0.0 6.5 %copy-start.9 = (f32[96,256]{1,0:T(8,128)S(1)}, f32[96,256]{1,0:T(8,128)}, u32[]{:S(2)}) copy-start(f32[96,256]{1,0:T(8,128)} %param.14) | copy-start | bytes 294916
  0.0 11.2 %copy-start.8 = (f32[32,128]{1,0:T(8,128)S(1)}, f32[32,128]{1,0:T(8,128)}, u32[]{:S(2)}) copy-start(f32[32,128]{1,0:T(8,128)} %constant.26.clone.freq_ref) | copy-start | bytes 49156
  0.0 12.8 %copy-start.5 = (f32[2,32,128]{2,1,0:T(8,128)S(1)}, f32[2,32,128]{2,1,0:T(8,128)}, u32[]{:S(2)}) copy-start(f32[2,32,128]{2,1,0:T(8,128)} %constant.25.clone.twist_ref) | copy-start | bytes 98308
  0.0 12.8 %copy-start.7 = (bf16[64,256]{1,0:T(8,128)(2,1)S(1)}, bf16[64,256]{1,0:T(8,128)(2,1)}, u32[]{:S(2)}) copy-start(bf16[64,256]{1,0:T(8,128)(2,1)} %constant.28.clone.first_ref) | copy-start | bytes 98308
  0.0 12.8 %all-to-all-start = ((f32[8,3,2,512]{3,2,1,0:T(2,128)}), f32[8,3,2,512]{3,2,1,0:T(2,128)S(1)}, u32[]{:S(2)}, u32[]{:S(2)}) async-start(f32[8,3,2,512]{3,2,1,0:T(2,128)} %bitcast.25), calls=%async_computation | async-start | bytes 196608 | tf_op jit(solution)/shard_map/all_to_all | solution.py:343
  6.5 6.3 %copy-start.4 = (bf16[64,256]{1,0:T(8,128)(2,1)S(1)}, bf16[64,256]{1,0:T(8,128)(2,1)}, u32[]{:S(2)}) copy-start(bf16[64,256]{1,0:T(8,128)(2,1)} %constant.29.clone.final_ref.first_ref) | copy-start | bytes 98308
  6.6 12.2 %collective-permute-start.1 = (f32[96,256]{1,0:T(8,128)S(1)}, f32[96,256]{1,0:T(8,128)S(1)}, u32[]{:S(2)}, u32[]{:S(2)}) collective-permute-start(f32[96,256]{1,0:T(8,128)S(1)} %copy-done.9), channel_id=1, source_target_pairs={{0,16},{8,24},{16,0},{24,8},{1,17},{9,25},{17,1},{25,9},{2,18},{10... | collective-permute-start | bytes 294920 | tf_op jit(solution)/shard_map/ppermute | solution.py:257
  8.1 10.6 %collective-permute-start = (f32[96,256]{1,0:T(8,128)S(1)}, f32[96,256]{1,0:T(8,128)S(1)}, u32[]{:S(2)}, u32[]{:S(2)}) collective-permute-start(f32[96,256]{1,0:T(8,128)S(1)} %copy-done.9), channel_id=1, source_target_pairs={{0,8},{8,16},{16,24},{24,0},{1,9},{9,17},{17,25},{25,1},{2,10},{10... | collective-permute-start | bytes 294920 | tf_op jit(solution)/shard_map/ppermute | solution.py:257
  9.6 9.1 %collective-permute-start.2 = (f32[96,256]{1,0:T(8,128)S(1)}, f32[96,256]{1,0:T(8,128)S(1)}, u32[]{:S(2)}, u32[]{:S(2)}) collective-permute-start(f32[96,256]{1,0:T(8,128)S(1)} %copy-done.9), channel_id=1, source_target_pairs={{0,24},{8,0},{16,8},{24,16},{1,25},{9,1},{17,9},{25,17},{2,26},{10... | collective-permute-start | bytes 294920 | tf_op jit(solution)/shard_map/ppermute | solution.py:257
  12.9 1.0 %copy-start.1 = (bf16[256,512]{1,0:T(8,128)(2,1)S(1)}, bf16[256,512]{1,0:T(8,128)(2,1)}, u32[]{:S(2)}) copy-start(bf16[256,512]{1,0:T(8,128)(2,1)} %constant.24.clone.last_ref) | copy-start | bytes 786436
  15.3 14.8 %all-to-all-start.1 = ((f32[32,9,2,128]{3,2,1,0:T(2,128)}), f32[32,9,2,128]{3,2,1,0:T(2,128)S(1)}, u32[]{:S(2)}, u32[]{:S(2)}) async-start(f32[32,9,2,128]{3,2,1,0:T(2,128)} %bitcast.1), calls=%async_computation.1 | async-start | bytes 589824 | tf_op jit(solution)/shard_map/all_to_all | solution.py:341
  19.3 10.7 %copy-start.3 = (bf16[384,256]{1,0:T(8,128)(2,1)S(1)}, bf16[384,256]{1,0:T(8,128)(2,1)}, u32[]{:S(2)}) copy-start(bf16[384,256]{1,0:T(8,128)(2,1)} %constant.27.clone.raman_ref) | copy-start | bytes 589828
  30.0 12.5 %copy-start.2 = (bf16[256,512]{1,0:T(8,128)(2,1)S(1)}, bf16[256,512]{1,0:T(8,128)(2,1)}, u32[]{:S(2)}) copy-start(bf16[256,512]{1,0:T(8,128)(2,1)} %constant.24.clone.last_ref) | copy-start | bytes 786436
  58.9 9.7 %copy-start.6 = (bf16[64,256]{1,0:T(8,128)(2,1)S(1)}, bf16[64,256]{1,0:T(8,128)(2,1)}, u32[]{:S(2)}) copy-start(bf16[64,256]{1,0:T(8,128)(2,1)} %constant.30.clone.final_ref) | copy-start | bytes 98308

commit v3 on v2

--- a/solution.py
+++ b/solution.py
@@ -6,6 +6,7 @@
 import numpy as np
 from jax import lax
 from jax.experimental import pallas as pl
+from jax.experimental.layout import Layout, with_layout_constraint
 from jax.experimental.pallas import tpu as pltpu
 from jax.sharding import PartitionSpec as P
 
@@ -28,11 +29,15 @@
     return np.stack([np.stack([cosine, -sine], 1), np.stack([sine, cosine], 1)], 0)
 
 
-def raman_matrix(block, halo):
+def raman_taps():
     positions = np.arange(1, RAMAN_TAPS + 1)
     spacing = 256.0 / RAMAN_TAPS
     raw = np.exp(-positions * spacing / 32.0) * np.sin(positions * spacing / 12.2)
-    taps = raw / raw.sum()
+    return raw / raw.sum()
+
+
+def raman_matrix(block, halo):
+    taps = raman_taps()
     lag = np.arange(block)[None, :] + halo * block - np.arange((halo + 1) * block)[:, None]
     return np.where((lag >= 1) & (lag <= RAMAN_TAPS), taps[np.clip(lag, 1, RAMAN_TAPS) - 1], 0.0)
 
@@ -133,7 +138,12 @@
     return jnp.dot(left, right, preferred_element_type=jnp.float32)
 
 
-def turn_kernel(scale, rates_ref, freq_ref, half_ref, full_ref):
+def turn_kernel(scale, rates_ref, freq_ref, taps_ref, half_ref, full_ref, raman_ref):
+    window, double = raman_ref.shape
+    block = double // 2
+    taps = jnp.broadcast_to(taps_ref[0:1, :], (window, taps_ref.shape[1]))
+    taps = pltpu.roll(taps, block, axis=1, stride=1, stride_axis=0)[:, :block]
+    raman_ref[...] = jnp.concatenate(split_two(taps), axis=1)
     freq = freq_ref[...]
     square = freq * freq
     size = freq.shape[0]
@@ -152,14 +162,36 @@
         full_ref[1, part] = (2.0 * scale) * cosine * sine
 
 
-def disperse_kernel(rows, load, store, x_ref, first_ref, last_ref, twist_ref, turn_ref, final_ref, o_ref):
+def profile_kernel(rows, *refs):
+    pieces, (up_ref, down_ref) = refs[:-3], refs[-2:]
+    count = pieces[0].shape[0]
+    n_dev = count // rows
+    place, mode = (lax.broadcasted_iota(jnp.int32, (count, count), d) for d in range(2))
+    order = (mode == (place % n_dev) * rows + place // n_dev).astype(jnp.float32).astype(jnp.bfloat16)
+    start = 0
+    for piece in pieces:
+        width = piece.shape[1]
+        wide, low = (product(order, part) for part in split_two(piece[...]))
+        down_ref[:, start : start + width] = jnp.concatenate([wide, low], axis=0).astype(jnp.bfloat16)
+        stack = jnp.concatenate([wide, low, wide, low], axis=0)
+        up_ref[start : start + width, :] = stack.T.astype(jnp.bfloat16)
+        start += width
+
+
+def disperse_kernel(rows, load, store, x_ref, first_ref, last_ref, twist_ref, turn_ref, o_ref):
     n_dev, block = twist_ref.shape[1:]
-    width = 2 * block
+    cos_high, sin_high, cos_low, sin_low = (last_ref[:, n * block : (n + 1) * block] for n in range(4))
+    last_high = jnp.concatenate(
+        [jnp.concatenate([cos_high, -sin_high], axis=1), jnp.concatenate([sin_high, cos_high], axis=1)], axis=0
+    )
+    last_low = jnp.concatenate(
+        [jnp.concatenate([cos_low, -sin_low], axis=1), jnp.concatenate([sin_low, cos_low], axis=1)], axis=0
+    )
     twist = [jnp.concatenate([twist_ref[c]] * rows, axis=1) for c in range(2)]
 
-    def across(matrix_ref, values):
+    def across(place, values):
         high, low = split_two(values)
-        return product(matrix_ref[...], jnp.concatenate([high, high, low, low], axis=0))
+        return product(first_ref[place], jnp.concatenate([high, high, low, low], axis=0))
 
     def twisted(values):
         re, im = values[:n_dev], values[n_dev:]
@@ -167,9 +199,9 @@
 
     def along(re, im):
         high, low = split_two(jnp.concatenate([re, im], axis=1))
-        both = product(jnp.concatenate([high, low], axis=0), last_ref[:, :width])
+        both = product(jnp.concatenate([high, low], axis=0), last_high)
         size = high.shape[0]
-        return both[:size] + both[size:] + product(high, last_ref[:, width:])
+        return both[:size] + both[size:] + product(high, last_low)
 
     def row_of(values):
         return jnp.concatenate([values[:, r * block : (r + 1) * block] for r in range(rows)], axis=0)
@@ -180,13 +212,13 @@
     x = jnp.concatenate(
         [jnp.concatenate([load(x_ref, r, c) for r in range(rows)], axis=1) for c in range(2)], axis=0
     )
-    re, im = twisted(across(first_ref, x))
+    re, im = twisted(across(0, x))
     z = along(row_of(re), row_of(im))
     z_re, z_im = z[:, :block], z[:, block:]
     turn_re, turn_im = turn_ref[0], turn_ref[1]
     z = along(z_re * turn_re - z_im * turn_im, -(z_re * turn_im + z_im * turn_re))
     re, im = twisted(jnp.concatenate([lane_of(z[:, :block]), lane_of(z[:, block:])], axis=0))
-    x = across(final_ref, jnp.concatenate([re, im], axis=0))
+    x = across(1, jnp.concatenate([re, im], axis=0))
     for r in range(rows):
         lanes = slice(r * block, (r + 1) * block)
         store(o_ref, r, 0, x[:n_dev, lanes])
@@ -212,19 +244,22 @@
             axis=1,
         )
 
+    taps = raman_ref[...]
+    taps = jnp.concatenate(
+        [taps, jnp.concatenate([taps[:, :block], jnp.zeros_like(taps[:, :block])], axis=1)], axis=0
+    )
     values = [window(0), window(1)]
     high, low = split_two(jnp.concatenate(values, axis=1))
-    high = jnp.concatenate([high, high], axis=0)
-    low = jnp.concatenate([low, low], axis=0)
+    fields = jnp.concatenate([high, high, low, low], axis=0)
     response = None
     for start in range(0, n_grid, step):
         up = up_ref[start : start + step, :]
-        grid = product(up, low) + product(up, high)
+        grid = product(up, fields)
         g_re, g_im = grid[:, :span], grid[:, span:]
         intensity = g_re * g_re + g_im * g_im
         i_high, i_low = split_two(intensity)
-        both = product(i_high, raman_ref[...])
-        delayed = both[:, :block] + both[:, block:] + product(i_low, raman_ref[:, :block])
+        both = product(jnp.concatenate([i_high, i_low], axis=1), taps)
+        delayed = both[:, :block] + both[:, block:]
         weight = (1.0 - RAMAN_SHARE) * intensity[:, halo * block :] + delayed
         drive = jnp.concatenate([g_re[:, halo * block :] * weight, g_im[:, halo * block :] * weight], axis=1)
         d_high, d_low = split_two(drive)
@@ -255,41 +290,44 @@
     pieces = [modes]
     for shift in range(1, n_mode):
         pieces.append(lax.ppermute(modes, "mode", [(i, (i + shift) % n_mode) for i in range(n_mode)]))
-    profiles = jnp.concatenate(pieces, axis=1)
-    profiles = profiles.reshape(n_dev, rows, -1).transpose(1, 0, 2).reshape(n_dev * rows, -1)
-    high = lax.reduce_precision(profiles, 8, 7)
-    low = profiles - high
-    down = jnp.concatenate([high, low], axis=0).astype(jnp.bfloat16)
-    up = down.T
-
     dev, pos = np.arange(n_dev), np.arange(block)
     cos_a, sin_a = exp_table(dev[:, None] * dev[None, :], n_dev)
     cos_t, sin_t = exp_table(dev[:, None] * pos[None, :], total)
     cos_b, sin_b = exp_table(pos[:, None] * pos[None, :], block)
     first = block_matrix(cos_a, sin_a).transpose(2, 3, 0, 1)
-    last = block_matrix(cos_b, sin_b).reshape(2 * block, 2 * block)
-    last = jnp.asarray(np.concatenate(np_split(last), axis=1))
+    (cos_high, cos_low), (sin_high, sin_low) = np_split(cos_b), np_split(sin_b)
+    last = jnp.asarray(np.concatenate([cos_high, sin_high, cos_low, sin_low], axis=1))
     twist = jnp.asarray(np.stack([cos_t, sin_t]), f32)
     edge = np.arange(n_dev).reshape(n_tm, per_tm).T.reshape(-1)
 
     def flat(matrix):
         high, low = np_split(matrix.reshape(2 * n_dev, 2 * n_dev))
-        return jnp.asarray(np.concatenate([high, low, high, low], axis=1))
+        return np.concatenate([high, low, high, low], axis=1)
+
+    span = (halo + 1) * block
+    lags = np.zeros((8, span + block))
+    lags[:, block + 1 : block + 1 + RAMAN_TAPS] = RAMAN_SHARE * raman_taps()
 
     frequency = dev[:, None] + n_dev * pos[None, :]
     norm_freq = jnp.asarray(np.where(frequency < total // 2, frequency, frequency - total) * (2.0 / total), f32)
     rates = lax.dynamic_slice_in_dim(betas, t_index * rows, rows, 0)
     table = jax.ShapeDtypeStruct((2, rows * n_dev, block), f32)
-    half_turn, full_turn = pl.pallas_call(
+    half_turn, full_turn, raman = pl.pallas_call(
         functools.partial(turn_kernel, 1.0 / total),
-        out_shape=(table, table),
-        in_specs=[pl.BlockSpec(memory_space=pltpu.SMEM), pl.BlockSpec(memory_space=pltpu.VMEM)],
+        out_shape=(table, table, jax.ShapeDtypeStruct((span, 2 * block), jnp.bfloat16)),
+        in_specs=[pl.BlockSpec(memory_space=pltpu.SMEM)] + [pl.BlockSpec(memory_space=pltpu.VMEM)] * 2,
         name="turns",
         compiler_params=PARAMS,
-    )(rates, norm_freq)
+    )(rates, norm_freq, jnp.asarray(lags, f32))
 
     def load_edge(ref, r, c):
-        return jnp.concatenate([ref[:, r, c, q * block : (q + 1) * block] for q in range(per_tm)], axis=0)
+        return jnp.concatenate(
+            [
+                ref[pl.ds(2 * (per_tm * r + q) + c, n_tm, stride=2 * per_tm * rows), :]
+                for q in range(per_tm)
+            ],
+            axis=0,
+        )
 
     def load_inner(ref, r, c):
         return ref[pl.ds(2 * r + c, n_dev, stride=2 * rows), :]
@@ -317,18 +355,28 @@
             compiler_params=PARAMS,
         )(
             values,
-            flat(first[..., edge] if entering else first),
+            jnp.asarray(np.stack([flat(first[..., edge] if entering else first), flat(first[:, edge] if leaving else first)])),
             last,
             twist,
             turn,
-            flat(first[:, edge] if leaving else first),
         )
 
-    taps = RAMAN_SHARE * raman_matrix(block, halo)
-    raman = jnp.asarray(np.concatenate(np_split(taps), axis=1))
-    step = math.gcd(up.shape[0], 256)
-
-    def nonlinear(windows):
+    def spread_profiles(windows):
+        total_grid = modes.shape[1] * n_mode
+        return pl.pallas_call(
+            functools.partial(profile_kernel, rows),
+            out_shape=(
+                jax.ShapeDtypeStruct((total_grid, 4 * n_dev * rows), jnp.bfloat16),
+                jax.ShapeDtypeStruct((2 * n_dev * rows, total_grid), jnp.bfloat16),
+            ),
+            in_specs=[pl.BlockSpec(memory_space=pltpu.VMEM)] * n_mode + [pl.BlockSpec(memory_space=pl.ANY)],
+            name="profiles",
+            compiler_params=PARAMS,
+        )(*pieces, windows)
+
+    step = math.gcd(modes.shape[1] * n_mode, 512)
+
+    def nonlinear(windows, up, down):
         return pl.pallas_call(
             functools.partial(nonlinear_kernel, rows, halo, step),
             out_shape=jax.ShapeDtypeStruct((n_dev * rows * 2, block), f32),
@@ -340,11 +388,16 @@
         shaped = values.reshape(n_dev, -1, 2, block)
         return lax.all_to_all(shaped, BOTH, 0, 0, tiled=True).reshape(-1, block)
 
-    values = lax.all_to_all(field.reshape(n_tm, rows, 2, samples), "tm", 0, 0, tiled=True)
+    entry = field.reshape(own_modes, 2, per_tm, block)
+    entry = with_layout_constraint(entry, Layout((0, 2, 1, 3)))
+    entry = entry.transpose(0, 2, 1, 3).reshape(n_tm, rows * per_tm, 2, block)
+    values = lax.all_to_all(entry, "tm", 0, 0, tiled=True).reshape(-1, block)
     values = disperse(values, half_turn, True, False)
     for number in range(ITERS):
         values = exchange(values)
-        values = nonlinear(values)
+        if number == 0:
+            up, down = spread_profiles(values)
+        values = nonlinear(values, up, down)
         leaving = number == ITERS - 1
         values = disperse(exchange(values), half_turn if leaving else full_turn, False, leaving)
     return lax.all_to_all(values, "tm", 0, 0, tiled=True).reshape(field.shape)

time: 79.1 us -> 79.1 us (level)
  blocking collectives: 41.3 us -> 42.7 us
  local copies, waits for them, and re-layouts: 2.4 us -> 1.56 us
    all_to_all x1, waiting for transfers between devices: 10.5 us -> 0.96 us  [exchange(): return lax.all_to_all(shaped, BOTH, 0, 0, tiled=True).reshape(-1, block)]
    ppermute x3, waiting for transfers between devices: 0.01 us -> 5.58 us  [tiled(): lax.ppermute(modes, 'mode', [(i, (i + shift) % n_mode) for i in range(n_m...]
    all_to_all x1, waiting for transfers between devices: 0.82 us -> 4.56 us  [tiled(): values = lax.all_to_all(entry, 'tm', 0, 0, tiled=True).reshape(-1, block)]
    all_to_all x3, blocking collectives: 32.6 us -> 34 us  [exchange(): return lax.all_to_all(shaped, BOTH, 0, 0, tiled=True).reshape(-1, block)]
    pallas_call x2, Pallas kernels: 5.25 us -> 4.31 us  [nonlinear(): pl.pallas_call(functools.partial(nonlinear_kernel, rows, halo, step), out...]
    unnamed x22 -> x20, local copies, waits for them, and re-layouts: 1.73 us -> 1.49 us
  transfers between devices with their start and end apart: 5 -> 5, of which waited for: 2 -> 4; matrix products, arithmetic and copies ran while one was open for 1% -> 0% of each run, Pallas kernels for 3% -> 1%
where the time goes in v3:
time: 79.1 us; the launch traced here: 78.6 us
  blocking collectives  42.7 us (54%)
  starting transfers between devices  14.7 us (19%)
  waiting for transfers between devices  11.1 us (14%)
  Pallas kernels  8.42 us (11%)
  local copies, waits for them, and re-layouts  1.56 us (2%)
    all_to_all x3, blocking collectives, exchange(): return lax.all_to_all(shaped, BOTH, 0, 0, tiled=True).reshape(-1, block)  34 us
    all_to_all x1, blocking collectives, tiled(): return lax.all_to_all(values, 'tm', 0, 0, tiled=True).reshape(field.shape)  8.7 us
    all_to_all x1, starting transfers between devices, tiled(): values = lax.all_to_all(entry, 'tm', 0, 0, tiled=True).reshape(-1, block)  6.51 us
    ppermute x3, waiting for transfers between devices, tiled(): lax.ppermute(modes, 'mode', [(i, (i + shift) % n_mode) for i in range(n_m...  5.58 us
    ppermute x3, starting transfers between devices, tiled(): lax.ppermute(modes, 'mode', [(i, (i + shift) % n_mode) for i in range(n_m...  4.76 us
    all_to_all x1, waiting for transfers between devices, tiled(): values = lax.all_to_all(entry, 'tm', 0, 0, tiled=True).reshape(-1, block)  4.56 us
    pallas_call x2, Pallas kernels, nonlinear(): pl.pallas_call(functools.partial(nonlinear_kernel, rows, halo, step), out...  4.31 us
    all_to_all x1, starting transfers between devices, exchange(): return lax.all_to_all(shaped, BOTH, 0, 0, tiled=True).reshape(-1, block)  3.43 us
  transfers between devices with their start and end apart: 5, of which 4 were waited for; matrix products, arithmetic and copies ran while one was open for 0% of the time, Pallas kernels for 1%

profile of v3, /device:TPU:0, one launch (start us, length us, event | category | flops | bytes accessed | tf_op | source)
XLA Modules:
  0.0 78.6 jit_solution(2441216504520956188)
XLA Ops:
  0.0 0.0 copy-start
  0.0 6.5 %all-to-all-start = ((f32[8,12,2,128]{3,2,1,0:T(2,128)}), f32[8,12,2,128]{3,2,1,0:T(2,128)S(1)}, u32[]{:S(2)}, u32[]{:S(2)}) async-start(f32[8,12,2,128]{3,2,1,0:T(2,128)} %bitcast.25), calls=%async_computation | async-start | bytes 196608 | tf_op jit(solution)/shard_map/all_to_all | solution.py:394
  6.5 0.0 copy-done
  6.5 0.1 constant_dynamic-slice_fusion
  6.6 0.1 copy.12.rates_ref
  6.7 0.0 copy-done.7
  6.7 0.7 copy-done.8
  7.4 0.8 %turns.1 = (f32[2,96,128]{2,1,0:T(8,128)S(1)}, f32[2,96,128]{2,1,0:T(8,128)S(1)}, bf16[384,256]{1,0:T(8,128)(2,1)S(1)}) custom-call(f32[3,4]{1,0:T(4,128)S(1)} %copy.12.rates_ref, f32[32,128]{1,0:T(8,128)S(1)} %copy-done.8, f32[8,512]{1,0:T(8,128)S(1)} %copy-done.7), custom_call_target="tpu_custom_call" | custom-call | tf_op jit(solution)/shard_map/turns/pallas_call | solution.py:315
  8.3 4.6 %all-to-all-done = f32[8,12,2,128]{3,2,1,0:T(2,128)S(1)} async-done(((f32[8,12,2,128]{3,2,1,0:T(2,128)}), f32[8,12,2,128]{3,2,1,0:T(2,128)S(1)}, u32[]{:S(2)}, u32[]{:S(2)}) %all-to-all-start) | async-done | bytes 98336 | tf_op jit(solution)/shard_map/all_to_all | solution.py:394
  12.8 1.4 %disperse.3 = f32[576,128]{1,0:T(8,128)} custom-call(f32[192,128]{1,0:T(8,128)S(1)} %bitcast.22, bf16[2,64,256]{2,1,0:T(8,128)(2,1)S(1)} %copy-done.6, bf16[128,512]{1,0:T(8,128)(2,1)S(1)} %copy-done.1, f32[2,32,128]{2,1,0:T(8,128)S(1)} %copy-done.2, f32[2,96,128]{2,1,0:T(8,128)S(1)} %get-tuple-element.10.turn_ref), custom_call_target="tpu_custom_call" | custom-call | tf_op jit(solution)/shard_map/disperse/pallas_call | solution.py:346
  14.3 3.4 %all-to-all-start.1 = ((f32[32,9,2,128]{3,2,1,0:T(2,128)}), f32[32,9,2,128]{3,2,1,0:T(2,128)S(1)}, u32[]{:S(2)}, u32[]{:S(2)}) async-start(f32[32,9,2,128]{3,2,1,0:T(2,128)} %bitcast.4), calls=%async_computation.1 | async-start | bytes 589824 | tf_op jit(solution)/shard_map/all_to_all | solution.py:389
  17.7 0.0 copy-done.3
  17.7 1.8 %collective-permute-start.1 = (f32[96,256]{1,0:T(8,128)S(1)}, f32[96,256]{1,0:T(8,128)S(1)}, u32[]{:S(2)}, u32[]{:S(2)}) collective-permute-start(f32[96,256]{1,0:T(8,128)S(1)} %copy-done.3), channel_id=1, source_target_pairs={{0,16},{8,24},{16,0},{24,8},{1,17},{9,25},{17,1},{25,9},{2,18},{10... | collective-permute-start | bytes 294920 | tf_op jit(solution)/shard_map/ppermute | solution.py:292
  19.5 1.5 %collective-permute-start = (f32[96,256]{1,0:T(8,128)S(1)}, f32[96,256]{1,0:T(8,128)S(1)}, u32[]{:S(2)}, u32[]{:S(2)}) collective-permute-start(f32[96,256]{1,0:T(8,128)S(1)} %copy-done.3), channel_id=1, source_target_pairs={{0,8},{8,16},{16,24},{24,0},{1,9},{9,17},{17,25},{25,1},{2,10},{10... | collective-permute-start | bytes 294920 | tf_op jit(solution)/shard_map/ppermute | solution.py:292
  21.0 1.5 %collective-permute-start.2 = (f32[96,256]{1,0:T(8,128)S(1)}, f32[96,256]{1,0:T(8,128)S(1)}, u32[]{:S(2)}, u32[]{:S(2)}) collective-permute-start(f32[96,256]{1,0:T(8,128)S(1)} %copy-done.3), channel_id=1, source_target_pairs={{0,24},{8,0},{16,8},{24,16},{1,25},{9,1},{17,9},{25,17},{2,26},{10... | collective-permute-start | bytes 294920 | tf_op jit(solution)/shard_map/ppermute | solution.py:292
  22.5 5.0 %collective-permute-done.1.refs_2_ = f32[96,256]{1,0:T(8,128)S(1)} collective-permute-done((f32[96,256]{1,0:T(8,128)S(1)}, f32[96,256]{1,0:T(8,128)S(1)}, u32[]{:S(2)}, u32[]{:S(2)}) %collective-permute-start.1) | collective-permute-done | bytes 98336 | tf_op jit(solution)/shard_map/ppermute | solution.py:292
  27.5 0.0 collective-permute-done.refs_1_
  27.5 0.5 collective-permute-done.2.refs_3_
  28.1 1.0 %all-to-all-done.1 = f32[32,9,2,128]{3,2,1,0:T(2,128)S(1)} async-done(((f32[32,9,2,128]{3,2,1,0:T(2,128)}), f32[32,9,2,128]{3,2,1,0:T(2,128)S(1)}, u32[]{:S(2)}, u32[]{:S(2)}) %all-to-all-start.1) | async-done | bytes 294944 | tf_op jit(solution)/shard_map/all_to_all | solution.py:389
  29.0 0.4 profiles.1
  29.5 2.2 %nonlinear.2 = f32[192,128]{1,0:T(8,128)S(1)} custom-call(f32[576,128]{1,0:T(8,128)S(1)} %bitcast.16, bf16[1024,384]{1,0:T(8,128)(2,1)S(1)} %get-tuple-element.11.up_ref, bf16[192,1024]{1,0:T(8,128)(2,1)S(1)} %get-tuple-element.12.down_ref, bf16[384,256]{1,0:T(8,128)(2,1)S(1)} %get-tuple-element.13.raman_ref), custom_call_target="tpu_custom_call" | custom-call | tf_op jit(solution)/shard_map/nonlinear/pallas_call | solution.py:380
  31.6 0.0 copy-start.5
  31.6 11.3 %all_to_all.30 = f32[32,3,2,128]{3,2,1,0:T(2,128)S(1)} all-to-all(f32[32,3,2,128]{3,2,1,0:T(2,128)S(1)} %bitcast.21), channel_id=1, replica_groups=mesh['mode'=4,'tm'=8] {'mode','tm'}, dimensions={0} | all-to-all | bytes 196608 | tf_op jit(solution)/shard_map/all_to_all | solution.py:389
  42.9 0.7 disperse.4
  43.6 13.0 %all_to_all.31 = f32[32,9,2,128]{3,2,1,0:T(2,128)S(1)} all-to-all(f32[32,9,2,128]{3,2,1,0:T(2,128)S(1)} %bitcast.18), channel_id=1, replica_groups=mesh['mode'=4,'tm'=8] {'mode','tm'}, dimensions={0} | all-to-all | bytes 589824 | tf_op jit(solution)/shard_map/all_to_all | solution.py:389
  56.7 2.2 %nonlinear.3 = f32[192,128]{1,0:T(8,128)S(1)} custom-call(f32[576,128]{1,0:T(8,128)S(1)} %bitcast.17, bf16[1024,384]{1,0:T(8,128)(2,1)S(1)} %get-tuple-element.11.up_ref, bf16[192,1024]{1,0:T(8,128)(2,1)S(1)} %get-tuple-element.12.down_ref, bf16[384,256]{1,0:T(8,128)(2,1)S(1)} %get-tuple-element.13.raman_ref), custom_call_target="tpu_custom_call" | custom-call | tf_op jit(solution)/shard_map/nonlinear/pallas_call | solution.py:380
  58.8 0.0 copy-start.4
  58.8 9.7 %all_to_all.32 = f32[32,3,2,128]{3,2,1,0:T(2,128)S(1)} all-to-all(f32[32,3,2,128]{3,2,1,0:T(2,128)S(1)} %bitcast.20), channel_id=1, replica_groups=mesh['mode'=4,'tm'=8] {'mode','tm'}, dimensions={0} | all-to-all | bytes 196608 | tf_op jit(solution)/shard_map/all_to_all | solution.py:389
  68.6 0.0 copy-done.4
  68.6 0.7 disperse.5
  69.3 8.7 %all_to_all.33 = f32[8,3,2,512]{3,2,1,0:T(2,128)S(1)} all-to-all(f32[8,3,2,512]{3,2,1,0:T(2,128)S(1)} %disperse.5), channel_id=1, replica_groups=mesh['mode'=4,'tm'=8] {'tm'}, dimensions={0} | all-to-all | bytes 196608 | tf_op jit(solution)/shard_map/all_to_all | solution.py:403
  78.0 0.6 copy.14
  (10 shorter events, 0.0 us)
Async XLA Ops:
  0.0 6.5 %copy-start = (f32[24,4]{0,1:T(4,128)S(1)}, f32[24,4]{0,1:T(4,128)}, u32[]{:S(2)}) copy-start(f32[24,4]{0,1:T(4,128)} %param.12) | copy-start | bytes 1156
  0.0 12.8 %copy-start.1 = (bf16[128,512]{1,0:T(8,128)(2,1)S(1)}, bf16[128,512]{1,0:T(8,128)(2,1)}, u32[]{:S(2)}) copy-start(bf16[128,512]{1,0:T(8,128)(2,1)} %constant.24.clone.last_ref) | copy-start | bytes 393220
  0.0 6.7 %copy-start.7 = (f32[8,512]{1,0:T(8,128)S(1)}, f32[8,512]{1,0:T(8,128)}, u32[]{:S(2)}) copy-start(f32[8,512]{1,0:T(8,128)} %constant.27.clone.taps_ref) | copy-start | bytes 49156
  0.0 12.8 %copy-start.6 = (bf16[2,64,256]{2,1,0:T(8,128)(2,1)S(1)}, bf16[2,64,256]{2,1,0:T(8,128)(2,1)}, u32[]{:S(2)}) copy-start(bf16[2,64,256]{2,1,0:T(8,128)(2,1)} %constant.28.clone.first_ref) | copy-start | bytes 196612
  0.0 12.8 %all-to-all-start = ((f32[8,12,2,128]{3,2,1,0:T(2,128)}), f32[8,12,2,128]{3,2,1,0:T(2,128)S(1)}, u32[]{:S(2)}, u32[]{:S(2)}) async-start(f32[8,12,2,128]{3,2,1,0:T(2,128)} %bitcast.25), calls=%async_computation | async-start | bytes 196608 | tf_op jit(solution)/shard_map/all_to_all | solution.py:394
  6.5 6.3 %copy-start.2 = (f32[2,32,128]{2,1,0:T(8,128)S(1)}, f32[2,32,128]{2,1,0:T(8,128)}, u32[]{:S(2)}) copy-start(f32[2,32,128]{2,1,0:T(8,128)} %constant.25.clone.twist_ref) | copy-start | bytes 98308
  6.7 0.7 copy-start.8
  14.3 3.4 %copy-start.3 = (f32[96,256]{1,0:T(8,128)S(1)}, f32[96,256]{1,0:T(8,128)}, u32[]{:S(2)}) copy-start(f32[96,256]{1,0:T(8,128)} %refs_0_.1) | copy-start | bytes 294916
  14.3 14.8 %all-to-all-start.1 = ((f32[32,9,2,128]{3,2,1,0:T(2,128)}), f32[32,9,2,128]{3,2,1,0:T(2,128)S(1)}, u32[]{:S(2)}, u32[]{:S(2)}) async-start(f32[32,9,2,128]{3,2,1,0:T(2,128)} %bitcast.4), calls=%async_computation.1 | async-start | bytes 589824 | tf_op jit(solution)/shard_map/all_to_all | solution.py:389
  17.7 9.8 %collective-permute-start.1 = (f32[96,256]{1,0:T(8,128)S(1)}, f32[96,256]{1,0:T(8,128)S(1)}, u32[]{:S(2)}, u32[]{:S(2)}) collective-permute-start(f32[96,256]{1,0:T(8,128)S(1)} %copy-done.3), channel_id=1, source_target_pairs={{0,16},{8,24},{16,0},{24,8},{1,17},{9,25},{17,1},{25,9},{2,18},{10... | collective-permute-start | bytes 294920 | tf_op jit(solution)/shard_map/ppermute | solution.py:292
  19.5 8.0 %collective-permute-start = (f32[96,256]{1,0:T(8,128)S(1)}, f32[96,256]{1,0:T(8,128)S(1)}, u32[]{:S(2)}, u32[]{:S(2)}) collective-permute-start(f32[96,256]{1,0:T(8,128)S(1)} %copy-done.3), channel_id=1, source_target_pairs={{0,8},{8,16},{16,24},{24,0},{1,9},{9,17},{17,25},{25,1},{2,10},{10... | collective-permute-start | bytes 294920 | tf_op jit(solution)/shard_map/ppermute | solution.py:292
  21.0 7.0 %collective-permute-start.2 = (f32[96,256]{1,0:T(8,128)S(1)}, f32[96,256]{1,0:T(8,128)S(1)}, u32[]{:S(2)}, u32[]{:S(2)}) collective-permute-start(f32[96,256]{1,0:T(8,128)S(1)} %copy-done.3), channel_id=1, source_target_pairs={{0,24},{8,0},{16,8},{24,16},{1,25},{9,1},{17,9},{25,17},{2,26},{10... | collective-permute-start | bytes 294920 | tf_op jit(solution)/shard_map/ppermute | solution.py:292
  31.6 11.3 %copy-start.5 = (bf16[2,64,256]{2,1,0:T(8,128)(2,1)S(1)}, bf16[2,64,256]{2,1,0:T(8,128)(2,1)}, u32[]{:S(2)}) copy-start(bf16[2,64,256]{2,1,0:T(8,128)(2,1)} %constant.29.clone.first_ref) | copy-start | bytes 196612
  58.8 9.7 %copy-start.4 = (bf16[2,64,256]{2,1,0:T(8,128)(2,1)S(1)}, bf16[2,64,256]{2,1,0:T(8,128)(2,1)}, u32[]{:S(2)}) copy-start(bf16[2,64,256]{2,1,0:T(8,128)(2,1)} %constant.30.clone.first_ref) | copy-start | bytes 196612

commit v4 on v3

--- a/solution.py
+++ b/solution.py
@@ -138,32 +138,58 @@
     return jnp.dot(left, right, preferred_element_type=jnp.float32)
 
 
-def turn_kernel(scale, rates_ref, freq_ref, taps_ref, half_ref, full_ref, raman_ref):
+def cos_sin(angle):
+    quarter = jnp.floor(angle * (2.0 / math.pi) + 0.5)
+    rest = angle - quarter * 1.5703125
+    rest = rest - quarter * 4.837512969970703e-4
+    rest = rest - quarter * 7.549789948768648e-8
+    square = rest * rest
+    sine = rest + rest * square * (-1.6666654611e-1 + square * (8.3321608736e-3 - square * 1.9515295891e-4))
+    cosine = 1.0 - 0.5 * square
+    cosine = cosine + square * square * (
+        4.166664568298827e-2 + square * (-1.388731625493765e-3 + square * 2.443315711809948e-5)
+    )
+    turn = quarter.astype(jnp.int32)
+    odd = (turn & 1) == 1
+    out_cos = jnp.where(odd, sine, cosine)
+    out_sin = jnp.where(odd, cosine, sine)
+    return (
+        jnp.where(((turn + 1) & 2) == 2, -out_cos, out_cos),
+        jnp.where((turn & 2) == 2, -out_sin, out_sin),
+    )
+
+
+def work_out_turns(total, rates_ref, half_ref, full_ref):
+    rows = rates_ref.shape[0]
+    _, count, block = half_ref.shape
+    size = count // rows
+    first, last = (lax.broadcasted_iota(jnp.int32, (size, block), d) for d in range(2))
+    freq = first + size * last
+    freq = jnp.where(freq < total // 2, freq, freq - total).astype(jnp.float32) * (2.0 / total)
+    square = freq * freq
+    scale = 1.0 / total
+    for r in range(rows):
+        phase = (
+            rates_ref[r : r + 1, 0 : 1]
+            + rates_ref[r : r + 1, 1 : 2] * freq
+            + rates_ref[r : r + 1, 2 : 3] * square / 2.0
+            + rates_ref[r : r + 1, 3 : 4] * (square * freq) / 6.0
+        )
+        cosine, sine = cos_sin(phase * 0.5)
+        part = pl.ds(r * size, size)
+        half_ref[0, part] = cosine * scale
+        half_ref[1, part] = sine * scale
+        full_ref[0, part] = (cosine * cosine - sine * sine) * scale
+        full_ref[1, part] = (2.0 * scale) * cosine * sine
+
+
+def profile_kernel(rows, *refs):
+    pieces, taps_ref, (up_ref, down_ref, raman_ref) = refs[:-5], refs[-5], refs[-3:]
     window, double = raman_ref.shape
     block = double // 2
     taps = jnp.broadcast_to(taps_ref[0:1, :], (window, taps_ref.shape[1]))
     taps = pltpu.roll(taps, block, axis=1, stride=1, stride_axis=0)[:, :block]
     raman_ref[...] = jnp.concatenate(split_two(taps), axis=1)
-    freq = freq_ref[...]
-    square = freq * freq
-    size = freq.shape[0]
-    for r in range(rates_ref.shape[0]):
-        phase = (
-            rates_ref[r, 0]
-            + rates_ref[r, 1] * freq
-            + rates_ref[r, 2] * square / 2.0
-            + rates_ref[r, 3] * (square * freq) / 6.0
-        )
-        cosine, sine = jnp.cos(phase * 0.5), jnp.sin(phase * 0.5)
-        part = pl.ds(r * size, size)
-        half_ref[0, part] = cosine * scale
-        half_ref[1, part] = sine * scale
-        full_ref[0, part] = (cosine * cosine - sine * sine) * scale
-        full_ref[1, part] = (2.0 * scale) * cosine * sine
-
-
-def profile_kernel(rows, *refs):
-    pieces, (up_ref, down_ref) = refs[:-3], refs[-2:]
     count = pieces[0].shape[0]
     n_dev = count // rows
     place, mode = (lax.broadcasted_iota(jnp.int32, (count, count), d) for d in range(2))
@@ -178,7 +204,12 @@
         start += width
 
 
-def disperse_kernel(rows, load, store, x_ref, first_ref, last_ref, twist_ref, turn_ref, o_ref):
+def disperse_kernel(rows, total, load, store, x_ref, first_ref, last_ref, twist_ref, *refs):
+    if total is not None:
+        rates_ref, o_ref, turn_ref, full_ref = refs
+        work_out_turns(total, rates_ref, turn_ref, full_ref)
+    else:
+        turn_ref, o_ref = refs
     n_dev, block = twist_ref.shape[1:]
     cos_high, sin_high, cos_low, sin_low = (last_ref[:, n * block : (n + 1) * block] for n in range(4))
     last_high = jnp.concatenate(
@@ -225,50 +256,46 @@
         store(o_ref, r, 1, -x[n_dev:, lanes])
 
 
-def nonlinear_kernel(rows, halo, step, w_ref, up_ref, down_ref, raman_ref, o_ref):
+def nonlinear_kernel(rows, halo, w_ref, up_ref, down_ref, raman_ref, o_ref):
     block = w_ref.shape[1]
-    span = (halo + 1) * block
     n_dev = w_ref.shape[0] // ((halo + 1) * rows * 2)
     n_modes = n_dev * rows
-    n_grid = up_ref.shape[0]
     chunk = (halo + 1) * rows * 2
 
-    def window(c):
+    def part(h, c):
         return jnp.concatenate(
-            [
-                jnp.concatenate(
-                    [w_ref[pl.ds(h * 2 * rows + 2 * r + c, n_dev, stride=chunk), :] for r in range(rows)], axis=0
-                )
-                for h in range(halo + 1)
-            ],
-            axis=1,
+            [w_ref[pl.ds(h * 2 * rows + 2 * r + c, n_dev, stride=chunk), :] for r in range(rows)], axis=0
         )
 
+    own, highs, lows = None, [], []
+    for h in range(halo + 1):
+        values = jnp.concatenate([part(h, 0), part(h, 1)], axis=1)
+        high, low = split_two(values)
+        if halo > 1 and h == 0:
+            grid = product(up_ref[:, : 2 * n_modes], jnp.concatenate([high, high], axis=0))
+        else:
+            grid = product(up_ref[...], jnp.concatenate([high, high, low, low], axis=0))
+        g_re, g_im = grid[:, :block], grid[:, block:]
+        intensity = g_re * g_re + g_im * g_im
+        high, low = split_two(intensity)
+        highs.append(high)
+        lows.append(low)
+        if h == halo:
+            own = (values, g_re, g_im, intensity)
+    values, g_re, g_im, intensity = own
     taps = raman_ref[...]
     taps = jnp.concatenate(
         [taps, jnp.concatenate([taps[:, :block], jnp.zeros_like(taps[:, :block])], axis=1)], axis=0
     )
-    values = [window(0), window(1)]
-    high, low = split_two(jnp.concatenate(values, axis=1))
-    fields = jnp.concatenate([high, high, low, low], axis=0)
-    response = None
-    for start in range(0, n_grid, step):
-        up = up_ref[start : start + step, :]
-        grid = product(up, fields)
-        g_re, g_im = grid[:, :span], grid[:, span:]
-        intensity = g_re * g_re + g_im * g_im
-        i_high, i_low = split_two(intensity)
-        both = product(jnp.concatenate([i_high, i_low], axis=1), taps)
-        delayed = both[:, :block] + both[:, block:]
-        weight = (1.0 - RAMAN_SHARE) * intensity[:, halo * block :] + delayed
-        drive = jnp.concatenate([g_re[:, halo * block :] * weight, g_im[:, halo * block :] * weight], axis=1)
-        d_high, d_low = split_two(drive)
-        both = product(down_ref[:, start : start + step], d_high)
-        part = both[:n_modes] + both[n_modes:] + product(down_ref[:n_modes, start : start + step], d_low)
-        response = part if response is None else response + part
+    both = product(jnp.concatenate(highs + lows, axis=1), taps)
+    weight = (1.0 - RAMAN_SHARE) * intensity + (both[:, :block] + both[:, block:])
+    drive = jnp.concatenate([g_re * weight, g_im * weight], axis=1)
+    d_high, d_low = split_two(drive)
+    both = product(down_ref[...], d_high)
+    response = both[:n_modes] + both[n_modes:] + product(down_ref[:n_modes, :], d_low)
     out = [
-        values[0][:, halo * block :] - KERR_GAIN * response[:, block:],
-        values[1][:, halo * block :] + KERR_GAIN * response[:, :block],
+        values[:, :block] - KERR_GAIN * response[:, block:],
+        values[:, block:] + KERR_GAIN * response[:, :block],
     ]
     for c in range(2):
         for r in range(rows):
@@ -308,17 +335,7 @@
     lags = np.zeros((8, span + block))
     lags[:, block + 1 : block + 1 + RAMAN_TAPS] = RAMAN_SHARE * raman_taps()
 
-    frequency = dev[:, None] + n_dev * pos[None, :]
-    norm_freq = jnp.asarray(np.where(frequency < total // 2, frequency, frequency - total) * (2.0 / total), f32)
     rates = lax.dynamic_slice_in_dim(betas, t_index * rows, rows, 0)
-    table = jax.ShapeDtypeStruct((2, rows * n_dev, block), f32)
-    half_turn, full_turn, raman = pl.pallas_call(
-        functools.partial(turn_kernel, 1.0 / total),
-        out_shape=(table, table, jax.ShapeDtypeStruct((span, 2 * block), jnp.bfloat16)),
-        in_specs=[pl.BlockSpec(memory_space=pltpu.SMEM)] + [pl.BlockSpec(memory_space=pltpu.VMEM)] * 2,
-        name="turns",
-        compiler_params=PARAMS,
-    )(rates, norm_freq, jnp.asarray(lags, f32))
 
     def load_edge(ref, r, c):
         return jnp.concatenate(
@@ -343,23 +360,21 @@
 
     def disperse(values, turn, entering, leaving):
         shape = (n_tm, rows, 2, samples) if leaving else (n_dev * (halo + 1) * rows * 2, block)
+        shape = jax.ShapeDtypeStruct(shape, f32)
+        table = jax.ShapeDtypeStruct((2, rows * n_dev, block), f32)
+        matrices = np.stack([flat(first[..., edge] if entering else first), flat(first[:, edge] if leaving else first)])
         return pl.pallas_call(
             functools.partial(
                 disperse_kernel,
                 rows,
+                total if entering else None,
                 load_edge if entering else load_inner,
                 store_edge if leaving else store_inner,
             ),
-            out_shape=jax.ShapeDtypeStruct(shape, f32),
-            name="disperse",
+            out_shape=(shape, table, table) if entering else shape,
+                        name="disperse",
             compiler_params=PARAMS,
-        )(
-            values,
-            jnp.asarray(np.stack([flat(first[..., edge] if entering else first), flat(first[:, edge] if leaving else first)])),
-            last,
-            twist,
-            turn,
-        )
+        )(values, jnp.asarray(matrices), last, twist, turn)
 
     def spread_profiles(windows):
         total_grid = modes.shape[1] * n_mode
@@ -368,17 +383,16 @@
             out_shape=(
                 jax.ShapeDtypeStruct((total_grid, 4 * n_dev * rows), jnp.bfloat16),
                 jax.ShapeDtypeStruct((2 * n_dev * rows, total_grid), jnp.bfloat16),
+                jax.ShapeDtypeStruct((span, 2 * block), jnp.bfloat16),
             ),
-            in_specs=[pl.BlockSpec(memory_space=pltpu.VMEM)] * n_mode + [pl.BlockSpec(memory_space=pl.ANY)],
+            in_specs=[pl.BlockSpec(memory_space=pltpu.VMEM)] * (n_mode + 1) + [pl.BlockSpec(memory_space=pl.ANY)],
             name="profiles",
             compiler_params=PARAMS,
-        )(*pieces, windows)
-
-    step = math.gcd(modes.shape[1] * n_mode, 512)
-
-    def nonlinear(windows, up, down):
+        )(*pieces, jnp.asarray(lags, f32), windows)
+
+    def nonlinear(windows, up, down, raman):
         return pl.pallas_call(
-            functools.partial(nonlinear_kernel, rows, halo, step),
+            functools.partial(nonlinear_kernel, rows, halo),
             out_shape=jax.ShapeDtypeStruct((n_dev * rows * 2, block), f32),
             name="nonlinear",
             compiler_params=PARAMS,
@@ -392,12 +406,12 @@
     entry = with_layout_constraint(entry, Layout((0, 2, 1, 3)))
     entry = entry.transpose(0, 2, 1, 3).reshape(n_tm, rows * per_tm, 2, block)
     values = lax.all_to_all(entry, "tm", 0, 0, tiled=True).reshape(-1, block)
-    values = disperse(values, half_turn, True, False)
+    values, half_turn, full_turn = disperse(values, rates, True, False)
     for number in range(ITERS):
         values = exchange(values)
         if number == 0:
-            up, down = spread_profiles(values)
-        values = nonlinear(values, up, down)
+            profiles = spread_profiles(values)
+        values = nonlinear(values, *profiles)
         leaving = number == ITERS - 1
         values = disperse(exchange(values), half_turn if leaving else full_turn, False, leaving)
     return lax.all_to_all(values, "tm", 0, 0, tiled=True).reshape(field.shape)

time: 79.1 us -> 78.4 us (level)
  waiting for transfers between devices: 11.1 us -> 12.7 us
  Pallas kernels: 8.42 us -> 6.9 us
    all_to_all x1, waiting for transfers between devices: 4.56 us -> 6.13 us  [tiled(): values = lax.all_to_all(entry, 'tm', 0, 0, tiled=True).reshape(-1, block)]
    pallas_call x6 -> x5, Pallas kernels: 7.99 us -> 6.46 us  [the longest x2 3.59 us: nonlinear(): pl.pallas_call(functools.partial(nonlinear_kernel, rows, halo), out_shape...]
  transfers between devices with their start and end apart: 5 -> 5, of which waited for: 4 -> 4; matrix products, arithmetic and copies ran while one was open for 0% -> 0% of each run, Pallas kernels for 1% -> 0%
where the time goes in v4:
time: 78.4 us; the launch traced here: 77.9 us
  blocking collectives  42.7 us (54%)
  starting transfers between devices  14.7 us (19%)
  waiting for transfers between devices  12.7 us (16%)
  Pallas kernels  6.9 us (9%)
  local copies, waits for them, and re-layouts  0.85 us (1%)
    all_to_all x3, blocking collectives, exchange(): return lax.all_to_all(shaped, BOTH, 0, 0, tiled=True).reshape(-1, block)  34 us
    all_to_all x1, blocking collectives, tiled(): return lax.all_to_all(values, 'tm', 0, 0, tiled=True).reshape(field.shape)  8.7 us
    all_to_all x1, starting transfers between devices, tiled(): values = lax.all_to_all(entry, 'tm', 0, 0, tiled=True).reshape(-1, block)  6.51 us
    all_to_all x1, waiting for transfers between devices, tiled(): values = lax.all_to_all(entry, 'tm', 0, 0, tiled=True).reshape(-1, block)  6.13 us
    ppermute x3, waiting for transfers between devices, tiled(): lax.ppermute(modes, 'mode', [(i, (i + shift) % n_mode) for i in range(n_m...  5.58 us
    ppermute x3, starting transfers between devices, tiled(): lax.ppermute(modes, 'mode', [(i, (i + shift) % n_mode) for i in range(n_m...  4.76 us
    pallas_call x2, Pallas kernels, nonlinear(): pl.pallas_call(functools.partial(nonlinear_kernel, rows, halo), out_shape...  3.59 us
    all_to_all x1, starting transfers between devices, exchange(): return lax.all_to_all(shaped, BOTH, 0, 0, tiled=True).reshape(-1, block)  3.43 us
  transfers between devices with their start and end apart: 5, of which 4 were waited for; matrix products, arithmetic and copies ran while one was open for 0% of the time, Pallas kernels for 0%

profile of v4, /device:TPU:0, one launch (start us, length us, event | category | flops | bytes accessed | tf_op | source)
XLA Modules:
  0.0 77.9 jit_solution(6329932212635386248)
XLA Ops:
  0.0 0.0 copy-start
  0.0 6.5 %all-to-all-start = ((f32[8,12,2,128]{3,2,1,0:T(2,128)}), f32[8,12,2,128]{3,2,1,0:T(2,128)S(1)}, u32[]{:S(2)}, u32[]{:S(2)}) async-start(f32[8,12,2,128]{3,2,1,0:T(2,128)} %bitcast.25), calls=%async_computation | async-start | bytes 196608 | tf_op jit(solution)/shard_map/all_to_all | solution.py:408
  6.5 0.0 copy-done
  6.5 0.1 constant_dynamic-slice_fusion
  6.6 0.1 copy.11.refs_0_
  6.7 6.1 %all-to-all-done = f32[8,12,2,128]{3,2,1,0:T(2,128)S(1)} async-done(((f32[8,12,2,128]{3,2,1,0:T(2,128)}), f32[8,12,2,128]{3,2,1,0:T(2,128)S(1)}, u32[]{:S(2)}, u32[]{:S(2)}) %all-to-all-start) | async-done | bytes 98336 | tf_op jit(solution)/shard_map/all_to_all | solution.py:408
  12.8 0.0 copy-done.1
  12.8 0.0 copy-done.2
  12.8 0.0 copy-done.4
  12.8 1.4 %disperse.3 = (f32[576,128]{1,0:T(8,128)}, f32[2,96,128]{2,1,0:T(8,128)S(1)}, f32[2,96,128]{2,1,0:T(8,128)S(1)}) custom-call(f32[192,128]{1,0:T(8,128)S(1)} %bitcast.22, bf16[2,64,256]{2,1,0:T(8,128)(2,1)S(1)} %copy-done.4, bf16[128,512]{1,0:T(8,128)(2,1)S(1)} %copy-done.1, f32[2,32,128]{2,1,0:T(8,128)S(1)} %copy-done.2, f32[3,4]{1,0:T(4,128)S(1)} %copy.11.refs_0_), custom_call_target="tpu_custom_call" | custom-call | tf_op jit(solution)/shard_map/disperse/pallas_call | solution.py:366
  14.3 3.4 %all-to-all-start.1 = ((f32[32,9,2,128]{3,2,1,0:T(2,128)}), f32[32,9,2,128]{3,2,1,0:T(2,128)S(1)}, u32[]{:S(2)}, u32[]{:S(2)}) async-start(f32[32,9,2,128]{3,2,1,0:T(2,128)} %bitcast.4), calls=%async_computation.1 | async-start | bytes 589824 | tf_op jit(solution)/shard_map/all_to_all | solution.py:403
  17.7 0.0 copy-done.3
  17.7 1.8 %collective-permute-start.1 = (f32[96,256]{1,0:T(8,128)S(1)}, f32[96,256]{1,0:T(8,128)S(1)}, u32[]{:S(2)}, u32[]{:S(2)}) collective-permute-start(f32[96,256]{1,0:T(8,128)S(1)} %copy-done.3), channel_id=1, source_target_pairs={{0,16},{8,24},{16,0},{24,8},{1,17},{9,25},{17,1},{25,9},{2,18},{10... | collective-permute-start | bytes 294920 | tf_op jit(solution)/shard_map/ppermute | solution.py:319
  19.6 1.5 %collective-permute-start = (f32[96,256]{1,0:T(8,128)S(1)}, f32[96,256]{1,0:T(8,128)S(1)}, u32[]{:S(2)}, u32[]{:S(2)}) collective-permute-start(f32[96,256]{1,0:T(8,128)S(1)} %copy-done.3), channel_id=1, source_target_pairs={{0,8},{8,16},{16,24},{24,0},{1,9},{9,17},{17,25},{25,1},{2,10},{10... | collective-permute-start | bytes 294920 | tf_op jit(solution)/shard_map/ppermute | solution.py:319
  21.0 1.5 %collective-permute-start.2 = (f32[96,256]{1,0:T(8,128)S(1)}, f32[96,256]{1,0:T(8,128)S(1)}, u32[]{:S(2)}, u32[]{:S(2)}) collective-permute-start(f32[96,256]{1,0:T(8,128)S(1)} %copy-done.3), channel_id=1, source_target_pairs={{0,24},{8,0},{16,8},{24,16},{1,25},{9,1},{17,9},{25,17},{2,26},{10... | collective-permute-start | bytes 294920 | tf_op jit(solution)/shard_map/ppermute | solution.py:319
  22.5 5.0 %collective-permute-done.1.refs_2_ = f32[96,256]{1,0:T(8,128)S(1)} collective-permute-done((f32[96,256]{1,0:T(8,128)S(1)}, f32[96,256]{1,0:T(8,128)S(1)}, u32[]{:S(2)}, u32[]{:S(2)}) %collective-permute-start.1) | collective-permute-done | bytes 98336 | tf_op jit(solution)/shard_map/ppermute | solution.py:319
  27.5 0.0 collective-permute-done.refs_1_
  27.5 0.5 collective-permute-done.2.refs_3_
  28.1 1.0 %all-to-all-done.1 = f32[32,9,2,128]{3,2,1,0:T(2,128)S(1)} async-done(((f32[32,9,2,128]{3,2,1,0:T(2,128)}), f32[32,9,2,128]{3,2,1,0:T(2,128)S(1)}, u32[]{:S(2)}, u32[]{:S(2)}) %all-to-all-start.1) | async-done | bytes 294944 | tf_op jit(solution)/shard_map/all_to_all | solution.py:403
  29.0 0.0 copy-done.7
  29.0 0.4 profiles.1
  29.5 1.8 %nonlinear.2 = f32[192,128]{1,0:T(8,128)S(1)} custom-call(f32[576,128]{1,0:T(8,128)S(1)} %bitcast.16, bf16[1024,384]{1,0:T(8,128)(2,1)S(1)} %get-tuple-element.12.up_ref, bf16[192,1024]{1,0:T(8,128)(2,1)S(1)} %get-tuple-element.13.down_ref, bf16[384,256]{1,0:T(8,128)(2,1)S(1)} %get-tuple-element.14.raman_ref), custom_call_target="tpu_custom_call" | custom-call | tf_op jit(solution)/shard_map/nonlinear/pallas_call | solution.py:394
  31.3 0.0 copy-start.6
  31.3 11.3 %all_to_all.30 = f32[32,3,2,128]{3,2,1,0:T(2,128)S(1)} all-to-all(f32[32,3,2,128]{3,2,1,0:T(2,128)S(1)} %bitcast.21), channel_id=1, replica_groups=mesh['mode'=4,'tm'=8] {'mode','tm'}, dimensions={0} | all-to-all | bytes 196608 | tf_op jit(solution)/shard_map/all_to_all | solution.py:403
  42.6 0.7 disperse.4
  43.3 13.0 %all_to_all.31 = f32[32,9,2,128]{3,2,1,0:T(2,128)S(1)} all-to-all(f32[32,9,2,128]{3,2,1,0:T(2,128)S(1)} %bitcast.18), channel_id=1, replica_groups=mesh['mode'=4,'tm'=8] {'mode','tm'}, dimensions={0} | all-to-all | bytes 589824 | tf_op jit(solution)/shard_map/all_to_all | solution.py:403
  56.3 1.8 %nonlinear.3 = f32[192,128]{1,0:T(8,128)S(1)} custom-call(f32[576,128]{1,0:T(8,128)S(1)} %bitcast.17, bf16[1024,384]{1,0:T(8,128)(2,1)S(1)} %get-tuple-element.12.up_ref, bf16[192,1024]{1,0:T(8,128)(2,1)S(1)} %get-tuple-element.13.down_ref, bf16[384,256]{1,0:T(8,128)(2,1)S(1)} %get-tuple-element.14.raman_ref), custom_call_target="tpu_custom_call" | custom-call | tf_op jit(solution)/shard_map/nonlinear/pallas_call | solution.py:394
  58.1 0.0 copy-start.5
  58.1 9.7 %all_to_all.32 = f32[32,3,2,128]{3,2,1,0:T(2,128)S(1)} all-to-all(f32[32,3,2,128]{3,2,1,0:T(2,128)S(1)} %bitcast.20), channel_id=1, replica_groups=mesh['mode'=4,'tm'=8] {'mode','tm'}, dimensions={0} | all-to-all | bytes 196608 | tf_op jit(solution)/shard_map/all_to_all | solution.py:403
  67.9 0.7 disperse.5
  68.6 8.7 %all_to_all.33 = f32[8,3,2,512]{3,2,1,0:T(2,128)S(1)} all-to-all(f32[8,3,2,512]{3,2,1,0:T(2,128)S(1)} %disperse.5), channel_id=1, replica_groups=mesh['mode'=4,'tm'=8] {'tm'}, dimensions={0} | all-to-all | bytes 196608 | tf_op jit(solution)/shard_map/all_to_all | solution.py:417
  77.3 0.6 copy.13
  (7 shorter events, 0.0 us)
Async XLA Ops:
  0.0 6.5 %copy-start = (f32[24,4]{0,1:T(4,128)S(1)}, f32[24,4]{0,1:T(4,128)}, u32[]{:S(2)}) copy-start(f32[24,4]{0,1:T(4,128)} %param.11) | copy-start | bytes 1156
  0.0 12.8 %copy-start.1 = (bf16[128,512]{1,0:T(8,128)(2,1)S(1)}, bf16[128,512]{1,0:T(8,128)(2,1)}, u32[]{:S(2)}) copy-start(bf16[128,512]{1,0:T(8,128)(2,1)} %constant.22.clone.last_ref) | copy-start | bytes 393220
  0.0 12.8 %copy-start.2 = (f32[2,32,128]{2,1,0:T(8,128)S(1)}, f32[2,32,128]{2,1,0:T(8,128)}, u32[]{:S(2)}) copy-start(f32[2,32,128]{2,1,0:T(8,128)} %constant.23.clone.twist_ref) | copy-start | bytes 98308
  0.0 12.8 %copy-start.4 = (bf16[2,64,256]{2,1,0:T(8,128)(2,1)S(1)}, bf16[2,64,256]{2,1,0:T(8,128)(2,1)}, u32[]{:S(2)}) copy-start(bf16[2,64,256]{2,1,0:T(8,128)(2,1)} %constant.24.clone.first_ref) | copy-start | bytes 196612
  0.0 12.8 %all-to-all-start = ((f32[8,12,2,128]{3,2,1,0:T(2,128)}), f32[8,12,2,128]{3,2,1,0:T(2,128)S(1)}, u32[]{:S(2)}, u32[]{:S(2)}) async-start(f32[8,12,2,128]{3,2,1,0:T(2,128)} %bitcast.25), calls=%async_computation | async-start | bytes 196608 | tf_op jit(solution)/shard_map/all_to_all | solution.py:408
  14.3 3.4 %copy-start.3 = (f32[96,256]{1,0:T(8,128)S(1)}, f32[96,256]{1,0:T(8,128)}, u32[]{:S(2)}) copy-start(f32[96,256]{1,0:T(8,128)} %refs_0_.1) | copy-start | bytes 294916
  14.3 14.8 %copy-start.7 = (f32[8,512]{1,0:T(8,128)S(1)}, f32[8,512]{1,0:T(8,128)}, u32[]{:S(2)}) copy-start(f32[8,512]{1,0:T(8,128)} %constant.25.clone.refs_4_) | copy-start | bytes 49156
  14.3 14.8 %all-to-all-start.1 = ((f32[32,9,2,128]{3,2,1,0:T(2,128)}), f32[32,9,2,128]{3,2,1,0:T(2,128)S(1)}, u32[]{:S(2)}, u32[]{:S(2)}) async-start(f32[32,9,2,128]{3,2,1,0:T(2,128)} %bitcast.4), calls=%async_computation.1 | async-start | bytes 589824 | tf_op jit(solution)/shard_map/all_to_all | solution.py:403
  17.7 9.8 %collective-permute-start.1 = (f32[96,256]{1,0:T(8,128)S(1)}, f32[96,256]{1,0:T(8,128)S(1)}, u32[]{:S(2)}, u32[]{:S(2)}) collective-permute-start(f32[96,256]{1,0:T(8,128)S(1)} %copy-done.3), channel_id=1, source_target_pairs={{0,16},{8,24},{16,0},{24,8},{1,17},{9,25},{17,1},{25,9},{2,18},{10... | collective-permute-start | bytes 294920 | tf_op jit(solution)/shard_map/ppermute | solution.py:319
  19.6 8.0 %collective-permute-start = (f32[96,256]{1,0:T(8,128)S(1)}, f32[96,256]{1,0:T(8,128)S(1)}, u32[]{:S(2)}, u32[]{:S(2)}) collective-permute-start(f32[96,256]{1,0:T(8,128)S(1)} %copy-done.3), channel_id=1, source_target_pairs={{0,8},{8,16},{16,24},{24,0},{1,9},{9,17},{17,25},{25,1},{2,10},{10... | collective-permute-start | bytes 294920 | tf_op jit(solution)/shard_map/ppermute | solution.py:319
  21.0 7.0 %collective-permute-start.2 = (f32[96,256]{1,0:T(8,128)S(1)}, f32[96,256]{1,0:T(8,128)S(1)}, u32[]{:S(2)}, u32[]{:S(2)}) collective-permute-start(f32[96,256]{1,0:T(8,128)S(1)} %copy-done.3), channel_id=1, source_target_pairs={{0,24},{8,0},{16,8},{24,16},{1,25},{9,1},{17,9},{25,17},{2,26},{10... | collective-permute-start | bytes 294920 | tf_op jit(solution)/shard_map/ppermute | solution.py:319
  31.3 11.3 %copy-start.6 = (bf16[2,64,256]{2,1,0:T(8,128)(2,1)S(1)}, bf16[2,64,256]{2,1,0:T(8,128)(2,1)}, u32[]{:S(2)}) copy-start(bf16[2,64,256]{2,1,0:T(8,128)(2,1)} %constant.26.clone.first_ref) | copy-start | bytes 196612
  58.1 9.7 %copy-start.5 = (bf16[2,64,256]{2,1,0:T(8,128)(2,1)S(1)}, bf16[2,64,256]{2,1,0:T(8,128)(2,1)}, u32[]{:S(2)}) copy-start(bf16[2,64,256]{2,1,0:T(8,128)(2,1)} %constant.27.clone.first_ref) | copy-start | bytes 196612

commit v5 on v4

--- a/solution.py
+++ b/solution.py
@@ -159,9 +159,9 @@
     )
 
 
-def work_out_turns(total, rates_ref, half_ref, full_ref):
+def work_out_turns(total, share, rates_ref, table_ref):
     rows = rates_ref.shape[0]
-    _, count, block = half_ref.shape
+    _, count, block = table_ref.shape
     size = count // rows
     first, last = (lax.broadcasted_iota(jnp.int32, (size, block), d) for d in range(2))
     freq = first + size * last
@@ -175,12 +175,10 @@
             + rates_ref[r : r + 1, 2 : 3] * square / 2.0
             + rates_ref[r : r + 1, 3 : 4] * (square * freq) / 6.0
         )
-        cosine, sine = cos_sin(phase * 0.5)
+        cosine, sine = cos_sin(phase * share)
         part = pl.ds(r * size, size)
-        half_ref[0, part] = cosine * scale
-        half_ref[1, part] = sine * scale
-        full_ref[0, part] = (cosine * cosine - sine * sine) * scale
-        full_ref[1, part] = (2.0 * scale) * cosine * sine
+        table_ref[0, part] = cosine * scale
+        table_ref[1, part] = sine * scale
 
 
 def profile_kernel(rows, *refs):
@@ -204,12 +202,12 @@
         start += width
 
 
-def disperse_kernel(rows, total, load, store, x_ref, first_ref, last_ref, twist_ref, *refs):
-    if total is not None:
-        rates_ref, o_ref, turn_ref, full_ref = refs
-        work_out_turns(total, rates_ref, turn_ref, full_ref)
+def disperse_kernel(rows, total, share, load, store, x_ref, first_ref, final_ref, last_ref, twist_ref, *refs):
+    if total is None:
+        turn_ref, o_ref = refs
     else:
-        turn_ref, o_ref = refs
+        o_ref, turn_ref = refs[-2:]
+        work_out_turns(total, share, refs[0], turn_ref)
     n_dev, block = twist_ref.shape[1:]
     cos_high, sin_high, cos_low, sin_low = (last_ref[:, n * block : (n + 1) * block] for n in range(4))
     last_high = jnp.concatenate(
@@ -220,9 +218,9 @@
     )
     twist = [jnp.concatenate([twist_ref[c]] * rows, axis=1) for c in range(2)]
 
-    def across(place, values):
+    def across(matrix_ref, values):
         high, low = split_two(values)
-        return product(first_ref[place], jnp.concatenate([high, high, low, low], axis=0))
+        return product(matrix_ref[...], jnp.concatenate([high, high, low, low], axis=0))
 
     def twisted(values):
         re, im = values[:n_dev], values[n_dev:]
@@ -243,29 +241,26 @@
     x = jnp.concatenate(
         [jnp.concatenate([load(x_ref, r, c) for r in range(rows)], axis=1) for c in range(2)], axis=0
     )
-    re, im = twisted(across(0, x))
+    re, im = twisted(across(first_ref, x))
     z = along(row_of(re), row_of(im))
     z_re, z_im = z[:, :block], z[:, block:]
     turn_re, turn_im = turn_ref[0], turn_ref[1]
     z = along(z_re * turn_re - z_im * turn_im, -(z_re * turn_im + z_im * turn_re))
     re, im = twisted(jnp.concatenate([lane_of(z[:, :block]), lane_of(z[:, block:])], axis=0))
-    x = across(1, jnp.concatenate([re, im], axis=0))
+    x = across(final_ref, jnp.concatenate([re, im], axis=0))
     for r in range(rows):
         lanes = slice(r * block, (r + 1) * block)
-        store(o_ref, r, 0, x[:n_dev, lanes])
-        store(o_ref, r, 1, -x[n_dev:, lanes])
-
-
-def nonlinear_kernel(rows, halo, w_ref, up_ref, down_ref, raman_ref, o_ref):
+        store(o_ref, r, 0, x[: x.shape[0] // 2, lanes])
+        store(o_ref, r, 1, -x[x.shape[0] // 2 :, lanes])
+
+
+def nonlinear_kernel(rows, halo, load, store, w_ref, up_ref, down_ref, raman_ref, o_ref):
     block = w_ref.shape[1]
-    n_dev = w_ref.shape[0] // ((halo + 1) * rows * 2)
-    n_modes = n_dev * rows
-    chunk = (halo + 1) * rows * 2
+    n_modes = up_ref.shape[1] // 4
+    count = n_modes // rows
 
     def part(h, c):
-        return jnp.concatenate(
-            [w_ref[pl.ds(h * 2 * rows + 2 * r + c, n_dev, stride=chunk), :] for r in range(rows)], axis=0
-        )
+        return jnp.concatenate([load(w_ref, h, r, c) for r in range(rows)], axis=0)
 
     own, highs, lows = None, [], []
     for h in range(halo + 1):
@@ -299,7 +294,7 @@
     ]
     for c in range(2):
         for r in range(rows):
-            o_ref[pl.ds(2 * r + c, n_dev, stride=2 * rows), :] = out[c][r * n_dev : (r + 1) * n_dev]
+            store(o_ref, r, c, out[c][r * count : (r + 1) * count])
 
 
 def tiled(field, modes, betas):
@@ -313,6 +308,13 @@
     rows = own_modes // n_tm
     per_tm = samples // block
     f32 = jnp.float32
+
+    quarter = n_tm // 2
+    n_pair = n_mode * quarter
+    wide = 2 * rows
+    halves = [[m * n_tm + h * quarter + q for m in range(n_mode) for q in range(quarter)] for h in range(2)]
+    both_halves = [halves[0] + halves[1]]
+    half = t_index // quarter
 
     pieces = [modes]
     for shift in range(1, n_mode):
@@ -328,7 +330,7 @@
     edge = np.arange(n_dev).reshape(n_tm, per_tm).T.reshape(-1)
 
     def flat(matrix):
-        high, low = np_split(matrix.reshape(2 * n_dev, 2 * n_dev))
+        high, low = np_split(matrix.reshape(-1, 2 * n_dev))
         return np.concatenate([high, low, high, low], axis=1)
 
     span = (halo + 1) * block
@@ -336,6 +338,10 @@
     lags[:, block + 1 : block + 1 + RAMAN_TAPS] = RAMAN_SHARE * raman_taps()
 
     rates = lax.dynamic_slice_in_dim(betas, t_index * rows, rows, 0)
+    rates_wide = lax.dynamic_slice_in_dim(betas, (t_index % quarter) * wide, wide, 0)
+    windows_of = [[(a - halo + h) % n_dev for h in range(halo + 1) for a in devices] for devices in halves]
+    final_wide = jnp.asarray(np.stack([flat(first[:, blocks]) for blocks in windows_of]))
+    final_wide = lax.dynamic_index_in_dim(final_wide, half, 0, keepdims=False)
 
     def load_edge(ref, r, c):
         return jnp.concatenate(
@@ -358,28 +364,51 @@
             moved = pltpu.roll(values, halo - h, axis=0) if h < halo else values
             ref[pl.ds(2 * (h * rows + r) + c, n_dev, stride=2 * (halo + 1) * rows), :] = moved
 
-    def disperse(values, turn, entering, leaving):
-        shape = (n_tm, rows, 2, samples) if leaving else (n_dev * (halo + 1) * rows * 2, block)
-        shape = jax.ShapeDtypeStruct(shape, f32)
-        table = jax.ShapeDtypeStruct((2, rows * n_dev, block), f32)
-        matrices = np.stack([flat(first[..., edge] if entering else first), flat(first[:, edge] if leaving else first)])
-        return pl.pallas_call(
-            functools.partial(
-                disperse_kernel,
-                rows,
-                total if entering else None,
-                load_edge if entering else load_inner,
-                store_edge if leaving else store_inner,
-            ),
-            out_shape=(shape, table, table) if entering else shape,
-                        name="disperse",
-            compiler_params=PARAMS,
-        )(values, jnp.asarray(matrices), last, twist, turn)
+    def load_wide(ref, r, c):
+        return ref[pl.ds(2 * r + c, n_dev, stride=2 * wide), :]
+
+    def store_wide(ref, r, c, values):
+        for h in range(halo + 1):
+            ref[pl.ds(2 * (h * wide + r) + c, n_pair, stride=2 * (halo + 1) * wide), :] = values[
+                h * n_pair : (h + 1) * n_pair
+            ]
+
+    def call_disperse(kernel, shape, *operands, **options):
+        return pl.pallas_call(kernel, out_shape=shape, compiler_params=PARAMS, **options)(*operands)
+
+    def table_of(count):
+        return (2, count * n_dev, block)
+
+    def enter(values):
+        kernel = functools.partial(disperse_kernel, rows, total, 0.5, load_edge, store_inner)
+        shapes = ((n_dev * (halo + 1) * rows * 2, block), table_of(rows))
+        matrices = (jnp.asarray(flat(first[..., edge])), jnp.asarray(flat(first)))
+        return call_disperse(
+            kernel,
+            tuple(jax.ShapeDtypeStruct(shape, f32) for shape in shapes),
+            *(values, *matrices, last, twist, rates, rates_wide, final_wide),
+        )
+
+    def go_on(values):
+        kernel = functools.partial(disperse_kernel, wide, total, 1.0, load_wide, store_wide)
+        shape = jax.ShapeDtypeStruct((n_pair * (halo + 1) * wide * 2, block), f32)
+        return call_disperse(
+            kernel,
+            shape,
+            *(values, jnp.asarray(flat(first[..., both_halves[0]])), final_wide, last, twist, rates_wide),
+            scratch_shapes=[pltpu.VMEM(table_of(wide), f32)],
+        )
+
+    def leave(values, turn):
+        kernel = functools.partial(disperse_kernel, rows, None, None, load_inner, store_edge)
+        shape = jax.ShapeDtypeStruct((n_tm, rows, 2, samples), f32)
+        matrices = (jnp.asarray(flat(first)), jnp.asarray(flat(first[:, edge])))
+        return call_disperse(kernel, shape, values, *matrices, last, twist, turn)
 
     def spread_profiles(windows):
         total_grid = modes.shape[1] * n_mode
         return pl.pallas_call(
-            functools.partial(profile_kernel, rows),
+            functools.partial(profile_kernel, wide),
             out_shape=(
                 jax.ShapeDtypeStruct((total_grid, 4 * n_dev * rows), jnp.bfloat16),
                 jax.ShapeDtypeStruct((2 * n_dev * rows, total_grid), jnp.bfloat16),
@@ -390,30 +419,54 @@
             compiler_params=PARAMS,
         )(*pieces, jnp.asarray(lags, f32), windows)
 
-    def nonlinear(windows, up, down, raman):
+    def load_spread(ref, h, r, c):
+        start = (r // rows) * 2 * (halo + 1) * rows + 2 * (h * rows + r % rows) + c
+        return ref[pl.ds(start, n_pair, stride=4 * (halo + 1) * rows), :]
+
+    def load_half(ref, h, r, c):
+        return ref[pl.ds(2 * (h * wide + r) + c, n_pair, stride=2 * (halo + 1) * wide), :]
+
+    def store_halves(ref, r, c, values):
+        for h in range(2):
+            ref[pl.ds(h * n_pair * 2 * wide + 2 * r + c, n_pair, stride=2 * wide), :] = values
+
+    def store_last(ref, r, c, values):
+        ref[pl.ds((r // rows) * 2 * rows + 2 * (r % rows) + c, n_pair, stride=4 * rows), :] = values
+
+    def nonlinear(number, windows, up, down, raman):
+        is_last = number == ITERS - 1
+        height = n_dev * (rows if is_last else wide) * 2
         return pl.pallas_call(
-            functools.partial(nonlinear_kernel, rows, halo),
-            out_shape=jax.ShapeDtypeStruct((n_dev * rows * 2, block), f32),
+            functools.partial(
+                nonlinear_kernel,
+                wide,
+                halo,
+                load_half if number else load_spread,
+                store_last if is_last else store_halves,
+            ),
+            out_shape=jax.ShapeDtypeStruct((height, block), f32),
             name="nonlinear",
             compiler_params=PARAMS,
         )(windows, up, down, raman)
 
-    def exchange(values):
-        shaped = values.reshape(n_dev, -1, 2, block)
-        return lax.all_to_all(shaped, BOTH, 0, 0, tiled=True).reshape(-1, block)
+    def exchange(values, groups=None):
+        count = len(groups[0]) if groups else n_dev
+        shaped = values.reshape(count, -1, 2, block)
+        return lax.all_to_all(shaped, BOTH, 0, 0, tiled=True, axis_index_groups=groups).reshape(-1, block)
 
     entry = field.reshape(own_modes, 2, per_tm, block)
     entry = with_layout_constraint(entry, Layout((0, 2, 1, 3)))
     entry = entry.transpose(0, 2, 1, 3).reshape(n_tm, rows * per_tm, 2, block)
     values = lax.all_to_all(entry, "tm", 0, 0, tiled=True).reshape(-1, block)
-    values, half_turn, full_turn = disperse(values, rates, True, False)
+    values, half_turn = enter(values)
+    values = exchange(values)
+    profiles = spread_profiles(values)
     for number in range(ITERS):
-        values = exchange(values)
-        if number == 0:
-            profiles = spread_profiles(values)
-        values = nonlinear(values, *profiles)
-        leaving = number == ITERS - 1
-        values = disperse(exchange(values), half_turn if leaving else full_turn, False, leaving)
+        values = nonlinear(number, values, *profiles)
+        if number < ITERS - 1:
+            values = go_on(exchange(values, both_halves))
+            values = exchange(values, halves)
+    values = leave(exchange(values), half_turn)
     return lax.all_to_all(values, "tm", 0, 0, tiled=True).reshape(field.shape)
 
 

time: 78.4 us -> 77.2 us (0.985)
  blocking collectives: 42.7 us -> 41.3 us
    all_to_all x3, blocking collectives: 34 us -> 32.6 us  [exchange(): lax.all_to_all(shaped, BOTH, 0, 0, tiled=True, axis_index_groups=groups)]
where the time goes in v5:
time: 77.2 us; the launch traced here: 76.7 us
  blocking collectives  41.3 us (53%)
  starting transfers between devices  14.7 us (19%)
  waiting for transfers between devices  12.5 us (16%)
  Pallas kernels  7.09 us (9%)
  local copies, waits for them, and re-layouts  1.03 us (1%)
    all_to_all x3, blocking collectives, exchange(): lax.all_to_all(shaped, BOTH, 0, 0, tiled=True, axis_index_groups=groups)  32.6 us
    all_to_all x1, blocking collectives, tiled(): return lax.all_to_all(values, 'tm', 0, 0, tiled=True).reshape(field.shape)  8.7 us
    all_to_all x1, starting transfers between devices, tiled(): values = lax.all_to_all(entry, 'tm', 0, 0, tiled=True).reshape(-1, block)  6.51 us
    all_to_all x1, waiting for transfers between devices, tiled(): values = lax.all_to_all(entry, 'tm', 0, 0, tiled=True).reshape(-1, block)  5.91 us
    ppermute x3, waiting for transfers between devices, tiled(): lax.ppermute(modes, 'mode', [(i, (i + shift) % n_mode) for i in range(n_m...  5.58 us
    ppermute x3, starting transfers between devices, tiled(): lax.ppermute(modes, 'mode', [(i, (i + shift) % n_mode) for i in range(n_m...  4.76 us
    pallas_call x2, Pallas kernels, nonlinear(): pl.pallas_call(functools.partial(nonlinear_kernel, wide, halo, load_half...  3.6 us
    all_to_all x1, starting transfers between devices, exchange(): lax.all_to_all(shaped, BOTH, 0, 0, tiled=True, axis_index_groups=groups)  3.43 us
  transfers between devices with their start and end apart: 5, of which 4 were waited for; matrix products, arithmetic and copies ran while one was open for 0% of the time, Pallas kernels for 0%

profile of v5, /device:TPU:0, one launch (start us, length us, event | category | flops | bytes accessed | tf_op | source)
XLA Modules:
  0.0 76.7 jit_solution(7387802035565386346)
XLA Ops:
  0.0 0.0 copy-start
  0.0 6.5 %all-to-all-start = ((f32[8,12,2,128]{3,2,1,0:T(2,128)}), f32[8,12,2,128]{3,2,1,0:T(2,128)S(1)}, u32[]{:S(2)}, u32[]{:S(2)}) async-start(f32[8,12,2,128]{3,2,1,0:T(2,128)} %bitcast.27), calls=%async_computation | async-start | bytes 196608 | tf_op jit(solution)/shard_map/all_to_all | solution.py:460
  6.6 0.0 copy-done
  6.6 0.1 constant_dynamic-slice_fusion.1
  6.6 0.1 copy.15.refs_0_
  6.7 0.1 constant_dynamic-slice_fusion
  6.8 0.1 copy.16.refs_1_.refs_0_
  6.9 0.0 copy-done.9
  6.9 5.9 %all-to-all-done = f32[8,12,2,128]{3,2,1,0:T(2,128)S(1)} async-done(((f32[8,12,2,128]{3,2,1,0:T(2,128)}), f32[8,12,2,128]{3,2,1,0:T(2,128)S(1)}, u32[]{:S(2)}, u32[]{:S(2)}) %all-to-all-start) | async-done | bytes 98336 | tf_op jit(solution)/shard_map/all_to_all | solution.py:460
  12.8 0.0 copy-done.2
  12.9 1.4 %shard_map.118 = (f32[576,128]{1,0:T(8,128)}, f32[2,96,128]{2,1,0:T(8,128)S(1)}) custom-call(f32[192,128]{1,0:T(8,128)S(1)} %bitcast.25, bf16[64,256]{1,0:T(8,128)(2,1)S(1)} %copy-done.7, bf16[64,256]{1,0:T(8,128)(2,1)S(1)} %copy-done.3, bf16[128,512]{1,0:T(8,128)(2,1)S(1)} %copy-done.1, f32[2,32,128]{2,1,0:T(8,128)S(1)} %copy-done.2, ...), custom_call_target="tpu_custom_call" | custom-call | tf_op jit(solution)/shard_map/pallas_call | solution.py:377
  14.3 3.4 %all-to-all-start.1 = ((f32[32,9,2,128]{3,2,1,0:T(2,128)}), f32[32,9,2,128]{3,2,1,0:T(2,128)S(1)}, u32[]{:S(2)}, u32[]{:S(2)}) async-start(f32[32,9,2,128]{3,2,1,0:T(2,128)} %bitcast.5), calls=%async_computation.1 | async-start | bytes 589824 | tf_op jit(solution)/shard_map/all_to_all | solution.py:455
  17.7 1.8 %collective-permute-start.1 = (f32[96,256]{1,0:T(8,128)S(1)}, f32[96,256]{1,0:T(8,128)S(1)}, u32[]{:S(2)}, u32[]{:S(2)}) collective-permute-start(f32[96,256]{1,0:T(8,128)S(1)} %copy-done.4), channel_id=1, source_target_pairs={{0,16},{8,24},{16,0},{24,8},{1,17},{9,25},{17,1},{25,9},{2,18},{10... | collective-permute-start | bytes 294920 | tf_op jit(solution)/shard_map/ppermute | solution.py:321
  19.6 1.5 %collective-permute-start = (f32[96,256]{1,0:T(8,128)S(1)}, f32[96,256]{1,0:T(8,128)S(1)}, u32[]{:S(2)}, u32[]{:S(2)}) collective-permute-start(f32[96,256]{1,0:T(8,128)S(1)} %copy-done.4), channel_id=1, source_target_pairs={{0,8},{8,16},{16,24},{24,0},{1,9},{9,17},{17,25},{25,1},{2,10},{10... | collective-permute-start | bytes 294920 | tf_op jit(solution)/shard_map/ppermute | solution.py:321
  21.0 1.5 %collective-permute-start.2 = (f32[96,256]{1,0:T(8,128)S(1)}, f32[96,256]{1,0:T(8,128)S(1)}, u32[]{:S(2)}, u32[]{:S(2)}) collective-permute-start(f32[96,256]{1,0:T(8,128)S(1)} %copy-done.4), channel_id=1, source_target_pairs={{0,24},{8,0},{16,8},{24,16},{1,25},{9,1},{17,9},{25,17},{2,26},{10... | collective-permute-start | bytes 294920 | tf_op jit(solution)/shard_map/ppermute | solution.py:321
  22.5 5.0 %collective-permute-done.1.refs_2_ = f32[96,256]{1,0:T(8,128)S(1)} collective-permute-done((f32[96,256]{1,0:T(8,128)S(1)}, f32[96,256]{1,0:T(8,128)S(1)}, u32[]{:S(2)}, u32[]{:S(2)}) %collective-permute-start.1) | collective-permute-done | bytes 98336 | tf_op jit(solution)/shard_map/ppermute | solution.py:321
  27.5 0.0 collective-permute-done.refs_1_
  27.6 0.5 collective-permute-done.2.refs_3_
  28.1 1.0 %all-to-all-done.1 = f32[32,9,2,128]{3,2,1,0:T(2,128)S(1)} async-done(((f32[32,9,2,128]{3,2,1,0:T(2,128)}), f32[32,9,2,128]{3,2,1,0:T(2,128)S(1)}, u32[]{:S(2)}, u32[]{:S(2)}) %all-to-all-start.1) | async-done | bytes 294944 | tf_op jit(solution)/shard_map/all_to_all | solution.py:455
  29.1 0.4 profiles.1
  29.5 1.8 %nonlinear.2 = f32[384,128]{1,0:T(8,128)S(1)} custom-call(f32[576,128]{1,0:T(8,128)S(1)} %bitcast.18, bf16[1024,384]{1,0:T(8,128)(2,1)S(1)} %get-tuple-element.11.up_ref, bf16[192,1024]{1,0:T(8,128)(2,1)S(1)} %get-tuple-element.12.down_ref, bf16[384,256]{1,0:T(8,128)(2,1)S(1)} %get-tuple-element.13.raman_ref), custom_call_target="tpu_custom_call" | custom-call | tf_op jit(solution)/shard_map/nonlinear/pallas_call | solution.py:439
  31.3 0.0 copy-start.6
  31.3 12.3 %all_to_all.30 = f32[32,6,2,128]{3,2,1,0:T(2,128)S(1)} all-to-all(f32[32,6,2,128]{3,2,1,0:T(2,128)S(1)} %bitcast.21), channel_id=1, replica_groups={{0,1,2,3,8,9,10,11,16,17,18,19,24,25,26,27,4,5,6,7,12,13,14,15,20,21,22..., dimensions={0} | all-to-all | bytes 393216 | tf_op jit(solution)/shard_map/all_to_all | solution.py:455
  43.7 0.9 %shard_map.119 = f32[576,128]{1,0:T(8,128)S(1)} custom-call(f32[384,128]{1,0:T(8,128)S(1)} %bitcast.22, bf16[64,256]{1,0:T(8,128)(2,1)S(1)} %copy-done.6, bf16[96,256]{1,0:T(8,128)(2,1)S(1)} %dynamic-slice_bitcast_fusion.refs_2_.final_ref, bf16[128,512]{1,0:T(8,128)(2,1)S(1)} %copy-done.1, f32[2,32,128]{2,1,0:T(8,128)S(1)} %copy-done.2, ...), custom_call_target="tpu_custom_call" | custom-call | tf_op jit(solution)/shard_map/pallas_call | solution.py:377
  44.6 10.8 %all_to_all.31 = f32[16,18,2,128]{3,2,1,0:T(2,128)S(1)} all-to-all(f32[16,18,2,128]{3,2,1,0:T(2,128)S(1)} %bitcast.20), channel_id=1, replica_groups={{0,1,2,3,8,9,10,11,16,17,18,19,24,25,26,27},{4,5,6,7,12,13,14,15,20,21,..., dimensions={0} | all-to-all | bytes 589824 | tf_op jit(solution)/shard_map/all_to_all | solution.py:455
  55.3 1.8 %nonlinear.3 = f32[192,128]{1,0:T(8,128)S(1)} custom-call(f32[576,128]{1,0:T(8,128)S(1)} %bitcast.19, bf16[1024,384]{1,0:T(8,128)(2,1)S(1)} %get-tuple-element.11.up_ref, bf16[192,1024]{1,0:T(8,128)(2,1)S(1)} %get-tuple-element.12.down_ref, bf16[384,256]{1,0:T(8,128)(2,1)S(1)} %get-tuple-element.13.raman_ref), custom_call_target="tpu_custom_call" | custom-call | tf_op jit(solution)/shard_map/nonlinear/pallas_call | solution.py:439
  57.1 0.0 copy-start.5
  57.1 9.4 %all_to_all.32 = f32[32,3,2,128]{3,2,1,0:T(2,128)S(1)} all-to-all(f32[32,3,2,128]{3,2,1,0:T(2,128)S(1)} %bitcast.24), channel_id=1, replica_groups=mesh['mode'=4,'tm'=8] {'mode','tm'}, dimensions={0} | all-to-all | bytes 196608 | tf_op jit(solution)/shard_map/all_to_all | solution.py:455
  66.6 0.0 copy-done.5
  66.6 0.7 shard_map.120
  67.3 8.7 %all_to_all.33 = f32[8,3,2,512]{3,2,1,0:T(2,128)S(1)} all-to-all(f32[8,3,2,512]{3,2,1,0:T(2,128)S(1)} %shard_map.120), channel_id=1, replica_groups=mesh['mode'=4,'tm'=8] {'tm'}, dimensions={0} | all-to-all | bytes 196608 | tf_op jit(solution)/shard_map/all_to_all | solution.py:470
  76.0 0.6 copy.18
  (14 shorter events, 0.0 us)
Async XLA Ops:
  0.0 6.6 %copy-start = (f32[24,4]{0,1:T(4,128)S(1)}, f32[24,4]{0,1:T(4,128)}, u32[]{:S(2)}) copy-start(f32[24,4]{0,1:T(4,128)} %param.14) | copy-start | bytes 1156
  0.0 6.9 %copy-start.9 = (bf16[2,96,256]{2,1,0:T(8,128)(2,1)S(1)}, bf16[2,96,256]{2,1,0:T(8,128)(2,1)}, u32[]{:S(2)}) copy-start(bf16[2,96,256]{2,1,0:T(8,128)(2,1)} %constant.58.clone) | copy-start | bytes 294916
  0.0 12.8 %copy-start.3 = (bf16[64,256]{1,0:T(8,128)(2,1)S(1)}, bf16[64,256]{1,0:T(8,128)(2,1)}, u32[]{:S(2)}) copy-start(bf16[64,256]{1,0:T(8,128)(2,1)} %constant.60.clone.final_ref.first_ref) | copy-start | bytes 98308
  0.0 12.8 %copy-start.7 = (bf16[64,256]{1,0:T(8,128)(2,1)S(1)}, bf16[64,256]{1,0:T(8,128)(2,1)}, u32[]{:S(2)}) copy-start(bf16[64,256]{1,0:T(8,128)(2,1)} %constant.59.clone.first_ref) | copy-start | bytes 98308
  0.0 12.8 %all-to-all-start = ((f32[8,12,2,128]{3,2,1,0:T(2,128)}), f32[8,12,2,128]{3,2,1,0:T(2,128)S(1)}, u32[]{:S(2)}, u32[]{:S(2)}) async-start(f32[8,12,2,128]{3,2,1,0:T(2,128)} %bitcast.27), calls=%async_computation | async-start | bytes 196608 | tf_op jit(solution)/shard_map/all_to_all | solution.py:460
  6.5 6.3 %copy-start.1 = (bf16[128,512]{1,0:T(8,128)(2,1)S(1)}, bf16[128,512]{1,0:T(8,128)(2,1)}, u32[]{:S(2)}) copy-start(bf16[128,512]{1,0:T(8,128)(2,1)} %constant.56.clone.last_ref) | copy-start | bytes 393220
  6.9 5.9 %copy-start.2 = (f32[2,32,128]{2,1,0:T(8,128)S(1)}, f32[2,32,128]{2,1,0:T(8,128)}, u32[]{:S(2)}) copy-start(f32[2,32,128]{2,1,0:T(8,128)} %constant.57.clone.twist_ref) | copy-start | bytes 98308
  14.3 3.4 %copy-start.4 = (f32[96,256]{1,0:T(8,128)S(1)}, f32[96,256]{1,0:T(8,128)}, u32[]{:S(2)}) copy-start(f32[96,256]{1,0:T(8,128)} %refs_0_.1) | copy-start | bytes 294916
  14.3 14.8 %copy-start.8 = (f32[8,512]{1,0:T(8,128)S(1)}, f32[8,512]{1,0:T(8,128)}, u32[]{:S(2)}) copy-start(f32[8,512]{1,0:T(8,128)} %constant.61.clone.refs_4_) | copy-start | bytes 49156
  14.3 14.8 %all-to-all-start.1 = ((f32[32,9,2,128]{3,2,1,0:T(2,128)}), f32[32,9,2,128]{3,2,1,0:T(2,128)S(1)}, u32[]{:S(2)}, u32[]{:S(2)}) async-start(f32[32,9,2,128]{3,2,1,0:T(2,128)} %bitcast.5), calls=%async_computation.1 | async-start | bytes 589824 | tf_op jit(solution)/shard_map/all_to_all | solution.py:455
  17.7 9.8 %collective-permute-start.1 = (f32[96,256]{1,0:T(8,128)S(1)}, f32[96,256]{1,0:T(8,128)S(1)}, u32[]{:S(2)}, u32[]{:S(2)}) collective-permute-start(f32[96,256]{1,0:T(8,128)S(1)} %copy-done.4), channel_id=1, source_target_pairs={{0,16},{8,24},{16,0},{24,8},{1,17},{9,25},{17,1},{25,9},{2,18},{10... | collective-permute-start | bytes 294920 | tf_op jit(solution)/shard_map/ppermute | solution.py:321
  19.6 8.0 %collective-permute-start = (f32[96,256]{1,0:T(8,128)S(1)}, f32[96,256]{1,0:T(8,128)S(1)}, u32[]{:S(2)}, u32[]{:S(2)}) collective-permute-start(f32[96,256]{1,0:T(8,128)S(1)} %copy-done.4), channel_id=1, source_target_pairs={{0,8},{8,16},{16,24},{24,0},{1,9},{9,17},{17,25},{25,1},{2,10},{10... | collective-permute-start | bytes 294920 | tf_op jit(solution)/shard_map/ppermute | solution.py:321
  21.0 7.0 %collective-permute-start.2 = (f32[96,256]{1,0:T(8,128)S(1)}, f32[96,256]{1,0:T(8,128)S(1)}, u32[]{:S(2)}, u32[]{:S(2)}) collective-permute-start(f32[96,256]{1,0:T(8,128)S(1)} %copy-done.4), channel_id=1, source_target_pairs={{0,24},{8,0},{16,8},{24,16},{1,25},{9,1},{17,9},{25,17},{2,26},{10... | collective-permute-start | bytes 294920 | tf_op jit(solution)/shard_map/ppermute | solution.py:321
  31.3 12.4 %copy-start.6 = (bf16[64,256]{1,0:T(8,128)(2,1)S(1)}, bf16[64,256]{1,0:T(8,128)(2,1)}, u32[]{:S(2)}) copy-start(bf16[64,256]{1,0:T(8,128)(2,1)} %constant.62.clone.first_ref) | copy-start | bytes 98308
  57.1 9.5 %copy-start.5 = (bf16[64,256]{1,0:T(8,128)(2,1)S(1)}, bf16[64,256]{1,0:T(8,128)(2,1)}, u32[]{:S(2)}) copy-start(bf16[64,256]{1,0:T(8,128)(2,1)} %constant.63.clone.final_ref) | copy-start | bytes 98308

commit v6 on v5

--- a/solution.py
+++ b/solution.py
@@ -159,8 +159,7 @@
     )
 
 
-def work_out_turns(total, share, rates_ref, table_ref):
-    rows = rates_ref.shape[0]
+def work_out_turns(total, share, rows, start, betas_ref, table_ref):
     _, count, block = table_ref.shape
     size = count // rows
     first, last = (lax.broadcasted_iota(jnp.int32, (size, block), d) for d in range(2))
@@ -169,11 +168,12 @@
     square = freq * freq
     scale = 1.0 / total
     for r in range(rows):
+        rates = betas_ref[pl.ds(start + r, 1), :]
         phase = (
-            rates_ref[r : r + 1, 0 : 1]
-            + rates_ref[r : r + 1, 1 : 2] * freq
-            + rates_ref[r : r + 1, 2 : 3] * square / 2.0
-            + rates_ref[r : r + 1, 3 : 4] * (square * freq) / 6.0
+            rates[:, 0 : 1]
+            + rates[:, 1 : 2] * freq
+            + rates[:, 2 : 3] * square / 2.0
+            + rates[:, 3 : 4] * (square * freq) / 6.0
         )
         cosine, sine = cos_sin(phase * share)
         part = pl.ds(r * size, size)
@@ -181,8 +181,7 @@
         table_ref[1, part] = sine * scale
 
 
-def profile_kernel(rows, *refs):
-    pieces, taps_ref, (up_ref, down_ref, raman_ref) = refs[:-5], refs[-5], refs[-3:]
+def make_profiles(rows, pieces, taps_ref, up_ref, down_ref, raman_ref):
     window, double = raman_ref.shape
     block = double // 2
     taps = jnp.broadcast_to(taps_ref[0:1, :], (window, taps_ref.shape[1]))
@@ -197,18 +196,23 @@
         width = piece.shape[1]
         wide, low = (product(order, part) for part in split_two(piece[...]))
         down_ref[:, start : start + width] = jnp.concatenate([wide, low], axis=0).astype(jnp.bfloat16)
-        stack = jnp.concatenate([wide, low, wide, low], axis=0)
+        stack = jnp.concatenate([wide, low, wide], axis=0)
         up_ref[start : start + width, :] = stack.T.astype(jnp.bfloat16)
         start += width
 
 
-def disperse_kernel(rows, total, share, load, store, x_ref, first_ref, final_ref, last_ref, twist_ref, *refs):
+def disperse_kernel(rows, total, share, joined, load, store, x_ref, *refs):
+    count = 1 if joined else 2
+    matrices, last_ref, refs = refs[:count], refs[count], refs[count + 1 :]
+    n_dev, block = matrices[0].shape[1] // 2, last_ref.shape[0]
     if total is None:
         turn_ref, o_ref = refs
     else:
-        o_ref, turn_ref = refs[-2:]
-        work_out_turns(total, share, refs[0], turn_ref)
-    n_dev, block = twist_ref.shape[1:]
+        betas_ref, o_ref, turn_ref = refs
+        place = lax.axis_index("tm")
+        holders = betas_ref.shape[0] // rows
+        work_out_turns(total, share, rows, place % holders * rows, betas_ref, turn_ref)
+        place = place // holders
     cos_high, sin_high, cos_low, sin_low = (last_ref[:, n * block : (n + 1) * block] for n in range(4))
     last_high = jnp.concatenate(
         [jnp.concatenate([cos_high, -sin_high], axis=1), jnp.concatenate([sin_high, cos_high], axis=1)], axis=0
@@ -216,11 +220,14 @@
     last_low = jnp.concatenate(
         [jnp.concatenate([cos_low, -sin_low], axis=1), jnp.concatenate([sin_low, cos_low], axis=1)], axis=0
     )
-    twist = [jnp.concatenate([twist_ref[c]] * rows, axis=1) for c in range(2)]
-
-    def across(matrix_ref, values):
+    place_of, time_of = (lax.broadcasted_iota(jnp.int32, (n_dev, block), d) for d in range(2))
+    twist = cos_sin((place_of * time_of).astype(jnp.float32) * (2.0 * math.pi / (n_dev * block)))
+    twist = [jnp.concatenate([part] * rows, axis=1) for part in twist]
+
+    def across(matrix, values):
         high, low = split_two(values)
-        return product(matrix_ref[...], jnp.concatenate([high, high, low, low], axis=0))
+        matrix = jnp.concatenate([matrix, matrix], axis=1)
+        return product(matrix, jnp.concatenate([high, high, low, low], axis=0))
 
     def twisted(values):
         re, im = values[:n_dev], values[n_dev:]
@@ -241,22 +248,27 @@
     x = jnp.concatenate(
         [jnp.concatenate([load(x_ref, r, c) for r in range(rows)], axis=1) for c in range(2)], axis=0
     )
-    re, im = twisted(across(first_ref, x))
+    re, im = twisted(across(matrices[0][0], x))
     z = along(row_of(re), row_of(im))
     z_re, z_im = z[:, :block], z[:, block:]
     turn_re, turn_im = turn_ref[0], turn_ref[1]
     z = along(z_re * turn_re - z_im * turn_im, -(z_re * turn_im + z_im * turn_re))
     re, im = twisted(jnp.concatenate([lane_of(z[:, :block]), lane_of(z[:, block:])], axis=0))
-    x = across(final_ref, jnp.concatenate([re, im], axis=0))
+    x = across(matrices[0][1] if joined else matrices[1][place], jnp.concatenate([re, im], axis=0))
     for r in range(rows):
         lanes = slice(r * block, (r + 1) * block)
         store(o_ref, r, 0, x[: x.shape[0] // 2, lanes])
         store(o_ref, r, 1, -x[x.shape[0] // 2 :, lanes])
 
 
-def nonlinear_kernel(rows, halo, load, store, w_ref, up_ref, down_ref, raman_ref, o_ref):
+def nonlinear_kernel(rows, halo, load, store, pieces, w_ref, *refs):
+    if pieces:
+        o_ref, up_ref, down_ref, raman_ref = refs[pieces + 1 :]
+        make_profiles(rows, refs[:pieces], refs[pieces], up_ref, down_ref, raman_ref)
+    else:
+        up_ref, down_ref, raman_ref, o_ref = refs
     block = w_ref.shape[1]
-    n_modes = up_ref.shape[1] // 4
+    n_modes = up_ref.shape[1] // 3
     count = n_modes // rows
 
     def part(h, c):
@@ -269,7 +281,7 @@
         if halo > 1 and h == 0:
             grid = product(up_ref[:, : 2 * n_modes], jnp.concatenate([high, high], axis=0))
         else:
-            grid = product(up_ref[...], jnp.concatenate([high, high, low, low], axis=0))
+            grid = product(up_ref[...], jnp.concatenate([high, high, low], axis=0))
         g_re, g_im = grid[:, :block], grid[:, block:]
         intensity = g_re * g_re + g_im * g_im
         high, low = split_two(intensity)
@@ -299,7 +311,6 @@
 
 def tiled(field, modes, betas):
     n_mode, n_tm = lax.axis_size("mode"), lax.axis_size("tm")
-    t_index = lax.axis_index("tm")
     own_modes, _, samples = field.shape
     n_dev = n_mode * n_tm
     total = samples * n_tm
@@ -314,34 +325,28 @@
     wide = 2 * rows
     halves = [[m * n_tm + h * quarter + q for m in range(n_mode) for q in range(quarter)] for h in range(2)]
     both_halves = [halves[0] + halves[1]]
-    half = t_index // quarter
 
     pieces = [modes]
     for shift in range(1, n_mode):
         pieces.append(lax.ppermute(modes, "mode", [(i, (i + shift) % n_mode) for i in range(n_mode)]))
     dev, pos = np.arange(n_dev), np.arange(block)
     cos_a, sin_a = exp_table(dev[:, None] * dev[None, :], n_dev)
-    cos_t, sin_t = exp_table(dev[:, None] * pos[None, :], total)
     cos_b, sin_b = exp_table(pos[:, None] * pos[None, :], block)
     first = block_matrix(cos_a, sin_a).transpose(2, 3, 0, 1)
     (cos_high, cos_low), (sin_high, sin_low) = np_split(cos_b), np_split(sin_b)
     last = jnp.asarray(np.concatenate([cos_high, sin_high, cos_low, sin_low], axis=1))
-    twist = jnp.asarray(np.stack([cos_t, sin_t]), f32)
     edge = np.arange(n_dev).reshape(n_tm, per_tm).T.reshape(-1)
 
     def flat(matrix):
         high, low = np_split(matrix.reshape(-1, 2 * n_dev))
-        return np.concatenate([high, low, high, low], axis=1)
+        return np.concatenate([high, low], axis=1)
 
     span = (halo + 1) * block
     lags = np.zeros((8, span + block))
     lags[:, block + 1 : block + 1 + RAMAN_TAPS] = RAMAN_SHARE * raman_taps()
 
-    rates = lax.dynamic_slice_in_dim(betas, t_index * rows, rows, 0)
-    rates_wide = lax.dynamic_slice_in_dim(betas, (t_index % quarter) * wide, wide, 0)
     windows_of = [[(a - halo + h) % n_dev for h in range(halo + 1) for a in devices] for devices in halves]
     final_wide = jnp.asarray(np.stack([flat(first[:, blocks]) for blocks in windows_of]))
-    final_wide = lax.dynamic_index_in_dim(final_wide, half, 0, keepdims=False)
 
     def load_edge(ref, r, c):
         return jnp.concatenate(
@@ -380,44 +385,28 @@
         return (2, count * n_dev, block)
 
     def enter(values):
-        kernel = functools.partial(disperse_kernel, rows, total, 0.5, load_edge, store_inner)
+        kernel = functools.partial(disperse_kernel, rows, total, 0.5, True, load_edge, store_inner)
         shapes = ((n_dev * (halo + 1) * rows * 2, block), table_of(rows))
-        matrices = (jnp.asarray(flat(first[..., edge])), jnp.asarray(flat(first)))
+        matrices = jnp.asarray(np.stack([flat(first[..., edge]), flat(first)]))
         return call_disperse(
-            kernel,
-            tuple(jax.ShapeDtypeStruct(shape, f32) for shape in shapes),
-            *(values, *matrices, last, twist, rates, rates_wide, final_wide),
+            kernel, tuple(jax.ShapeDtypeStruct(shape, f32) for shape in shapes), *(values, matrices, last, betas)
         )
 
     def go_on(values):
-        kernel = functools.partial(disperse_kernel, wide, total, 1.0, load_wide, store_wide)
+        kernel = functools.partial(disperse_kernel, wide, total, 1.0, False, load_wide, store_wide)
         shape = jax.ShapeDtypeStruct((n_pair * (halo + 1) * wide * 2, block), f32)
         return call_disperse(
             kernel,
             shape,
-            *(values, jnp.asarray(flat(first[..., both_halves[0]])), final_wide, last, twist, rates_wide),
+            *(values, jnp.asarray(flat(first[..., both_halves[0]]))[None], final_wide, last, betas),
             scratch_shapes=[pltpu.VMEM(table_of(wide), f32)],
         )
 
     def leave(values, turn):
-        kernel = functools.partial(disperse_kernel, rows, None, None, load_inner, store_edge)
+        kernel = functools.partial(disperse_kernel, rows, None, None, True, load_inner, store_edge)
         shape = jax.ShapeDtypeStruct((n_tm, rows, 2, samples), f32)
-        matrices = (jnp.asarray(flat(first)), jnp.asarray(flat(first[:, edge])))
-        return call_disperse(kernel, shape, values, *matrices, last, twist, turn)
-
-    def spread_profiles(windows):
-        total_grid = modes.shape[1] * n_mode
-        return pl.pallas_call(
-            functools.partial(profile_kernel, wide),
-            out_shape=(
-                jax.ShapeDtypeStruct((total_grid, 4 * n_dev * rows), jnp.bfloat16),
-                jax.ShapeDtypeStruct((2 * n_dev * rows, total_grid), jnp.bfloat16),
-                jax.ShapeDtypeStruct((span, 2 * block), jnp.bfloat16),
-            ),
-            in_specs=[pl.BlockSpec(memory_space=pltpu.VMEM)] * (n_mode + 1) + [pl.BlockSpec(memory_space=pl.ANY)],
-            name="profiles",
-            compiler_params=PARAMS,
-        )(*pieces, jnp.asarray(lags, f32), windows)
+        matrices = jnp.asarray(np.stack([flat(first), flat(first[:, edge])]))
+        return call_disperse(kernel, shape, values, matrices, last, turn)
 
     def load_spread(ref, h, r, c):
         start = (r // rows) * 2 * (halo + 1) * rows + 2 * (h * rows + r % rows) + c
@@ -433,9 +422,16 @@
     def store_last(ref, r, c, values):
         ref[pl.ds((r // rows) * 2 * rows + 2 * (r % rows) + c, n_pair, stride=4 * rows), :] = values
 
-    def nonlinear(number, windows, up, down, raman):
+    def nonlinear(number, windows, profiles):
         is_last = number == ITERS - 1
         height = n_dev * (rows if is_last else wide) * 2
+        total_grid, all_modes = modes.shape[1] * n_mode, own_modes * n_mode
+        shapes = (
+            jax.ShapeDtypeStruct((height, block), f32),
+            jax.ShapeDtypeStruct((total_grid, 3 * all_modes), jnp.bfloat16),
+            jax.ShapeDtypeStruct((2 * all_modes, total_grid), jnp.bfloat16),
+            jax.ShapeDtypeStruct((span, 2 * block), jnp.bfloat16),
+        )
         return pl.pallas_call(
             functools.partial(
                 nonlinear_kernel,
@@ -443,11 +439,12 @@
                 halo,
                 load_half if number else load_spread,
                 store_last if is_last else store_halves,
+                0 if number else n_mode,
             ),
-            out_shape=jax.ShapeDtypeStruct((height, block), f32),
+            out_shape=shapes[0] if number else shapes,
             name="nonlinear",
             compiler_params=PARAMS,
-        )(windows, up, down, raman)
+        )(windows, *(profiles if number else (*pieces, jnp.asarray(lags, f32))))
 
     def exchange(values, groups=None):
         count = len(groups[0]) if groups else n_dev
@@ -460,9 +457,12 @@
     values = lax.all_to_all(entry, "tm", 0, 0, tiled=True).reshape(-1, block)
     values, half_turn = enter(values)
     values = exchange(values)
-    profiles = spread_profiles(values)
+    profiles = None
     for number in range(ITERS):
-        values = nonlinear(number, values, *profiles)
+        if number == 0:
+            values, *profiles = nonlinear(number, values, None)
+        else:
+            values = nonlinear(number, values, profiles)
         if number < ITERS - 1:
             values = go_on(exchange(values, both_halves))
             values = exchange(values, halves)

time: 77.2 us -> 76.9 us (level)
  no operation moved by 1% of the time
where the time goes in v6:
time: 76.9 us; the launch traced here: 76.4 us
  blocking collectives  41.2 us (54%)
  starting transfers between devices  14.7 us (19%)
  waiting for transfers between devices  12.8 us (17%)
  Pallas kernels  6.84 us (9%)
  local copies, waits for them, and re-layouts  0.77 us (1%)
    all_to_all x3, blocking collectives, exchange(): lax.all_to_all(shaped, BOTH, 0, 0, tiled=True, axis_index_groups=groups)  32.6 us
    all_to_all x1, blocking collectives, tiled(): return lax.all_to_all(values, 'tm', 0, 0, tiled=True).reshape(field.shape)  8.7 us
    all_to_all x1, starting transfers between devices, tiled(): values = lax.all_to_all(entry, 'tm', 0, 0, tiled=True).reshape(-1, block)  6.5 us
    all_to_all x1, waiting for transfers between devices, tiled(): values = lax.all_to_all(entry, 'tm', 0, 0, tiled=True).reshape(-1, block)  6.22 us
    ppermute x3, waiting for transfers between devices, tiled(): lax.ppermute(modes, 'mode', [(i, (i + shift) % n_mode) for i in range(n_m...  5.58 us
    ppermute x3, starting transfers between devices, tiled(): lax.ppermute(modes, 'mode', [(i, (i + shift) % n_mode) for i in range(n_m...  4.76 us
    pallas_call x2, Pallas kernels, nonlinear(): pl.pallas_call(functools.partial(nonlinear_kernel, wide, halo, load_half...  3.78 us
    all_to_all x1, starting transfers between devices, exchange(): lax.all_to_all(shaped, BOTH, 0, 0, tiled=True, axis_index_groups=groups)  3.43 us
  transfers between devices with their start and end apart: 5, of which 4 were waited for; matrix products, arithmetic and copies ran while one was open for 0% of the time, Pallas kernels for 0%

profile of v6, /device:TPU:0, one launch (start us, length us, event | category | flops | bytes accessed | tf_op | source)
XLA Modules:
  0.0 76.4 jit_solution(1866586991865796319)
XLA Ops:
  0.0 6.5 %all-to-all-start = ((f32[8,12,2,128]{3,2,1,0:T(2,128)}), f32[8,12,2,128]{3,2,1,0:T(2,128)S(1)}, u32[]{:S(2)}, u32[]{:S(2)}) async-start(f32[8,12,2,128]{3,2,1,0:T(2,128)} %bitcast.24), calls=%async_computation | async-start | bytes 196608 | tf_op jit(solution)/shard_map/all_to_all | solution.py:457
  6.5 0.0 copy-done.7
  6.5 0.1 copy.10.refs_2_.refs_3_
  6.6 6.2 %all-to-all-done = f32[8,12,2,128]{3,2,1,0:T(2,128)S(1)} async-done(((f32[8,12,2,128]{3,2,1,0:T(2,128)}), f32[8,12,2,128]{3,2,1,0:T(2,128)S(1)}, u32[]{:S(2)}, u32[]{:S(2)}) %all-to-all-start) | async-done | bytes 98336 | tf_op jit(solution)/shard_map/all_to_all | solution.py:457
  12.8 0.0 copy-done
  12.8 0.0 copy-done.4
  12.8 1.4 %shard_map.91 = (f32[576,128]{1,0:T(8,128)}, f32[2,96,128]{2,1,0:T(8,128)S(1)}) custom-call(f32[192,128]{1,0:T(8,128)S(1)} %bitcast.19, bf16[2,64,128]{2,1,0:T(8,128)(2,1)S(1)} %copy-done.4, bf16[128,512]{1,0:T(8,128)(2,1)S(1)} %copy-done, f32[24,4]{1,0:T(8,128)S(1)} %copy.10.refs_2_.refs_3_), custom_call_target="tpu_custom_call" | custom-call | tf_op jit(solution)/shard_map/pallas_call | solution.py:382
  14.3 3.4 %all-to-all-start.1 = ((f32[32,9,2,128]{3,2,1,0:T(2,128)}), f32[32,9,2,128]{3,2,1,0:T(2,128)S(1)}, u32[]{:S(2)}, u32[]{:S(2)}) async-start(f32[32,9,2,128]{3,2,1,0:T(2,128)} %bitcast.4), calls=%async_computation.1 | async-start | bytes 589824 | tf_op jit(solution)/shard_map/all_to_all | solution.py:452
  17.7 0.0 copy-done.1
  17.7 1.8 %collective-permute-start.1 = (f32[96,256]{1,0:T(8,128)S(1)}, f32[96,256]{1,0:T(8,128)S(1)}, u32[]{:S(2)}, u32[]{:S(2)}) collective-permute-start(f32[96,256]{1,0:T(8,128)S(1)} %copy-done.1), channel_id=1, source_target_pairs={{0,16},{8,24},{16,0},{24,8},{1,17},{9,25},{17,1},{25,9},{2,18},{10... | collective-permute-start | bytes 294920 | tf_op jit(solution)/shard_map/ppermute | solution.py:331
  19.5 1.5 %collective-permute-start = (f32[96,256]{1,0:T(8,128)S(1)}, f32[96,256]{1,0:T(8,128)S(1)}, u32[]{:S(2)}, u32[]{:S(2)}) collective-permute-start(f32[96,256]{1,0:T(8,128)S(1)} %copy-done.1), channel_id=1, source_target_pairs={{0,8},{8,16},{16,24},{24,0},{1,9},{9,17},{17,25},{25,1},{2,10},{10... | collective-permute-start | bytes 294920 | tf_op jit(solution)/shard_map/ppermute | solution.py:331
  21.0 1.5 %collective-permute-start.2 = (f32[96,256]{1,0:T(8,128)S(1)}, f32[96,256]{1,0:T(8,128)S(1)}, u32[]{:S(2)}, u32[]{:S(2)}) collective-permute-start(f32[96,256]{1,0:T(8,128)S(1)} %copy-done.1), channel_id=1, source_target_pairs={{0,24},{8,0},{16,8},{24,16},{1,25},{9,1},{17,9},{25,17},{2,26},{10... | collective-permute-start | bytes 294920 | tf_op jit(solution)/shard_map/ppermute | solution.py:331
  22.5 5.0 %collective-permute-done.1.refs_2_ = f32[96,256]{1,0:T(8,128)S(1)} collective-permute-done((f32[96,256]{1,0:T(8,128)S(1)}, f32[96,256]{1,0:T(8,128)S(1)}, u32[]{:S(2)}, u32[]{:S(2)}) %collective-permute-start.1) | collective-permute-done | bytes 98336 | tf_op jit(solution)/shard_map/ppermute | solution.py:331
  27.5 0.0 collective-permute-done.refs_1_
  27.5 0.5 collective-permute-done.2.refs_3_
  28.1 1.0 %all-to-all-done.1 = f32[32,9,2,128]{3,2,1,0:T(2,128)S(1)} async-done(((f32[32,9,2,128]{3,2,1,0:T(2,128)}), f32[32,9,2,128]{3,2,1,0:T(2,128)S(1)}, u32[]{:S(2)}, u32[]{:S(2)}) %all-to-all-start.1) | async-done | bytes 294944 | tf_op jit(solution)/shard_map/all_to_all | solution.py:452
  29.0 0.0 copy-done.6
  29.0 2.0 %nonlinear.2 = (f32[384,128]{1,0:T(8,128)S(1)}, bf16[1024,288]{1,0:T(8,128)(2,1)S(1)}, bf16[192,1024]{1,0:T(8,128)(2,1)S(1)}, bf16[384,256]{1,0:T(8,128)(2,1)S(1)}) custom-call(f32[576,128]{1,0:T(8,128)S(1)} %bitcast.16, f32[96,256]{1,0:T(8,128)S(1)} %copy-done.1, f32[96,256]{1,0:T(8,128)S(1)} %collective-permute-done.refs_1_, ...), custom_call_target="tpu_custom_call" | custom-call | tf_op jit(solution)/shard_map/nonlinear/pallas_call | solution.py:435
  31.0 0.0 copy-start.2
  31.0 0.0 copy-start.5
  31.1 12.3 %all_to_all.30 = f32[32,6,2,128]{3,2,1,0:T(2,128)S(1)} all-to-all(f32[32,6,2,128]{3,2,1,0:T(2,128)S(1)} %bitcast.22), channel_id=1, replica_groups={{0,1,2,3,8,9,10,11,16,17,18,19,24,25,26,27,4,5,6,7,12,13,14,15,20,21,22..., dimensions={0} | all-to-all | bytes 393216 | tf_op jit(solution)/shard_map/all_to_all | solution.py:452
  43.4 0.0 copy-done.2
  43.4 0.0 copy-done.5
  43.4 0.9 %shard_map.92 = f32[576,128]{1,0:T(8,128)S(1)} custom-call(f32[384,128]{1,0:T(8,128)S(1)} %bitcast.18, bf16[1,64,128]{2,1,0:T(8,128)(2,1)S(1)} %copy-done.5, bf16[2,96,128]{2,1,0:T(8,128)(2,1)S(1)} %copy-done.2, bf16[128,512]{1,0:T(8,128)(2,1)S(1)} %copy-done, f32[24,4]{1,0:T(8,128)S(1)} %copy.10.refs_2_.refs_3_), custom_call_target="tpu_custom_call" | custom-call | tf_op jit(solution)/shard_map/pallas_call | solution.py:382
  44.3 10.8 %all_to_all.31 = f32[16,18,2,128]{3,2,1,0:T(2,128)S(1)} all-to-all(f32[16,18,2,128]{3,2,1,0:T(2,128)S(1)} %bitcast.17), channel_id=1, replica_groups={{0,1,2,3,8,9,10,11,16,17,18,19,24,25,26,27},{4,5,6,7,12,13,14,15,20,21,..., dimensions={0} | all-to-all | bytes 589824 | tf_op jit(solution)/shard_map/all_to_all | solution.py:452
  55.1 1.8 %nonlinear.3 = f32[192,128]{1,0:T(8,128)S(1)} custom-call(f32[576,128]{1,0:T(8,128)S(1)} %bitcast.15, bf16[1024,288]{1,0:T(8,128)(2,1)S(1)} %get-tuple-element.13.refs_0_, bf16[192,1024]{1,0:T(8,128)(2,1)S(1)} %get-tuple-element.14.refs_1_, bf16[384,256]{1,0:T(8,128)(2,1)S(1)} %get-tuple-element.15.refs_2_), custom_call_target="tpu_custom_call" | custom-call | tf_op jit(solution)/shard_map/nonlinear/pallas_call | solution.py:435
  56.9 0.0 copy-start.3
  56.9 9.4 %all_to_all.32 = f32[32,3,2,128]{3,2,1,0:T(2,128)S(1)} all-to-all(f32[32,3,2,128]{3,2,1,0:T(2,128)S(1)} %bitcast.21), channel_id=1, replica_groups=mesh['mode'=4,'tm'=8] {'mode','tm'}, dimensions={0} | all-to-all | bytes 196608 | tf_op jit(solution)/shard_map/all_to_all | solution.py:452
  66.3 0.0 copy-done.3
  66.3 0.7 shard_map.93
  67.1 8.7 %all_to_all.33 = f32[8,3,2,512]{3,2,1,0:T(2,128)S(1)} all-to-all(f32[8,3,2,512]{3,2,1,0:T(2,128)S(1)} %shard_map.93), channel_id=1, replica_groups=mesh['mode'=4,'tm'=8] {'tm'}, dimensions={0} | all-to-all | bytes 196608 | tf_op jit(solution)/shard_map/all_to_all | solution.py:470
  75.8 0.6 copy.13
  (5 shorter events, 0.0 us)
Async XLA Ops:
  0.0 12.8 %copy-start = (bf16[128,512]{1,0:T(8,128)(2,1)S(1)}, bf16[128,512]{1,0:T(8,128)(2,1)}, u32[]{:S(2)}) copy-start(bf16[128,512]{1,0:T(8,128)(2,1)} %constant.12.clone.refs_1_.refs_2_) | copy-start | bytes 393220
  0.0 6.5 %copy-start.7 = (f32[24,4]{0,1:T(4,128)S(1)}, f32[24,4]{0,1:T(4,128)}, u32[]{:S(2)}) copy-start(f32[24,4]{0,1:T(4,128)} %param.11) | copy-start | bytes 1156
  0.0 12.8 %copy-start.4 = (bf16[2,64,128]{2,1,0:T(8,128)(2,1)S(1)}, bf16[2,64,128]{2,1,0:T(8,128)(2,1)}, u32[]{:S(2)}) copy-start(bf16[2,64,128]{2,1,0:T(8,128)(2,1)} %constant.14.clone.refs_0_) | copy-start | bytes 98308
  0.0 12.8 %all-to-all-start = ((f32[8,12,2,128]{3,2,1,0:T(2,128)}), f32[8,12,2,128]{3,2,1,0:T(2,128)S(1)}, u32[]{:S(2)}, u32[]{:S(2)}) async-start(f32[8,12,2,128]{3,2,1,0:T(2,128)} %bitcast.24), calls=%async_computation | async-start | bytes 196608 | tf_op jit(solution)/shard_map/all_to_all | solution.py:457
  14.3 3.4 %copy-start.1 = (f32[96,256]{1,0:T(8,128)S(1)}, f32[96,256]{1,0:T(8,128)}, u32[]{:S(2)}) copy-start(f32[96,256]{1,0:T(8,128)} %refs_0_.3) | copy-start | bytes 294916
  14.3 14.8 %copy-start.6 = (f32[8,512]{1,0:T(8,128)S(1)}, f32[8,512]{1,0:T(8,128)}, u32[]{:S(2)}) copy-start(f32[8,512]{1,0:T(8,128)} %constant.15.clone.refs_4_) | copy-start | bytes 49156
  14.3 14.8 %all-to-all-start.1 = ((f32[32,9,2,128]{3,2,1,0:T(2,128)}), f32[32,9,2,128]{3,2,1,0:T(2,128)S(1)}, u32[]{:S(2)}, u32[]{:S(2)}) async-start(f32[32,9,2,128]{3,2,1,0:T(2,128)} %bitcast.4), calls=%async_computation.1 | async-start | bytes 589824 | tf_op jit(solution)/shard_map/all_to_all | solution.py:452
  17.7 9.8 %collective-permute-start.1 = (f32[96,256]{1,0:T(8,128)S(1)}, f32[96,256]{1,0:T(8,128)S(1)}, u32[]{:S(2)}, u32[]{:S(2)}) collective-permute-start(f32[96,256]{1,0:T(8,128)S(1)} %copy-done.1), channel_id=1, source_target_pairs={{0,16},{8,24},{16,0},{24,8},{1,17},{9,25},{17,1},{25,9},{2,18},{10... | collective-permute-start | bytes 294920 | tf_op jit(solution)/shard_map/ppermute | solution.py:331
  19.5 8.0 %collective-permute-start = (f32[96,256]{1,0:T(8,128)S(1)}, f32[96,256]{1,0:T(8,128)S(1)}, u32[]{:S(2)}, u32[]{:S(2)}) collective-permute-start(f32[96,256]{1,0:T(8,128)S(1)} %copy-done.1), channel_id=1, source_target_pairs={{0,8},{8,16},{16,24},{24,0},{1,9},{9,17},{17,25},{25,1},{2,10},{10... | collective-permute-start | bytes 294920 | tf_op jit(solution)/shard_map/ppermute | solution.py:331
  21.0 7.0 %collective-permute-start.2 = (f32[96,256]{1,0:T(8,128)S(1)}, f32[96,256]{1,0:T(8,128)S(1)}, u32[]{:S(2)}, u32[]{:S(2)}) collective-permute-start(f32[96,256]{1,0:T(8,128)S(1)} %copy-done.1), channel_id=1, source_target_pairs={{0,24},{8,0},{16,8},{24,16},{1,25},{9,1},{17,9},{25,17},{2,26},{10... | collective-permute-start | bytes 294920 | tf_op jit(solution)/shard_map/ppermute | solution.py:331
  31.0 12.4 %copy-start.2 = (bf16[2,96,128]{2,1,0:T(8,128)(2,1)S(1)}, bf16[2,96,128]{2,1,0:T(8,128)(2,1)}, u32[]{:S(2)}) copy-start(bf16[2,96,128]{2,1,0:T(8,128)(2,1)} %constant.13.clone.refs_1_) | copy-start | bytes 147460
  31.0 12.4 %copy-start.5 = (bf16[1,64,128]{2,1,0:T(8,128)(2,1)S(1)}, bf16[1,64,128]{2,1,0:T(8,128)(2,1)}, u32[]{:S(2)}) copy-start(bf16[1,64,128]{2,1,0:T(8,128)(2,1)} %constant.18.refs_0_) | copy-start | bytes 49156
  56.9 9.5 %copy-start.3 = (bf16[2,64,128]{2,1,0:T(8,128)(2,1)S(1)}, bf16[2,64,128]{2,1,0:T(8,128)(2,1)}, u32[]{:S(2)}) copy-start(bf16[2,64,128]{2,1,0:T(8,128)(2,1)} %constant.17.clone.refs_0_) | copy-start | bytes 98308

commit v7 on v6

--- a/solution.py
+++ b/solution.py
@@ -226,8 +226,8 @@
 
     def across(matrix, values):
         high, low = split_two(values)
-        matrix = jnp.concatenate([matrix, matrix], axis=1)
-        return product(matrix, jnp.concatenate([high, high, low, low], axis=0))
+        matrix = jnp.concatenate([matrix, matrix[:, : matrix.shape[1] // 2]], axis=1)
+        return product(matrix, jnp.concatenate([high, high, low], axis=0))
 
     def twisted(values):
         re, im = values[:n_dev], values[n_dev:]
@@ -291,10 +291,10 @@
             own = (values, g_re, g_im, intensity)
     values, g_re, g_im, intensity = own
     taps = raman_ref[...]
-    taps = jnp.concatenate(
-        [taps, jnp.concatenate([taps[:, :block], jnp.zeros_like(taps[:, :block])], axis=1)], axis=0
-    )
-    both = product(jnp.concatenate(highs + lows, axis=1), taps)
+    skip = 1 if halo > 1 else 0
+    rest = taps[skip * block :, :block]
+    taps = jnp.concatenate([taps, jnp.concatenate([rest, jnp.zeros_like(rest)], axis=1)], axis=0)
+    both = product(jnp.concatenate(highs + lows[skip:], axis=1), taps)
     weight = (1.0 - RAMAN_SHARE) * intensity + (both[:, :block] + both[:, block:])
     drive = jnp.concatenate([g_re * weight, g_im * weight], axis=1)
     d_high, d_low = split_two(drive)

time: 76.9 us -> 76.6 us (level)
  no operation moved by 1% of the time
where the time goes in v7:
time: 76.6 us; the launch traced here: 76.2 us
  blocking collectives  41.3 us (54%)
  starting transfers between devices  14.7 us (19%)
  waiting for transfers between devices  12.8 us (17%)
  Pallas kernels  6.59 us (9%)
  local copies, waits for them, and re-layouts  0.77 us (1%)
    all_to_all x3, blocking collectives, exchange(): lax.all_to_all(shaped, BOTH, 0, 0, tiled=True, axis_index_groups=groups)  32.6 us
    all_to_all x1, blocking collectives, tiled(): return lax.all_to_all(values, 'tm', 0, 0, tiled=True).reshape(field.shape)  8.7 us
    all_to_all x1, starting transfers between devices, tiled(): values = lax.all_to_all(entry, 'tm', 0, 0, tiled=True).reshape(-1, block)  6.5 us
    all_to_all x1, waiting for transfers between devices, tiled(): values = lax.all_to_all(entry, 'tm', 0, 0, tiled=True).reshape(-1, block)  6.22 us
    ppermute x3, waiting for transfers between devices, tiled(): lax.ppermute(modes, 'mode', [(i, (i + shift) % n_mode) for i in range(n_m...  5.58 us
    ppermute x3, starting transfers between devices, tiled(): lax.ppermute(modes, 'mode', [(i, (i + shift) % n_mode) for i in range(n_m...  4.76 us
    pallas_call x2, Pallas kernels, nonlinear(): pl.pallas_call(functools.partial(nonlinear_kernel, wide, halo, load_half...  3.57 us
    all_to_all x1, starting transfers between devices, exchange(): lax.all_to_all(shaped, BOTH, 0, 0, tiled=True, axis_index_groups=groups)  3.43 us
  transfers between devices with their start and end apart: 5, of which 4 were waited for; matrix products, arithmetic and copies ran while one was open for 0% of the time, Pallas kernels for 0%

profile of v7, /device:TPU:0, one launch (start us, length us, event | category | flops | bytes accessed | tf_op | source)
XLA Modules:
  0.0 76.2 jit_solution(12143134771046538270)
XLA Ops:
  0.0 6.5 %all-to-all-start = ((f32[8,12,2,128]{3,2,1,0:T(2,128)}), f32[8,12,2,128]{3,2,1,0:T(2,128)S(1)}, u32[]{:S(2)}, u32[]{:S(2)}) async-start(f32[8,12,2,128]{3,2,1,0:T(2,128)} %bitcast.24), calls=%async_computation | async-start | bytes 196608 | tf_op jit(solution)/shard_map/all_to_all | solution.py:457
  6.5 0.0 copy-done.7
  6.5 0.1 copy.10.refs_2_.refs_3_
  6.6 6.2 %all-to-all-done = f32[8,12,2,128]{3,2,1,0:T(2,128)S(1)} async-done(((f32[8,12,2,128]{3,2,1,0:T(2,128)}), f32[8,12,2,128]{3,2,1,0:T(2,128)S(1)}, u32[]{:S(2)}, u32[]{:S(2)}) %all-to-all-start) | async-done | bytes 98336 | tf_op jit(solution)/shard_map/all_to_all | solution.py:457
  12.8 0.0 copy-done
  12.8 0.0 copy-done.4
  12.8 1.4 %shard_map.91 = (f32[576,128]{1,0:T(8,128)}, f32[2,96,128]{2,1,0:T(8,128)S(1)}) custom-call(f32[192,128]{1,0:T(8,128)S(1)} %bitcast.19, bf16[2,64,128]{2,1,0:T(8,128)(2,1)S(1)} %copy-done.4, bf16[128,512]{1,0:T(8,128)(2,1)S(1)} %copy-done, f32[24,4]{1,0:T(8,128)S(1)} %copy.10.refs_2_.refs_3_), custom_call_target="tpu_custom_call" | custom-call | tf_op jit(solution)/shard_map/pallas_call | solution.py:382
  14.2 3.4 %all-to-all-start.1 = ((f32[32,9,2,128]{3,2,1,0:T(2,128)}), f32[32,9,2,128]{3,2,1,0:T(2,128)S(1)}, u32[]{:S(2)}, u32[]{:S(2)}) async-start(f32[32,9,2,128]{3,2,1,0:T(2,128)} %bitcast.4), calls=%async_computation.1 | async-start | bytes 589824 | tf_op jit(solution)/shard_map/all_to_all | solution.py:452
  17.7 0.0 copy-done.1
  17.7 1.8 %collective-permute-start.1 = (f32[96,256]{1,0:T(8,128)S(1)}, f32[96,256]{1,0:T(8,128)S(1)}, u32[]{:S(2)}, u32[]{:S(2)}) collective-permute-start(f32[96,256]{1,0:T(8,128)S(1)} %copy-done.1), channel_id=1, source_target_pairs={{0,16},{8,24},{16,0},{24,8},{1,17},{9,25},{17,1},{25,9},{2,18},{10... | collective-permute-start | bytes 294920 | tf_op jit(solution)/shard_map/ppermute | solution.py:331
  19.5 1.5 %collective-permute-start = (f32[96,256]{1,0:T(8,128)S(1)}, f32[96,256]{1,0:T(8,128)S(1)}, u32[]{:S(2)}, u32[]{:S(2)}) collective-permute-start(f32[96,256]{1,0:T(8,128)S(1)} %copy-done.1), channel_id=1, source_target_pairs={{0,8},{8,16},{16,24},{24,0},{1,9},{9,17},{17,25},{25,1},{2,10},{10... | collective-permute-start | bytes 294920 | tf_op jit(solution)/shard_map/ppermute | solution.py:331
  21.0 1.5 %collective-permute-start.2 = (f32[96,256]{1,0:T(8,128)S(1)}, f32[96,256]{1,0:T(8,128)S(1)}, u32[]{:S(2)}, u32[]{:S(2)}) collective-permute-start(f32[96,256]{1,0:T(8,128)S(1)} %copy-done.1), channel_id=1, source_target_pairs={{0,24},{8,0},{16,8},{24,16},{1,25},{9,1},{17,9},{25,17},{2,26},{10... | collective-permute-start | bytes 294920 | tf_op jit(solution)/shard_map/ppermute | solution.py:331
  22.5 5.0 %collective-permute-done.1.refs_2_ = f32[96,256]{1,0:T(8,128)S(1)} collective-permute-done((f32[96,256]{1,0:T(8,128)S(1)}, f32[96,256]{1,0:T(8,128)S(1)}, u32[]{:S(2)}, u32[]{:S(2)}) %collective-permute-start.1) | collective-permute-done | bytes 98336 | tf_op jit(solution)/shard_map/ppermute | solution.py:331
  27.5 0.0 collective-permute-done.refs_1_
  27.5 0.5 collective-permute-done.2.refs_3_
  28.0 1.0 %all-to-all-done.1 = f32[32,9,2,128]{3,2,1,0:T(2,128)S(1)} async-done(((f32[32,9,2,128]{3,2,1,0:T(2,128)}), f32[32,9,2,128]{3,2,1,0:T(2,128)S(1)}, u32[]{:S(2)}, u32[]{:S(2)}) %all-to-all-start.1) | async-done | bytes 294944 | tf_op jit(solution)/shard_map/all_to_all | solution.py:452
  29.0 0.0 copy-done.6
  29.0 1.9 %nonlinear.2 = (f32[384,128]{1,0:T(8,128)S(1)}, bf16[1024,288]{1,0:T(8,128)(2,1)S(1)}, bf16[192,1024]{1,0:T(8,128)(2,1)S(1)}, bf16[384,256]{1,0:T(8,128)(2,1)S(1)}) custom-call(f32[576,128]{1,0:T(8,128)S(1)} %bitcast.16, f32[96,256]{1,0:T(8,128)S(1)} %copy-done.1, f32[96,256]{1,0:T(8,128)S(1)} %collective-permute-done.refs_1_, ...), custom_call_target="tpu_custom_call" | custom-call | tf_op jit(solution)/shard_map/nonlinear/pallas_call | solution.py:435
  30.9 0.0 copy-start.2
  30.9 0.0 copy-start.5
  31.0 12.3 %all_to_all.30 = f32[32,6,2,128]{3,2,1,0:T(2,128)S(1)} all-to-all(f32[32,6,2,128]{3,2,1,0:T(2,128)S(1)} %bitcast.22), channel_id=1, replica_groups={{0,1,2,3,8,9,10,11,16,17,18,19,24,25,26,27,4,5,6,7,12,13,14,15,20,21,22..., dimensions={0} | all-to-all | bytes 393216 | tf_op jit(solution)/shard_map/all_to_all | solution.py:452
  43.3 0.0 copy-done.2
  43.3 0.0 copy-done.5
  43.3 0.9 %shard_map.92 = f32[576,128]{1,0:T(8,128)S(1)} custom-call(f32[384,128]{1,0:T(8,128)S(1)} %bitcast.18, bf16[1,64,128]{2,1,0:T(8,128)(2,1)S(1)} %copy-done.5, bf16[2,96,128]{2,1,0:T(8,128)(2,1)S(1)} %copy-done.2, bf16[128,512]{1,0:T(8,128)(2,1)S(1)} %copy-done, f32[24,4]{1,0:T(8,128)S(1)} %copy.10.refs_2_.refs_3_), custom_call_target="tpu_custom_call" | custom-call | tf_op jit(solution)/shard_map/pallas_call | solution.py:382
  44.2 10.8 %all_to_all.31 = f32[16,18,2,128]{3,2,1,0:T(2,128)S(1)} all-to-all(f32[16,18,2,128]{3,2,1,0:T(2,128)S(1)} %bitcast.17), channel_id=1, replica_groups={{0,1,2,3,8,9,10,11,16,17,18,19,24,25,26,27},{4,5,6,7,12,13,14,15,20,21,..., dimensions={0} | all-to-all | bytes 589824 | tf_op jit(solution)/shard_map/all_to_all | solution.py:452
  55.0 1.7 %nonlinear.3 = f32[192,128]{1,0:T(8,128)S(1)} custom-call(f32[576,128]{1,0:T(8,128)S(1)} %bitcast.15, bf16[1024,288]{1,0:T(8,128)(2,1)S(1)} %get-tuple-element.13.refs_0_, bf16[192,1024]{1,0:T(8,128)(2,1)S(1)} %get-tuple-element.14.refs_1_, bf16[384,256]{1,0:T(8,128)(2,1)S(1)} %get-tuple-element.15.refs_2_), custom_call_target="tpu_custom_call" | custom-call | tf_op jit(solution)/shard_map/nonlinear/pallas_call | solution.py:435
  56.6 0.0 copy-start.3
  56.6 9.4 %all_to_all.32 = f32[32,3,2,128]{3,2,1,0:T(2,128)S(1)} all-to-all(f32[32,3,2,128]{3,2,1,0:T(2,128)S(1)} %bitcast.21), channel_id=1, replica_groups=mesh['mode'=4,'tm'=8] {'mode','tm'}, dimensions={0} | all-to-all | bytes 196608 | tf_op jit(solution)/shard_map/all_to_all | solution.py:452
  66.1 0.0 copy-done.3
  66.1 0.7 shard_map.93
  66.8 8.7 %all_to_all.33 = f32[8,3,2,512]{3,2,1,0:T(2,128)S(1)} all-to-all(f32[8,3,2,512]{3,2,1,0:T(2,128)S(1)} %shard_map.93), channel_id=1, replica_groups=mesh['mode'=4,'tm'=8] {'tm'}, dimensions={0} | all-to-all | bytes 196608 | tf_op jit(solution)/shard_map/all_to_all | solution.py:470
  75.5 0.6 copy.13
  (5 shorter events, 0.0 us)
Async XLA Ops:
  0.0 12.8 %copy-start = (bf16[128,512]{1,0:T(8,128)(2,1)S(1)}, bf16[128,512]{1,0:T(8,128)(2,1)}, u32[]{:S(2)}) copy-start(bf16[128,512]{1,0:T(8,128)(2,1)} %constant.12.clone.refs_1_.refs_2_) | copy-start | bytes 393220
  0.0 6.5 %copy-start.7 = (f32[24,4]{0,1:T(4,128)S(1)}, f32[24,4]{0,1:T(4,128)}, u32[]{:S(2)}) copy-start(f32[24,4]{0,1:T(4,128)} %param.11) | copy-start | bytes 1156
  0.0 12.8 %copy-start.4 = (bf16[2,64,128]{2,1,0:T(8,128)(2,1)S(1)}, bf16[2,64,128]{2,1,0:T(8,128)(2,1)}, u32[]{:S(2)}) copy-start(bf16[2,64,128]{2,1,0:T(8,128)(2,1)} %constant.14.clone.refs_0_) | copy-start | bytes 98308
  0.0 12.8 %all-to-all-start = ((f32[8,12,2,128]{3,2,1,0:T(2,128)}), f32[8,12,2,128]{3,2,1,0:T(2,128)S(1)}, u32[]{:S(2)}, u32[]{:S(2)}) async-start(f32[8,12,2,128]{3,2,1,0:T(2,128)} %bitcast.24), calls=%async_computation | async-start | bytes 196608 | tf_op jit(solution)/shard_map/all_to_all | solution.py:457
  14.2 3.4 %copy-start.1 = (f32[96,256]{1,0:T(8,128)S(1)}, f32[96,256]{1,0:T(8,128)}, u32[]{:S(2)}) copy-start(f32[96,256]{1,0:T(8,128)} %refs_0_.3) | copy-start | bytes 294916
  14.2 14.8 %copy-start.6 = (f32[8,512]{1,0:T(8,128)S(1)}, f32[8,512]{1,0:T(8,128)}, u32[]{:S(2)}) copy-start(f32[8,512]{1,0:T(8,128)} %constant.15.clone.refs_4_) | copy-start | bytes 49156
  14.2 14.8 %all-to-all-start.1 = ((f32[32,9,2,128]{3,2,1,0:T(2,128)}), f32[32,9,2,128]{3,2,1,0:T(2,128)S(1)}, u32[]{:S(2)}, u32[]{:S(2)}) async-start(f32[32,9,2,128]{3,2,1,0:T(2,128)} %bitcast.4), calls=%async_computation.1 | async-start | bytes 589824 | tf_op jit(solution)/shard_map/all_to_all | solution.py:452
  17.7 9.8 %collective-permute-start.1 = (f32[96,256]{1,0:T(8,128)S(1)}, f32[96,256]{1,0:T(8,128)S(1)}, u32[]{:S(2)}, u32[]{:S(2)}) collective-permute-start(f32[96,256]{1,0:T(8,128)S(1)} %copy-done.1), channel_id=1, source_target_pairs={{0,16},{8,24},{16,0},{24,8},{1,17},{9,25},{17,1},{25,9},{2,18},{10... | collective-permute-start | bytes 294920 | tf_op jit(solution)/shard_map/ppermute | solution.py:331
  19.5 8.0 %collective-permute-start = (f32[96,256]{1,0:T(8,128)S(1)}, f32[96,256]{1,0:T(8,128)S(1)}, u32[]{:S(2)}, u32[]{:S(2)}) collective-permute-start(f32[96,256]{1,0:T(8,128)S(1)} %copy-done.1), channel_id=1, source_target_pairs={{0,8},{8,16},{16,24},{24,0},{1,9},{9,17},{17,25},{25,1},{2,10},{10... | collective-permute-start | bytes 294920 | tf_op jit(solution)/shard_map/ppermute | solution.py:331
  21.0 7.0 %collective-permute-start.2 = (f32[96,256]{1,0:T(8,128)S(1)}, f32[96,256]{1,0:T(8,128)S(1)}, u32[]{:S(2)}, u32[]{:S(2)}) collective-permute-start(f32[96,256]{1,0:T(8,128)S(1)} %copy-done.1), channel_id=1, source_target_pairs={{0,24},{8,0},{16,8},{24,16},{1,25},{9,1},{17,9},{25,17},{2,26},{10... | collective-permute-start | bytes 294920 | tf_op jit(solution)/shard_map/ppermute | solution.py:331
  30.9 12.4 %copy-start.2 = (bf16[2,96,128]{2,1,0:T(8,128)(2,1)S(1)}, bf16[2,96,128]{2,1,0:T(8,128)(2,1)}, u32[]{:S(2)}) copy-start(bf16[2,96,128]{2,1,0:T(8,128)(2,1)} %constant.13.clone.refs_1_) | copy-start | bytes 147460
  30.9 12.4 %copy-start.5 = (bf16[1,64,128]{2,1,0:T(8,128)(2,1)S(1)}, bf16[1,64,128]{2,1,0:T(8,128)(2,1)}, u32[]{:S(2)}) copy-start(bf16[1,64,128]{2,1,0:T(8,128)(2,1)} %constant.18.refs_0_) | copy-start | bytes 49156
  56.6 9.5 %copy-start.3 = (bf16[2,64,128]{2,1,0:T(8,128)(2,1)S(1)}, bf16[2,64,128]{2,1,0:T(8,128)(2,1)}, u32[]{:S(2)}) copy-start(bf16[2,64,128]{2,1,0:T(8,128)(2,1)} %constant.17.clone.refs_0_) | copy-start | bytes 98308
